TPU v7x, 256 devices: a whole 4x4x8 slice. The times are simulated.
256 devices in a mesh: pipe: 8 (over x, z_hi), expert: 32 (over y, z_lo, core).
Axes of the slice: x: 4, y: 4, z: 8 (z_hi: 2, z_lo: 4; z = z_hi * 4 + z_lo), core: 2. Of those that a mesh axis runs over, the one named last changes fastest.
Arguments:
- fwd_acts: bfloat16 [8, 2048, 3584], P('pipe', 'expert'), may hold values from -6 to 6
- fwd_routes: int32 [8, 2048, 2], P('pipe', 'expert'), may hold values from 0 to 7, all different within a row; in each aligned block of 64 rows (0 to 63, 64 to 127, ..., all dimensions but the last counted through in order) at most 20 rows name the same one
- fwd_gates: float32 [8, 2048, 2], P('pipe', 'expert'), may hold values from 0.25 to 1
- back_acts: bfloat16 [8, 2048, 3584], P('pipe', 'expert'), may hold values from -6 to 6
- back_routes: int32 [8, 2048, 2], P('pipe', 'expert'), may hold values from 0 to 7, all different within a row; in each aligned block of 64 rows (0 to 63, 64 to 127, ..., all dimensions but the last counted through in order) at most 20 rows name the same one
- back_gates: float32 [8, 2048, 2], P('pipe', 'expert'), may hold values from 0.25 to 1
- back_grads: bfloat16 [8, 2048, 3584], P('pipe', 'expert'), may hold values from -0.59765625 to 0.59765625
- w_up: bfloat16 [8, 32, 3584, 256], P('pipe', 'expert'), may hold values from -0.09375 to 0.09375
- w_down: bfloat16 [8, 32, 256, 3584], P('pipe', 'expert'), may hold values from -0.1875 to 0.1875
Outputs:
- fwd_next: bfloat16 [8, 2048, 3584], P('pipe', 'expert')
- back_next: bfloat16 [8, 2048, 3584], P('pipe', 'expert')
- grad_up: float32 [8, 32, 3584, 256], P('pipe', 'expert')
- grad_down: float32 [8, 32, 256, 3584], P('pipe', 'expert')
Inputs may be any that keep to these rules, and one draw needn't show every extreme that they name: `fwd_routes`: in each aligned block of 64 rows of a section the 2 experts of a row differ, and each expert is named by at most 20 rows, by exactly 20 in some block. `back_routes`: as for fwd_routes.
All inputs are finite; a program needn't handle non-finite values.
Results may differ from a plain program's by a relative error of at most 0.005.
Values may be sent and summed in bfloat16 or wider, within the bound.
A program may use at most 192 MiB of HBM per device.

v0:
```python
import jax
import jax.numpy as jnp
from jax import lax
from jax.sharding import PartitionSpec as P

GROUP = 4


HIGH = lax.Precision.HIGHEST


def passed_along(value, axis, steps):
    count = lax.axis_size(axis)
    pairs = [(source, (source + steps) % count) for source in range(count)]
    return lax.ppermute(value, axis, pairs)


def silu_grad(value):
    sigma = jax.nn.sigmoid(value)
    return sigma * (1.0 + value * (1.0 - sigma))


def tables(routes, gates, experts, slot_cap):
    tok_rows, top_count = routes.shape
    flat = routes.reshape(tok_rows * top_count)
    onehot = (flat[:, None] == jnp.arange(experts, dtype=jnp.int32)[None, :]).astype(jnp.int32)
    before = jnp.cumsum(onehot, axis=0) - onehot
    slots = jnp.sum(before * onehot, axis=1)
    places = flat * slot_cap + slots
    columns = jnp.arange(experts * slot_cap, dtype=jnp.int32)
    hits = (
        (places[:, None] == columns[None, :])
        .astype(jnp.float32)
        .reshape(tok_rows, top_count, experts * slot_cap)
    )
    plain = jnp.sum(hits, axis=1)
    gated = jnp.sum(hits * gates[:, :, None], axis=1)
    return (plain, gated)


def gather_rows(plain, values):
    return lax.dot_general(
        plain.astype(jnp.bfloat16),
        values,
        (((0,), (0,)), ((), ())),
        preferred_element_type=jnp.float32,
    ).astype(jnp.bfloat16)


def send_rows(stacked, experts, slot_cap):
    count, _, model_width = stacked.shape
    copies = jnp.repeat(stacked.reshape(count, experts, 1, slot_cap, model_width), GROUP, axis=2)
    copies = copies.reshape(count, experts * GROUP, slot_cap, model_width)
    received = lax.all_to_all(copies, "expert", split_axis=1, concat_axis=1, tiled=True)
    return received.reshape(count, -1, model_width)


def send_back(parts, experts, slot_cap):
    count, _, model_width = parts.shape
    arranged = parts.reshape(count, experts * GROUP, slot_cap, model_width)
    received = lax.all_to_all(arranged, "expert", split_axis=1, concat_axis=1, tiled=True)
    summed = jnp.sum(
        received.reshape(count, experts, GROUP, slot_cap, model_width), axis=2, dtype=jnp.float32
    )
    return summed.reshape(count, experts * slot_cap, model_width)


def expert_forward(rows, up_proj, down_proj):
    pre = jnp.dot(rows, up_proj, preferred_element_type=jnp.float32)
    act = jax.nn.silu(pre).astype(jnp.bfloat16)
    return jnp.dot(act, down_proj, preferred_element_type=jnp.float32).astype(jnp.bfloat16)


def expert_backward(rows, grad_rows, up_proj, down_proj):
    pre = jnp.dot(rows, up_proj, preferred_element_type=jnp.float32)
    act = jax.nn.silu(pre).astype(jnp.bfloat16)
    dact = lax.dot_general(
        grad_rows, down_proj, (((1,), (1,)), ((), ())), preferred_element_type=jnp.float32
    )
    dpre = (dact * silu_grad(pre)).astype(jnp.bfloat16)
    dpart = lax.dot_general(
        dpre, up_proj, (((1,), (1,)), ((), ())), preferred_element_type=jnp.float32
    ).astype(jnp.bfloat16)
    grad_up = lax.dot_general(
        rows, dpre, (((0,), (0,)), ((), ())), preferred_element_type=jnp.float32
    )
    grad_down = lax.dot_general(
        act, grad_rows, (((0,), (0,)), ((), ())), preferred_element_type=jnp.float32
    )
    return (dpart, grad_up, grad_down)


def local(
    fwd_acts, fwd_routes, fwd_gates, back_acts, back_routes, back_gates, back_grads, w_up, w_down
):
    devices = lax.axis_size("expert")
    experts = devices // GROUP
    tok_rows = fwd_acts.shape[1]
    top_count = fwd_routes.shape[2]
    slot_cap = GROUP * (5 * tok_rows * top_count // (4 * devices))
    up_proj = w_up[0, 0]
    down_proj = w_down[0, 0]
    fwd_input = fwd_acts[0]
    back_input = back_acts[0]
    out_grad = back_grads[0]
    plain_f, gated_f = tables(fwd_routes[0], fwd_gates[0], experts, slot_cap)
    plain_b, gated_b = tables(back_routes[0], back_gates[0], experts, slot_cap)
    buffer_f = gather_rows(plain_f, fwd_input)
    buffer_x = gather_rows(plain_b, back_input)
    buffer_g = lax.dot_general(
        gated_b, out_grad.astype(jnp.float32), (((0,), (0,)), ((), ())), precision=HIGH
    ).astype(jnp.bfloat16)
    got_f = send_rows(buffer_f[None], experts, slot_cap)
    part = expert_forward(got_f[0], up_proj, down_proj)
    summed_f = send_back(part[None], experts, slot_cap)[0]
    got_b = send_rows(jnp.stack([buffer_x, buffer_g]), experts, slot_cap)
    dpart, grad_up, grad_down = expert_backward(got_b[0], got_b[1], up_proj, down_proj)
    summed_b = send_back(dpart[None], experts, slot_cap)[0]
    merged = jnp.dot(gated_f, summed_f, precision=HIGH)
    section_out = (fwd_input.astype(jnp.float32) + merged).astype(jnp.bfloat16)
    spread_back = jnp.dot(plain_b, summed_b, precision=HIGH)
    section_grad = (out_grad.astype(jnp.float32) + spread_back).astype(jnp.bfloat16)
    fwd_next = passed_along(section_out[None], "pipe", 1)
    back_next = passed_along(section_grad[None], "pipe", -1)
    return (fwd_next, back_next, grad_up[None, None], grad_down[None, None])


def solution(mesh):
    in_specs = (
        P("pipe", "expert", None),
        P("pipe", "expert", None),
        P("pipe", "expert", None),
        P("pipe", "expert", None),
        P("pipe", "expert", None),
        P("pipe", "expert", None),
        P("pipe", "expert", None),
        P("pipe", "expert", None, None),
        P("pipe", "expert", None, None),
    )
    out_specs = (
        P("pipe", "expert", None),
        P("pipe", "expert", None),
        P("pipe", "expert", None, None),
        P("pipe", "expert", None, None),
    )
    return jax.shard_map(local, mesh=mesh, in_specs=in_specs, out_specs=out_specs, check_vma=False)
```

profile of v0, /device:TPU:1, one launch (start us, length us, event | category | flops | bytes accessed | tf_op | source)
XLA Modules:
  0.0 672.6 jit_solution(2642117069289322087)
XLA Ops:
  0.6 0.0 copy-start
  0.6 0.9 copy.40
  1.5 0.1 eq.58
  1.7 0.1 fusion.28
  1.8 0.2 reduce_window_sum.17
  2.0 0.2 select_reduce_fusion.3
  2.1 0.1 reduce_sum.77
  2.3 0.1 copy.41
  2.4 0.7 bitcast_add_fusion.1
  3.1 0.8 convert_reduce_fusion.3
  3.8 2.5 convolution_convert_fusion.4
  6.3 1.4 reshape_broadcast_in_dim.9
  7.7 2.9 broadcast_in_dim.26
  10.6 10.4 %all-to-all-start = ((bf16[1,32,20,3584]{3,2,0,1:T(8,128)(2,1)}), bf16[1,32,20,3584]{3,2,0,1:T(8,128)(2,1)}, u32[]{:S(2)}, u32[]{:S(2)}) async-start(bf16[1,32,20,3584]{3,2,0,1:T(8,128)(2,1)} %bitcast.71), calls=%async_computation | async-start | bytes 11010048 | tf_op jit(solution)/shard_map/all_to_all | solution.py:54
  21.0 0.0 copy-done.5
  21.0 0.1 copy.43
  21.1 0.1 eq.65
  21.2 0.1 fusion.27
  21.3 0.2 reduce_window_sum.18
  21.5 0.2 select_reduce_fusion.2
  21.7 0.1 reduce_sum.82
  21.8 0.1 copy.44
  21.9 0.0 copy-done.6
  21.9 0.1 select_reduce_fusion
  22.0 1.5 convolution_convert_fusion.3
  23.5 1.4 stack.9
  24.9 3.1 convolution_convert_fusion.2
  28.0 2.3 stack.10
  30.3 1.7 maximum_bitcast_fusion
  31.9 3.7 copy.45
  35.7 107.9 %all-to-all-done = bf16[1,32,20,3584]{3,2,0,1:T(8,128)(2,1)} async-done(((bf16[1,32,20,3584]{3,2,0,1:T(8,128)(2,1)}), bf16[1,32,20,3584]{3,2,0,1:T(8,128)(2,1)}, u32[]{:S(2)}, u32[]{:S(2)}) %all-to-all-start) | async-done | bytes 4587552 | tf_op jit(solution)/shard_map/all_to_all | solution.py:54
  143.6 7.1 %broadcast_in_dim.29 = bf16[2,8,1,4,20,3584]{5,0,4,3,1,2:T(2,128)(2,1)} broadcast(bf16[2,8,20,3584]{3,0,2,1:T(2,128)(2,1)} %copy.45), dimensions={0,1,4,5} | broadcast | bytes 11468800 | tf_op jit(solution)/shard_map/broadcast_in_dim | solution.py:52
  150.7 5.8 all-to-all-start.2
  156.4 7.3 %squeeze_reshape.9 = bf16[640,3584]{1,0:T(8,128)(2,1)} reshape(bf16[1,32,20,3584]{3,2,0,1:T(8,128)(2,1)} %all-to-all-done) | data formatting | bytes 9175040 | tf_op jit(solution)/shard_map/squeeze;reshape | solution.py:114
  163.7 9.8 %convolution_convert_fusion.1 = bf16[640,3584]{1,0:T(8,128)(2,1)} fusion(bf16[1,1,256,3584]{3,2,1,0:T(8,128)(2,1)} %param.17, bf16[640,3584]{1,0:T(8,128)(2,1)} %squeeze_reshape.9, bf16[1,1,3584,256]{3,2,1,0:T(8,128)(2,1)S(1)} %copy-done), kind=kOutput, calls=%fused_computation.5 | convolution fusion | flops 2351923200 | bytes 12845056 | tf_op jit(solution)/shard_map/dot_general | solution.py:71
  173.6 7.2 %reshape_broadcast_in_dim.10 = bf16[1,32,20,3584]{3,2,1,0:T(8,128)(2,1)} reshape(bf16[640,3584]{1,0:T(8,128)(2,1)} %convolution_convert_fusion.1) | data formatting | bytes 9175040 | tf_op jit(solution)/shard_map/reshape;broadcast_in_dim | solution.py:60
  180.8 177.0 %all-to-all-done.2 = bf16[2,32,20,3584]{3,0,2,1:T(2,128)(2,1)} async-done(((bf16[2,32,20,3584]{3,0,2,1:T(2,128)(2,1)}), bf16[2,32,20,3584]{3,0,2,1:T(2,128)(2,1)}, u32[]{:S(2)}, u32[]{:S(2)}) %all-to-all-start.2) | async-done | bytes 9175072 | tf_op jit(solution)/shard_map/all_to_all | solution.py:54
  357.8 5.7 all-to-all-start.1
  363.5 45.7 %slice_reduce_fusion = (bf16[32,20,3584]{2,1,0:T(8,128)(2,1)}, bf16[32,20,3584]{2,1,0:T(8,128)(2,1)}) fusion(bf16[2,32,20,3584]{3,0,2,1:T(2,128)(2,1)} %all-to-all-done.2), kind=kLoop, calls=%fused_computation.2 | loop fusion | bytes 18350080 | tf_op jit(solution)/shard_map/slice | solution.py:117
  409.2 7.3 %squeeze.27 = bf16[640,3584]{1,0:T(8,128)(2,1)} reshape(bf16[32,20,3584]{2,1,0:T(8,128)(2,1)} %get-tuple-element.4) | data formatting | bytes 9175040 | tf_op jit(solution)/shard_map/squeeze | solution.py:117
  416.5 7.3 %squeeze.26 = bf16[640,3584]{1,0:T(8,128)(2,1)} reshape(bf16[32,20,3584]{2,1,0:T(8,128)(2,1)} %get-tuple-element.5) | data formatting | bytes 9175040 | tf_op jit(solution)/shard_map/squeeze | solution.py:117
  423.8 3.8 fusion.8
  427.6 0.5 copy-done.7
  428.0 1.4 fusion.15
  429.4 3.6 convolution_convert_fusion
  433.0 7.3 %reshape_broadcast_in_dim.11 = bf16[1,32,20,3584]{3,2,1,0:T(8,128)(2,1)} reshape(bf16[640,3584]{1,0:T(8,128)(2,1)} %convolution_convert_fusion) | data formatting | bytes 9175040 | tf_op jit(solution)/shard_map/reshape;broadcast_in_dim | solution.py:60
  440.3 45.9 %all-to-all-done.1 = bf16[1,32,20,3584]{3,2,0,1:T(8,128)(2,1)} async-done(((bf16[1,32,20,3584]{3,2,0,1:T(8,128)(2,1)}), bf16[1,32,20,3584]{3,2,0,1:T(8,128)(2,1)}, u32[]{:S(2)}, u32[]{:S(2)}) %all-to-all-start.1) | async-done | bytes 4587552 | tf_op jit(solution)/shard_map/all_to_all | solution.py:61
  486.1 5.7 all-to-all-start.3
  491.8 5.3 convert_reduce_fusion.1
  497.1 2.9 squeeze_reshape.10
  500.1 3.7 fusion.3
  503.8 4.2 collective-permute-start
  508.0 5.8 convolution_bitcast_fusion.1
  513.8 120.4 %all-to-all-done.3 = bf16[1,32,20,3584]{3,2,0,1:T(8,128)(2,1)} async-done(((bf16[1,32,20,3584]{3,2,0,1:T(8,128)(2,1)}), bf16[1,32,20,3584]{3,2,0,1:T(8,128)(2,1)}, u32[]{:S(2)}, u32[]{:S(2)}) %all-to-all-start.3) | async-done | bytes 4587552 | tf_op jit(solution)/shard_map/all_to_all | solution.py:61
  634.2 5.3 convert_reduce_fusion
  639.5 2.9 squeeze_reshape.11
  642.4 0.0 copy-done.3
  642.4 3.0 fusion.2
  645.4 6.5 collective-permute-start.1
  651.9 5.8 convolution_bitcast_fusion
  657.6 0.0 collective-permute-done
  657.6 12.4 %collective-permute-done.1 = bf16[1,64,3584]{2,1,0:T(8,128)(2,1)S(1)} collective-permute-done((bf16[1,64,3584]{2,1,0:T(8,128)(2,1)S(1)}, bf16[1,64,3584]{2,1,0:T(8,128)(2,1)S(1)}, u32[]{:S(2)}, u32[]{:S(2)}) %collective-permute-start.1) | collective-permute-done | bytes 458784 | tf_op jit(solution)/shard_map/ppermute | solution.py:15
  670.0 1.8 copy.51
  671.8 0.8 copy.52
  (12 shorter events, 0.0 us)
Async XLA Ops:
  0.6 163.1 %copy-start = (bf16[1,1,3584,256]{3,2,1,0:T(8,128)(2,1)S(1)}, bf16[1,1,3584,256]{3,2,1,0:T(8,128)(2,1)}, u32[]{:S(2)}) copy-start(bf16[1,1,3584,256]{3,2,1,0:T(8,128)(2,1)} %param.16) | copy-start | bytes 5505028
  10.6 10.4 %copy-start.5 = (s32[1,64,2]{1,2,0:T(2,128)S(1)}, s32[1,64,2]{1,2,0:T(2,128)}, u32[]{:S(2)}) copy-start(s32[1,64,2]{1,2,0:T(2,128)} %param.13) | copy-start | bytes 1540
  10.6 11.3 %copy-start.6 = (f32[1,64,2]{1,2,0:T(2,128)S(1)}, f32[1,64,2]{1,2,0:T(2,128)}, u32[]{:S(2)}) copy-start(f32[1,64,2]{1,2,0:T(2,128)} %param.14) | copy-start | bytes 1540
  10.6 11.4 %copy-start.4 = (bf16[1,64,3584]{2,1,0:T(8,128)(2,1)S(1)}, bf16[1,64,3584]{2,1,0:T(8,128)(2,1)}, u32[]{:S(2)}) copy-start(bf16[1,64,3584]{2,1,0:T(8,128)(2,1)} %param.12) | copy-start | bytes 1376260
  10.6 133.0 %all-to-all-start = ((bf16[1,32,20,3584]{3,2,0,1:T(8,128)(2,1)}), bf16[1,32,20,3584]{3,2,0,1:T(8,128)(2,1)}, u32[]{:S(2)}, u32[]{:S(2)}) async-start(bf16[1,32,20,3584]{3,2,0,1:T(8,128)(2,1)} %bitcast.71), calls=%async_computation | async-start | bytes 11010048 | tf_op jit(solution)/shard_map/all_to_all | solution.py:54
  150.7 207.1 %all-to-all-start.2 = ((bf16[2,32,20,3584]{3,0,2,1:T(2,128)(2,1)}), bf16[2,32,20,3584]{3,0,2,1:T(2,128)(2,1)}, u32[]{:S(2)}, u32[]{:S(2)}) async-start(bf16[2,32,20,3584]{3,0,2,1:T(2,128)(2,1)} %bitcast.70), calls=%async_computation.2 | async-start | bytes 18350080 | tf_op jit(solution)/shard_map/all_to_all | solution.py:54
  357.8 128.4 %all-to-all-start.1 = ((bf16[1,32,20,3584]{3,2,0,1:T(8,128)(2,1)}), bf16[1,32,20,3584]{3,2,0,1:T(8,128)(2,1)}, u32[]{:S(2)}, u32[]{:S(2)}) async-start(bf16[1,32,20,3584]{3,2,0,1:T(8,128)(2,1)} %bitcast.73), calls=%async_computation.1 | async-start | bytes 11010048 | tf_op jit(solution)/shard_map/all_to_all | solution.py:61
  423.8 3.8 copy-start.1
  423.8 4.3 copy-start.7
  486.1 148.0 %all-to-all-start.3 = ((bf16[1,32,20,3584]{3,2,0,1:T(8,128)(2,1)}), bf16[1,32,20,3584]{3,2,0,1:T(8,128)(2,1)}, u32[]{:S(2)}, u32[]{:S(2)}) async-start(bf16[1,32,20,3584]{3,2,0,1:T(8,128)(2,1)} %bitcast.72), calls=%async_computation.3 | async-start | bytes 11010048 | tf_op jit(solution)/shard_map/all_to_all | solution.py:61
  497.1 2.9 copy-start.2
  503.8 153.8 %collective-permute-start = (bf16[1,64,3584]{2,1,0:T(8,128)(2,1)}, bf16[1,64,3584]{2,1,0:T(8,128)(2,1)}, u32[]{:S(2)}, u32[]{:S(2)}) collective-permute-start(bf16[1,64,3584]{2,1,0:T(8,128)(2,1)} %fusion.3), channel_id=1, source_target_pairs={{0,32},{32,64},{64,96},{96,128},{128,160},{160,192},{192,224},{224... | collective-permute-start | bytes 1376264 | tf_op jit(solution)/shard_map/ppermute | solution.py:15
  639.5 2.9 copy-start.3
  645.4 24.6 %collective-permute-start.1 = (bf16[1,64,3584]{2,1,0:T(8,128)(2,1)S(1)}, bf16[1,64,3584]{2,1,0:T(8,128)(2,1)S(1)}, u32[]{:S(2)}, u32[]{:S(2)}) collective-permute-start(bf16[1,64,3584]{2,1,0:T(8,128)(2,1)S(1)} %fusion.2), channel_id=1, source_target_pairs={{0,224},{32,0},{64,32},{96,64},{128,96},{160,128},{192,160},{224,1... | collective-permute-start | bytes 1376264 | tf_op jit(solution)/shard_map/ppermute | solution.py:15
where the time goes:
time: 675 us; the launch traced here: 673 us
  waiting for transfers between devices  464 us (69%)
  local copies, waits for them, and re-layouts  111 us (16%)
  matrix products  44 us (7%)
  starting transfers between devices  38.2 us (6%)
  other arithmetic  14.7 us (2%)
    all_to_all x2, waiting for transfers between devices, send_rows(): lax.all_to_all(copies, 'expert', split_axis=1, concat_axis=1, tiled=True)  285 us
    all_to_all x2, waiting for transfers between devices, send_back(): lax.all_to_all(arranged, 'expert', split_axis=1, concat_axis=1, tiled=True)  166 us
    slice x1, local copies, waits for them, and re-layouts, local(): got_b[0]  45.7 us
    all_to_all x2, starting transfers between devices, send_rows(): lax.all_to_all(copies, 'expert', split_axis=1, concat_axis=1, tiled=True)  16.1 us
    another operation x2, local copies, waits for them, and re-layouts, send_back(): arranged = parts.reshape(count, experts * GROUP, slot_cap, model_width)  14.5 us
  transfers between devices with their start and end apart: 6, of which 5 were waited for; matrix products, arithmetic and copies ran while one was open for 22% of the time, Pallas kernels for 0%

commit v1 on v0

--- a/solution.py
+++ b/solution.py
@@ -49,20 +49,20 @@
 
 def send_rows(stacked, experts, slot_cap):
     count, _, model_width = stacked.shape
-    copies = jnp.repeat(stacked.reshape(count, experts, 1, slot_cap, model_width), GROUP, axis=2)
-    copies = copies.reshape(count, experts * GROUP, slot_cap, model_width)
-    received = lax.all_to_all(copies, "expert", split_axis=1, concat_axis=1, tiled=True)
-    return received.reshape(count, -1, model_width)
+    chunks = stacked.reshape(count, experts, slot_cap, model_width)
+    received = lax.all_to_all(chunks, "eg", split_axis=1, concat_axis=1, tiled=True)
+    gathered = lax.all_gather(received, "em", axis=1, tiled=True)
+    return gathered.reshape(count, -1, model_width)
 
 
 def send_back(parts, experts, slot_cap):
     count, _, model_width = parts.shape
-    arranged = parts.reshape(count, experts * GROUP, slot_cap, model_width)
-    received = lax.all_to_all(arranged, "expert", split_axis=1, concat_axis=1, tiled=True)
-    summed = jnp.sum(
-        received.reshape(count, experts, GROUP, slot_cap, model_width), axis=2, dtype=jnp.float32
-    )
-    return summed.reshape(count, experts * slot_cap, model_width)
+    arranged = parts.reshape(count, GROUP, experts * slot_cap, model_width)
+    received = lax.all_to_all(arranged, "em", split_axis=1, concat_axis=1, tiled=True)
+    summed = jnp.sum(received, axis=1, dtype=jnp.float32).astype(jnp.bfloat16)
+    summed = summed.reshape(count, experts, slot_cap, model_width)
+    back = lax.all_to_all(summed, "eg", split_axis=1, concat_axis=1, tiled=True)
+    return back.reshape(count, experts * slot_cap, model_width).astype(jnp.float32)
 
 
 def expert_forward(rows, up_proj, down_proj):
@@ -93,7 +93,7 @@
 def local(
     fwd_acts, fwd_routes, fwd_gates, back_acts, back_routes, back_gates, back_grads, w_up, w_down
 ):
-    devices = lax.axis_size("expert")
+    devices = lax.axis_size("eg") * lax.axis_size("em")
     experts = devices // GROUP
     tok_rows = fwd_acts.shape[1]
     top_count = fwd_routes.shape[2]
@@ -126,21 +126,24 @@
 
 
 def solution(mesh):
+    groups = mesh.shape["expert"] // GROUP
+    devices = mesh.devices.reshape(mesh.shape["pipe"], groups, GROUP)
+    mesh = jax.sharding.Mesh(devices, ("pipe", "eg", "em"))
     in_specs = (
-        P("pipe", "expert", None),
-        P("pipe", "expert", None),
-        P("pipe", "expert", None),
-        P("pipe", "expert", None),
-        P("pipe", "expert", None),
-        P("pipe", "expert", None),
-        P("pipe", "expert", None),
-        P("pipe", "expert", None, None),
-        P("pipe", "expert", None, None),
+        P("pipe", ("eg", "em"), None),
+        P("pipe", ("eg", "em"), None),
+        P("pipe", ("eg", "em"), None),
+        P("pipe", ("eg", "em"), None),
+        P("pipe", ("eg", "em"), None),
+        P("pipe", ("eg", "em"), None),
+        P("pipe", ("eg", "em"), None),
+        P("pipe", ("eg", "em"), None, None),
+        P("pipe", ("eg", "em"), None, None),
     )
     out_specs = (
-        P("pipe", "expert", None),
-        P("pipe", "expert", None),
-        P("pipe", "expert", None, None),
-        P("pipe", "expert", None, None),
+        P("pipe", ("eg", "em"), None),
+        P("pipe", ("eg", "em"), None),
+        P("pipe", ("eg", "em"), None, None),
+        P("pipe", ("eg", "em"), None, None),
     )
     return jax.shard_map(local, mesh=mesh, in_specs=in_specs, out_specs=out_specs, check_vma=False)

time: 675 us -> 542 us (0.80)
  waiting for transfers between devices: 464 us -> 252 us
  blocking collectives: 0 us -> 93.4 us
  local copies, waits for them, and re-layouts: 111 us -> 97.2 us
  between operations: 0.82 us -> 14.2 us
  starting transfers between devices: 38.2 us -> 28.2 us
    all_to_all x4, waiting for transfers between devices: 451 us -> 114 us  [the longest x2 67.4 us: send_back(): back = lax.all_to_all(summed, 'eg', split_axis=1, concat_axis=1, tiled=True)]
    all_gather x0 -> x2, waiting for transfers between devices: none -> 123 us  [send_rows(): gathered = lax.all_gather(received, 'em', axis=1, tiled=True)]
    all_to_all x0 -> x2, blocking collectives: none -> 93.4 us  [send_rows(): lax.all_to_all(chunks, 'eg', split_axis=1, concat_axis=1, tiled=True)]
    another operation x5 -> x1, local copies, waits for them, and re-layouts: 21.7 us -> 1.37 us  [send_rows(): chunks = stacked.reshape(count, experts, slot_cap, model_width)]
    broadcast_in_dim x2 -> x0, local copies, waits for them, and re-layouts: 9.96 us -> none  [send_rows(): jnp.repeat(stacked.reshape(count, experts, 1, slot_cap, model_width), GRO...]
    all_to_all x4, starting transfers between devices: 27.5 us -> 19.7 us  [the longest x2 10.2 us: send_back(): lax.all_to_all(arranged, 'em', split_axis=1, concat_axis=1, tiled=True)]
    all_gather x0 -> x1, local copies, waits for them, and re-layouts: none -> 7.32 us  [send_rows(): gathered = lax.all_gather(received, 'em', axis=1, tiled=True)]
  transfers between devices with their start and end apart: 6 -> 8, of which waited for: 5 -> 6; matrix products, arithmetic and copies ran while one was open for 22% -> 26% of each run, Pallas kernels for 0% -> 0%
where the time goes in v1:
time: 542 us; the launch traced here: 540 us
  waiting for transfers between devices  252 us (46%)
  local copies, waits for them, and re-layouts  97.2 us (18%)
  blocking collectives  93.4 us (17%)
  matrix products  42.9 us (8%)
  starting transfers between devices  28.2 us (5%)
  between operations  14.2 us (3%)
  other arithmetic  12.1 us (2%)
    all_gather x2, waiting for transfers between devices, send_rows(): gathered = lax.all_gather(received, 'em', axis=1, tiled=True)  123 us
    all_to_all x2, blocking collectives, send_rows(): lax.all_to_all(chunks, 'eg', split_axis=1, concat_axis=1, tiled=True)  93.4 us
    all_to_all x2, waiting for transfers between devices, send_back(): back = lax.all_to_all(summed, 'eg', split_axis=1, concat_axis=1, tiled=True)  67.4 us
    all_to_all x2, waiting for transfers between devices, send_back(): lax.all_to_all(arranged, 'em', split_axis=1, concat_axis=1, tiled=True)  46.2 us
    slice x1, local copies, waits for them, and re-layouts, local(): got_b[0]  45.6 us
    ppermute x2, waiting for transfers between devices, passed_along(): return lax.ppermute(value, axis, pairs)  15.2 us
  transfers between devices with their start and end apart: 8, of which 6 were waited for; matrix products, arithmetic and copies ran while one was open for 26% of the time, Pallas kernels for 0%

profile of v1, /device:TPU:1, one launch (start us, length us, event | category | flops | bytes accessed | tf_op | source)
XLA Modules:
  0.0 540.3 jit_solution(244298509199671782)
XLA Ops:
  7.2 0.9 copy.61
  8.1 0.1 eq.58
  8.3 0.1 fusion.28
  8.4 0.2 reduce_window_sum.17
  8.5 0.2 select_reduce_fusion.3
  8.7 0.1 reduce_sum.83
  8.9 0.1 copy.62
  8.9 0.7 bitcast_add_fusion.1
  9.6 1.4 convert_reduce_fusion.1
  11.0 2.5 convolution_convert_fusion.4
  13.5 1.4 reshape_broadcast_in_dim.9
  14.9 41.2 %all_to_all.30 = bf16[1,8,20,3584]{3,2,0,1:T(8,128)(2,1)S(1)} all-to-all(bf16[1,8,20,3584]{3,2,0,1:T(8,128)(2,1)S(1)} %bitcast.73), channel_id=1, replica_groups=mesh['pipe'=8,'eg'=8,'em'=4] {'eg'}, dimensions={1} | all-to-all | bytes 2293760 | tf_op jit(solution)/shard_map/all_to_all | solution.py:53
  56.1 1.3 copy.64
  57.5 0.1 copy.68
  57.6 0.1 eq.65
  57.7 0.1 fusion.27
  57.8 0.2 reduce_window_sum.18
  58.0 0.2 select_reduce_fusion.2
  58.2 0.1 reduce_sum.88
  58.3 0.1 copy.69
  58.4 0.1 select_reduce_fusion
  58.6 0.6 copy-done.5
  59.2 1.5 convolution_convert_fusion.3
  60.6 1.4 stack.9
  62.0 3.1 convolution_convert_fusion.2
  65.1 2.3 stack.10
  67.4 1.7 pad_maximum_fusion
  69.1 2.4 copy.70
  71.4 52.3 %all_to_all.31 = bf16[2,8,20,3584]{3,0,2,1:T(2,128)(2,1)} all-to-all(bf16[2,8,20,3584]{3,0,2,1:T(2,128)(2,1)S(1)} %copy.70), channel_id=1, replica_groups=mesh['pipe'=8,'eg'=8,'em'=4] {'eg'}, dimensions={1} | all-to-all | bytes 4587520 | tf_op jit(solution)/shard_map/all_to_all | solution.py:53
  123.7 12.2 %all-gather.3.cloned.1.call-done = bf16[1,32,20,3584]{3,1,2,0:T(8,128)(2,1)} async-done(((bf16[1,8,20,3584]{3,1,2,0:T(8,128)(2,1)}), bf16[1,32,20,3584]{3,1,2,0:T(8,128)(2,1)}) %all-gather.3.cloned.1.call-update) | async-done | bytes 4587536 | tf_op jit(solution)/shard_map/all_gather | solution.py:54
  135.9 7.3 %copy.65 = bf16[1,32,20,3584]{3,2,1,0:T(8,128)(2,1)} copy(bf16[1,32,20,3584]{3,1,2,0:T(8,128)(2,1)} %all-gather.3.cloned.1.call-done) | data formatting | bytes 9175040 | tf_op jit(solution)/shard_map/all_gather | solution.py:54
  143.2 7.4 %squeeze_reshape.3 = bf16[640,3584]{1,0:T(8,128)(2,1)} reshape(bf16[1,32,20,3584]{3,2,1,0:T(8,128)(2,1)} %copy.65) | data formatting | bytes 9175040 | tf_op jit(solution)/shard_map/squeeze;reshape | solution.py:114
  150.6 10.6 %convolution_convert_fusion.1 = bf16[640,3584]{1,0:T(8,128)(2,1)} fusion(bf16[1,1,256,3584]{3,2,1,0:T(8,128)(2,1)} %param.17, bf16[640,3584]{1,0:T(8,128)(2,1)} %squeeze_reshape.3, bf16[1,1,3584,256]{3,2,1,0:T(8,128)(2,1)S(1)} %copy-done), kind=kOutput, calls=%fused_computation.3 | convolution fusion | flops 2351923200 | bytes 12845056 | tf_op jit(solution)/shard_map/dot_general | solution.py:71
  161.2 5.2 all-to-all-start.1
  166.5 111.3 %all-gather.5.cloned.1.call-done = bf16[2,32,20,3584]{3,0,2,1:T(2,128)(2,1)} async-done(((bf16[2,8,20,3584]{3,0,2,1:T(2,128)(2,1)}), bf16[2,32,20,3584]{3,0,2,1:T(2,128)(2,1)}) %all-gather.5.cloned.1.call-update) | async-done | bytes 9175056 | tf_op jit(solution)/shard_map/all_gather | solution.py:54
  277.7 45.6 %slice_reduce_fusion = (bf16[32,20,3584]{2,1,0:T(8,128)(2,1)}, bf16[32,20,3584]{2,1,0:T(8,128)(2,1)}) fusion(bf16[2,32,20,3584]{3,0,2,1:T(2,128)(2,1)} %all-gather.5.cloned.1.call-done), kind=kLoop, calls=%fused_computation | loop fusion | bytes 18350080 | tf_op jit(solution)/shard_map/slice | solution.py:117
  323.3 7.3 %squeeze.34 = bf16[640,3584]{1,0:T(8,128)(2,1)} reshape(bf16[32,20,3584]{2,1,0:T(8,128)(2,1)} %get-tuple-element.4) | data formatting | bytes 9175040 | tf_op jit(solution)/shard_map/squeeze | solution.py:117
  330.6 7.3 %squeeze.33 = bf16[640,3584]{1,0:T(8,128)(2,1)} reshape(bf16[32,20,3584]{2,1,0:T(8,128)(2,1)} %get-tuple-element.5) | data formatting | bytes 9175040 | tf_op jit(solution)/shard_map/squeeze | solution.py:117
  337.9 3.8 fusion.8
  341.7 0.8 copy-done.3
  342.5 1.4 fusion.15
  343.9 3.6 convolution_convert_fusion
  347.5 4.9 all-to-all-start.4
  352.4 3.1 reduce_sum.86
  355.5 1.2 reshape.76
  356.7 46.2 %all-to-all-done.4 = bf16[1,4,160,3584]{3,2,0,1:T(8,128)(2,1)} async-done(((bf16[1,4,160,3584]{3,2,0,1:T(8,128)(2,1)}), bf16[1,4,160,3584]{3,2,0,1:T(8,128)(2,1)}, u32[]{:S(2)}, u32[]{:S(2)}) %all-to-all-start.4) | async-done | bytes 4587552 | tf_op jit(solution)/shard_map/all_to_all | solution.py:61
  402.9 6.0 %all-to-all-start.2 = ((bf16[1,8,20,3584]{3,2,0,1:T(8,128)(2,1)}), bf16[1,8,20,3584]{3,2,0,1:T(8,128)(2,1)S(1)}, u32[]{:S(2)}, u32[]{:S(2)}) async-start(bf16[1,8,20,3584]{3,2,0,1:T(8,128)(2,1)} %bitcast.72), calls=%async_computation.2 | async-start | bytes 2752512 | tf_op jit(solution)/shard_map/all_to_all | solution.py:64
  408.9 4.3 reduce_sum.91
  413.2 2.3 reshape.77
  415.4 28.6 %all-to-all-done.2 = bf16[1,8,20,3584]{3,2,0,1:T(8,128)(2,1)S(1)} async-done(((bf16[1,8,20,3584]{3,2,0,1:T(8,128)(2,1)}), bf16[1,8,20,3584]{3,2,0,1:T(8,128)(2,1)S(1)}, u32[]{:S(2)}, u32[]{:S(2)}) %all-to-all-start.2) | async-done | bytes 1146912 | tf_op jit(solution)/shard_map/all_to_all | solution.py:64
  444.0 1.1 copy-done.2
  445.1 3.6 all-to-all-start.5
  448.7 2.2 squeeze.30
  450.9 2.8 fusion.3
  453.7 3.6 collective-permute-start
  457.3 5.8 %convolution_bitcast_fusion.1 = f32[1,1,3584,256]{3,2,1,0:T(8,128)} fusion(bf16[640,3584]{1,0:T(8,128)(2,1)} %squeeze.34, bf16[640,256]{1,0:T(8,128)(2,1)S(1)} %fusion.15), kind=kOutput, calls=%fused_computation.5 | convolution fusion | flops 1174405120 | bytes 8585216 | tf_op jit(solution)/shard_map/dot_general | solution.py:84
  463.1 38.9 %all-to-all-done.5 = bf16[1,8,20,3584]{3,2,0,1:T(8,128)(2,1)S(1)} async-done(((bf16[1,8,20,3584]{3,2,0,1:T(8,128)(2,1)}), bf16[1,8,20,3584]{3,2,0,1:T(8,128)(2,1)S(1)}, u32[]{:S(2)}, u32[]{:S(2)}) %all-to-all-start.5) | async-done | bytes 1146912 | tf_op jit(solution)/shard_map/all_to_all | solution.py:64
  501.9 1.1 squeeze.35
  503.1 2.0 fusion.2
  505.1 4.8 collective-permute-start.1
  510.0 5.8 %convolution_bitcast_fusion = f32[1,1,256,3584]{3,2,1,0:T(8,128)} fusion(bf16[640,3584]{1,0:T(8,128)(2,1)} %squeeze.33, f32[640,256]{1,0:T(8,128)S(1)} %copy-done.4), kind=kOutput, calls=%fused_computation.4 | convolution fusion | flops 1175224320 | bytes 8912896 | tf_op jit(solution)/shard_map/dot_general | solution.py:87
  515.7 15.2 %collective-permute-done.1 = bf16[1,64,3584]{2,1,0:T(8,128)(2,1)S(1)} collective-permute-done((bf16[1,64,3584]{2,1,0:T(8,128)(2,1)S(1)}, bf16[1,64,3584]{2,1,0:T(8,128)(2,1)S(1)}, u32[]{:S(2)}, u32[]{:S(2)}) %collective-permute-start.1) | collective-permute-done | bytes 458784 | tf_op jit(solution)/shard_map/ppermute | solution.py:15
  530.9 1.8 copy.77
  532.7 0.8 copy.78
  (26 shorter events, 0.2 us)
Async XLA Ops:
  7.2 143.4 %copy-start = (bf16[1,1,3584,256]{3,2,1,0:T(8,128)(2,1)S(1)}, bf16[1,1,3584,256]{3,2,1,0:T(8,128)(2,1)}, u32[]{:S(2)}) copy-start(bf16[1,1,3584,256]{3,2,1,0:T(8,128)(2,1)} %param.16) | copy-start | bytes 5505028
  7.2 128.7 %all-gather.3.cloned.1.call-start = ((), (), s32[]{:S(2)}) async-start(), calls=%async_computation.6 | async-start | bytes 5734400 | tf_op jit(solution)/shard_map/all_gather | solution.py:54
  56.1 1.4 copy-start.8
  56.1 2.3 copy-start.9
  56.1 3.1 copy-start.7
  57.5 220.3 %all-gather.5.cloned.1.call-start = ((), (), s32[]{:S(2)}) async-start(), calls=%async_computation.7 | async-start | bytes 11468800 | tf_op jit(solution)/shard_map/all_gather | solution.py:54
  58.5 0.6 copy-start.5
  161.2 186.3 %all-to-all-start.1 = ((bf16[1,4,160,3584]{3,2,0,1:T(8,128)(2,1)}), bf16[1,4,160,3584]{3,2,0,1:T(8,128)(2,1)}, u32[]{:S(2)}, u32[]{:S(2)}) async-start(bf16[1,4,160,3584]{3,2,0,1:T(8,128)(2,1)} %bitcast.74), calls=%async_computation.1 | async-start | bytes 9175040 | tf_op jit(solution)/shard_map/all_to_all | solution.py:61
  337.9 4.7 copy-start.1
  337.9 4.7 copy-start.10
  341.7 0.9 copy-start.3
  347.5 55.4 %all-to-all-start.4 = ((bf16[1,4,160,3584]{3,2,0,1:T(8,128)(2,1)}), bf16[1,4,160,3584]{3,2,0,1:T(8,128)(2,1)}, u32[]{:S(2)}, u32[]{:S(2)}) async-start(bf16[1,4,160,3584]{3,2,0,1:T(8,128)(2,1)} %bitcast.71), calls=%async_computation.4 | async-start | bytes 9175040 | tf_op jit(solution)/shard_map/all_to_all | solution.py:61
  402.9 41.1 %all-to-all-start.2 = ((bf16[1,8,20,3584]{3,2,0,1:T(8,128)(2,1)}), bf16[1,8,20,3584]{3,2,0,1:T(8,128)(2,1)S(1)}, u32[]{:S(2)}, u32[]{:S(2)}) async-start(bf16[1,8,20,3584]{3,2,0,1:T(8,128)(2,1)} %bitcast.72), calls=%async_computation.2 | async-start | bytes 2752512 | tf_op jit(solution)/shard_map/all_to_all | solution.py:64
  444.0 1.1 copy-start.2
  445.1 56.8 %all-to-all-start.5 = ((bf16[1,8,20,3584]{3,2,0,1:T(8,128)(2,1)}), bf16[1,8,20,3584]{3,2,0,1:T(8,128)(2,1)S(1)}, u32[]{:S(2)}, u32[]{:S(2)}) async-start(bf16[1,8,20,3584]{3,2,0,1:T(8,128)(2,1)} %bitcast.16), calls=%async_computation.5 | async-start | bytes 2752512 | tf_op jit(solution)/shard_map/all_to_all | solution.py:64
  453.7 62.1 %collective-permute-start = (bf16[1,64,3584]{2,1,0:T(8,128)(2,1)}, bf16[1,64,3584]{2,1,0:T(8,128)(2,1)}, u32[]{:S(2)}, u32[]{:S(2)}) collective-permute-start(bf16[1,64,3584]{2,1,0:T(8,128)(2,1)} %fusion.3), channel_id=1, source_target_pairs={{0,32},{32,64},{64,96},{96,128},{128,160},{160,192},{192,224},{224... | collective-permute-start | bytes 1376264 | tf_op jit(solution)/shard_map/ppermute | solution.py:15
  463.1 40.0 %copy-start.6 = (f32[64,160]{1,0:T(8,128)S(1)}, f32[64,160]{1,0:T(8,128)}, u32[]{:S(2)}) copy-start(f32[64,160]{1,0:T(8,128)} %copy-done.5) | copy-start | bytes 122884
  503.1 6.9 %copy-start.4 = (f32[640,256]{1,0:T(8,128)S(1)}, f32[640,256]{1,0:T(8,128)}, u32[]{:S(2)}) copy-start(f32[640,256]{1,0:T(8,128)} %copy-done.3) | copy-start | bytes 1966084
  505.1 25.8 %collective-permute-start.1 = (bf16[1,64,3584]{2,1,0:T(8,128)(2,1)S(1)}, bf16[1,64,3584]{2,1,0:T(8,128)(2,1)S(1)}, u32[]{:S(2)}, u32[]{:S(2)}) collective-permute-start(bf16[1,64,3584]{2,1,0:T(8,128)(2,1)S(1)} %fusion.2), channel_id=1, source_target_pairs={{0,224},{32,0},{64,32},{96,64},{128,96},{160,128},{192,160},{224,1... | collective-permute-start | bytes 1376264 | tf_op jit(solution)/shard_map/ppermute | solution.py:15
Sparse Core Ops, SparseCore 0:
  57.6 78.2 all-gather.2
  137.7 140.0 all-gather.4

commit v2 on v0

v2 whole, which is shorter than its diff:
```python
import jax
import jax.numpy as jnp
from jax import lax
from jax.sharding import PartitionSpec as P

GROUP = 4


HIGH = lax.Precision.HIGHEST


def passed_along(value, axis, steps):
    count = lax.axis_size(axis)
    pairs = [(source, (source + steps) % count) for source in range(count)]
    return lax.ppermute(value, axis, pairs)


def silu_grad(value):
    sigma = jax.nn.sigmoid(value)
    return sigma * (1.0 + value * (1.0 - sigma))


def tables(routes, gates, experts, slot_cap):
    tok_rows, top_count = routes.shape
    flat = routes.reshape(tok_rows * top_count)
    onehot = (flat[:, None] == jnp.arange(experts, dtype=jnp.int32)[None, :]).astype(jnp.int32)
    before = jnp.cumsum(onehot, axis=0) - onehot
    slots = jnp.sum(before * onehot, axis=1)
    places = flat * slot_cap + slots
    columns = jnp.arange(experts * slot_cap, dtype=jnp.int32)
    hits = (
        (places[:, None] == columns[None, :])
        .astype(jnp.float32)
        .reshape(tok_rows, top_count, experts * slot_cap)
    )
    plain = jnp.sum(hits, axis=1)
    gated = jnp.sum(hits * gates[:, :, None], axis=1)
    return (plain, gated)


def gather_rows(plain, values):
    return lax.dot_general(
        plain.astype(jnp.bfloat16),
        values,
        (((0,), (0,)), ((), ())),
        preferred_element_type=jnp.float32,
    ).astype(jnp.bfloat16)


def to_wire(rows, *lead):
    return rows.reshape(*lead, -1, 128)


def send_rows(rows, experts, slot_cap):
    model_width = rows.shape[-1]
    chunks = to_wire(rows, experts)
    received = lax.all_to_all(chunks, "eg", split_axis=0, concat_axis=0, tiled=True)
    across = lax.all_gather(received, "ez", axis=0)
    gathered = lax.all_gather(across, "ec", axis=0)
    return gathered.reshape(-1, model_width)


def send_back(parts, experts):
    model_width = parts.shape[-1]
    wire = to_wire(parts, 2, 2, experts)
    mine = lax.all_to_all(wire, "ec", split_axis=0, concat_axis=0, tiled=True)
    pair = jnp.sum(mine.astype(jnp.float32), axis=0)
    other = lax.all_to_all(pair, "ez", split_axis=0, concat_axis=0, tiled=True)
    summed = jnp.sum(other, axis=0).astype(jnp.bfloat16)
    back = lax.all_to_all(summed, "eg", split_axis=0, concat_axis=0, tiled=True)
    return back.reshape(-1, model_width).astype(jnp.float32)


def expert_forward(rows, up_proj, down_proj):
    pre = jnp.einsum("...d,df->...f", rows, up_proj, preferred_element_type=jnp.float32)
    act = jax.nn.silu(pre).astype(jnp.bfloat16)
    return jnp.einsum(
        "...f,fd->...d", act, down_proj, preferred_element_type=jnp.float32
    ).astype(jnp.bfloat16)


def expert_backward(rows, grad_rows, up_proj, down_proj):
    pre = jnp.einsum("...d,df->...f", rows, up_proj, preferred_element_type=jnp.float32)
    act = jax.nn.silu(pre).astype(jnp.bfloat16)
    dact = jnp.einsum("...d,fd->...f", grad_rows, down_proj, preferred_element_type=jnp.float32)
    dpre = (dact * silu_grad(pre)).astype(jnp.bfloat16)
    dpart = jnp.einsum(
        "...f,df->...d", dpre, up_proj, preferred_element_type=jnp.float32
    ).astype(jnp.bfloat16)
    grad_up = jnp.einsum("rd,rf->df", rows, dpre, preferred_element_type=jnp.float32)
    grad_down = jnp.einsum("rf,rd->fd", act, grad_rows, preferred_element_type=jnp.float32)
    return (dpart, grad_up, grad_down)


def local(
    fwd_acts, fwd_routes, fwd_gates, back_acts, back_routes, back_gates, back_grads, w_up, w_down
):
    devices = lax.axis_size("eg") * GROUP
    experts = devices // GROUP
    tok_rows = fwd_acts.shape[1]
    top_count = fwd_routes.shape[2]
    slot_cap = GROUP * (5 * tok_rows * top_count // (4 * devices))
    up_proj = w_up[0, 0]
    down_proj = w_down[0, 0]
    fwd_input = fwd_acts[0]
    back_input = back_acts[0]
    out_grad = back_grads[0]
    plain_f, gated_f = tables(fwd_routes[0], fwd_gates[0], experts, slot_cap)
    plain_b, gated_b = tables(back_routes[0], back_gates[0], experts, slot_cap)
    buffer_f = gather_rows(plain_f, fwd_input)
    buffer_x = gather_rows(plain_b, back_input)
    buffer_g = lax.dot_general(
        gated_b, out_grad.astype(jnp.float32), (((0,), (0,)), ((), ())), precision=HIGH
    ).astype(jnp.bfloat16)
    got_f = send_rows(buffer_f, experts, slot_cap)
    part = expert_forward(got_f, up_proj, down_proj)
    summed_f = send_back(part, experts)
    got_x = send_rows(buffer_x, experts, slot_cap)
    got_g = send_rows(buffer_g, experts, slot_cap)
    dpart, grad_up, grad_down = expert_backward(got_x, got_g, up_proj, down_proj)
    summed_b = send_back(dpart, experts)
    merged = jnp.dot(gated_f, summed_f, precision=HIGH)
    section_out = (fwd_input.astype(jnp.float32) + merged).astype(jnp.bfloat16)
    spread_back = jnp.dot(plain_b, summed_b, precision=HIGH)
    section_grad = (out_grad.astype(jnp.float32) + spread_back).astype(jnp.bfloat16)
    fwd_next = passed_along(section_out[None], "pipe", 1)
    back_next = passed_along(section_grad[None], "pipe", -1)
    return (fwd_next, back_next, grad_up[None, None], grad_down[None, None])


def solution(mesh):
    groups = mesh.shape["expert"] // GROUP
    devices = mesh.devices.reshape(mesh.shape["pipe"], groups, 2, GROUP // 2)
    mesh = jax.sharding.Mesh(devices, ("pipe", "eg", "ez", "ec"))
    in_specs = (
        P("pipe", ("eg", "ez", "ec"), None),
        P("pipe", ("eg", "ez", "ec"), None),
        P("pipe", ("eg", "ez", "ec"), None),
        P("pipe", ("eg", "ez", "ec"), None),
        P("pipe", ("eg", "ez", "ec"), None),
        P("pipe", ("eg", "ez", "ec"), None),
        P("pipe", ("eg", "ez", "ec"), None),
        P("pipe", ("eg", "ez", "ec"), None, None),
        P("pipe", ("eg", "ez", "ec"), None, None),
    )
    out_specs = (
        P("pipe", ("eg", "ez", "ec"), None),
        P("pipe", ("eg", "ez", "ec"), None),
        P("pipe", ("eg", "ez", "ec"), None, None),
        P("pipe", ("eg", "ez", "ec"), None, None),
    )
    return jax.shard_map(local, mesh=mesh, in_specs=in_specs, out_specs=out_specs, check_vma=False)
```

time: 675 us -> 553 us (0.82)
  waiting for transfers between devices: 464 us -> 273 us
  blocking collectives: 0 us -> 67.4 us
  local copies, waits for them, and re-layouts: 111 us -> 62.3 us
  starting transfers between devices: 38.2 us -> 66.2 us
  between operations: 0.82 us -> 14.4 us
  other arithmetic: 14.7 us -> 24.5 us
    all_to_all x4 -> x7, waiting for transfers between devices: 451 us -> 177 us  [the longest x2 93.1 us: send_back(): other = lax.all_to_all(pair, 'ez', split_axis=0, concat_axis=0, tiled=True)]
    all_gather x0 -> x6, waiting for transfers between devices: none -> 86.4 us  [the longest x3 64 us: send_rows(): across = lax.all_gather(received, 'ez', axis=0)]
    all_to_all x0 -> x2, blocking collectives: none -> 67.4 us  [send_rows(): lax.all_to_all(chunks, 'eg', split_axis=0, concat_axis=0, tiled=True)]
    reshape x1 -> x10, local copies, waits for them, and re-layouts: 3.74 us -> 56.9 us  [the longest x3 27.7 us: send_rows(): return gathered.reshape(-1, model_width)]
    slice x1 -> x0, local copies, waits for them, and re-layouts: 45.7 us -> none  [local(): got_b[0]]
    another operation x8 -> x0, local copies, waits for them, and re-layouts: 32.6 us -> none  [the longest x2 14.5 us: send_back(): arranged = parts.reshape(count, experts * GROUP, slot_cap, model_width)]
    ppermute x2, starting transfers between devices: 10.7 us -> 25.6 us  [passed_along(): return lax.ppermute(value, axis, pairs)]
    squeeze x2 -> x0, local copies, waits for them, and re-layouts: 14.5 us -> none  [the longest x1 7.27 us: local(): got_b[0]]
  transfers between devices with their start and end apart: 6 -> 15, of which waited for: 5 -> 9; matrix products, arithmetic and copies ran while one was open for 22% -> 21% of each run, Pallas kernels for 0% -> 0%
where the time goes in v2:
time: 553 us; the launch traced here: 548 us
  waiting for transfers between devices  273 us (49%)
  blocking collectives  67.4 us (12%)
  starting transfers between devices  66.2 us (12%)
  local copies, waits for them, and re-layouts  62.3 us (11%)
  matrix products  40.7 us (7%)
  other arithmetic  24.5 us (4%)
  between operations  14.4 us (3%)
    all_to_all x2, waiting for transfers between devices, send_back(): other = lax.all_to_all(pair, 'ez', split_axis=0, concat_axis=0, tiled=True)  93.1 us
    all_to_all x2, blocking collectives, send_rows(): lax.all_to_all(chunks, 'eg', split_axis=0, concat_axis=0, tiled=True)  67.4 us
    all_gather x3, waiting for transfers between devices, send_rows(): across = lax.all_gather(received, 'ez', axis=0)  64 us
    all_to_all x2, waiting for transfers between devices, send_back(): back = lax.all_to_all(summed, 'eg', split_axis=0, concat_axis=0, tiled=True)  57.7 us
    reshape x3, local copies, waits for them, and re-layouts, send_rows(): return gathered.reshape(-1, model_width)  27.7 us
    all_to_all x1, waiting for transfers between devices, send_rows(): lax.all_to_all(chunks, 'eg', split_axis=0, concat_axis=0, tiled=True)  26.6 us
    reshape x5, local copies, waits for them, and re-layouts, to_wire(): return rows.reshape(*lead, -1, 128)  25.9 us
    ppermute x2, starting transfers between devices, passed_along(): return lax.ppermute(value, axis, pairs)  25.6 us
  transfers between devices with their start and end apart: 15, of which 9 were waited for; matrix products, arithmetic and copies ran while one was open for 21% of the time, Pallas kernels for 0%

profile of v2, /device:TPU:1, one launch (start us, length us, event | category | flops | bytes accessed | tf_op | source)
XLA Modules:
  0.0 548.4 jit_solution(14333742434930892565)
XLA Ops:
  7.2 0.9 copy.37
  8.1 0.1 eq.58
  8.2 0.1 fusion.28
  8.3 0.2 reduce_window_sum.17
  8.5 0.2 select_reduce_fusion.3
  8.7 0.1 reduce_sum.95
  8.9 0.7 bitcast_add_fusion.1
  9.6 1.4 convert_reduce_fusion.3
  11.0 1.5 convolution_convert_fusion.4
  12.5 2.3 reshape.82
  14.8 7.9 %all-to-all-start = ((bf16[8,560,128]{2,1,0:T(8,128)(2,1)}), bf16[8,560,128]{2,1,0:T(8,128)(2,1)S(1)}, u32[]{:S(2)}, u32[]{:S(2)}) async-start(bf16[8,560,128]{2,1,0:T(8,128)(2,1)} %reshape.82), calls=%async_computation | async-start | bytes 2293760 | tf_op jit(solution)/shard_map/all_to_all | solution.py:57
  22.7 0.1 copy.39
  22.8 0.1 eq.65
  22.9 0.7 fusion.27
  23.7 1.0 reduce_window_sum.18
  24.7 0.2 select_reduce_fusion.2
  24.9 0.1 reduce_sum.101
  25.1 26.6 %all-to-all-done = bf16[8,560,128]{2,1,0:T(8,128)(2,1)S(1)} async-done(((bf16[8,560,128]{2,1,0:T(8,128)(2,1)}), bf16[8,560,128]{2,1,0:T(8,128)(2,1)S(1)}, u32[]{:S(2)}, u32[]{:S(2)}) %all-to-all-start) | async-done | bytes 1146912 | tf_op jit(solution)/shard_map/all_to_all | solution.py:57
  51.7 1.0 copy-done.2
  52.8 0.7 select_reduce_fusion
  53.5 0.5 convolution_convert_fusion.2
  54.0 2.3 reshape.88
  56.3 34.7 %all_to_all.45 = bf16[8,560,128]{2,1,0:T(8,128)(2,1)} all-to-all(bf16[8,560,128]{2,1,0:T(8,128)(2,1)} %reshape.88), channel_id=1, replica_groups=mesh['pipe'=8,'eg'=8,'ez'=2,'ec'=2] {'eg'}, dimensions={0} | all-to-all | bytes 2293760 | tf_op jit(solution)/shard_map/all_to_all | solution.py:57
  91.1 1.9 convolution_convert_fusion.3
  93.1 2.3 reshape.86
  95.3 32.7 %all_to_all.46 = bf16[8,560,128]{2,1,0:T(8,128)(2,1)} all-to-all(bf16[8,560,128]{2,1,0:T(8,128)(2,1)} %reshape.86), channel_id=1, replica_groups=mesh['pipe'=8,'eg'=8,'ez'=2,'ec'=2] {'eg'}, dimensions={0} | all-to-all | bytes 2293760 | tf_op jit(solution)/shard_map/all_to_all | solution.py:57
  128.1 0.5 all-gather.15.cloned.1.call-update
  128.7 21.9 %all-gather.21.cloned.1.call-done = bf16[16,560,128]{2,1,0:T(8,128)(2,1)} async-done(((bf16[8,560,128]{2,1,0:T(8,128)(2,1)}), bf16[16,560,128]{2,1,0:T(8,128)(2,1)}) %all-gather.21.cloned.1.call-update) | async-done | bytes 2293776 | tf_op jit(solution)/shard_map/all_gather | solution.py:58
  150.7 42.0 %all-gather.17.cloned.1.call-done = bf16[16,560,128]{2,1,0:T(8,128)(2,1)} async-done(((bf16[8,560,128]{2,1,0:T(8,128)(2,1)}), bf16[16,560,128]{2,1,0:T(8,128)(2,1)}) %all-gather.17.cloned.1.call-update) | async-done | bytes 2293776 | tf_op jit(solution)/shard_map/all_gather | solution.py:58
  192.7 22.4 %all-gather.15.cloned.1.call-done = bf16[4,8,560,128]{3,2,1,0:T(8,128)(2,1)} async-done(((bf16[2,8,560,128]{3,2,1,0:T(8,128)(2,1)}), bf16[4,8,560,128]{3,2,1,0:T(8,128)(2,1)}) %all-gather.15.cloned.1.call-update) | async-done | bytes 4587536 | tf_op jit(solution)/shard_map/all_gather | solution.py:59
  215.1 9.0 %reshape.83 = bf16[640,3584]{1,0:T(8,128)(2,1)} reshape(bf16[4,8,560,128]{3,2,1,0:T(8,128)(2,1)} %all-gather.15.cloned.1.call-done) | data formatting | bytes 9175040 | tf_op jit(solution)/shard_map/reshape | solution.py:60
  224.1 10.2 %convolution_convert_fusion.1 = bf16[640,3584]{1,0:T(8,128)(2,1)} fusion(bf16[1,1,256,3584]{3,2,1,0:T(8,128)(2,1)} %param.17, bf16[640,3584]{1,0:T(8,128)(2,1)} %reshape.83, bf16[1,1,3584,256]{3,2,1,0:T(8,128)(2,1)S(1)} %copy-done), kind=kOutput, calls=%fused_computation.3 | convolution fusion | flops 2351923200 | bytes 12845056 | tf_op jit(solution)/shard_map/...f,fd->...d/dot_general | solution.py:77
  234.3 9.5 %reshape.84 = bf16[2,2,8,560,128]{4,3,2,1,0:T(8,128)(2,1)} reshape(bf16[640,3584]{1,0:T(8,128)(2,1)} %convolution_convert_fusion.1) | data formatting | bytes 9175040 | tf_op jit(solution)/shard_map/reshape | solution.py:51
  243.9 5.9 %all-to-all-start.1 = ((bf16[2,2,8,560,128]{4,3,2,1,0:T(8,128)(2,1)}), bf16[2,2,8,560,128]{4,3,2,1,0:T(8,128)(2,1)}, u32[]{:S(2)}, u32[]{:S(2)}) async-start(bf16[2,2,8,560,128]{4,3,2,1,0:T(8,128)(2,1)} %reshape.84), calls=%async_computation.1 | async-start | bytes 9175040 | tf_op jit(solution)/shard_map/all_to_all | solution.py:66
  249.8 9.4 %reshape.89 = bf16[640,3584]{1,0:T(8,128)(2,1)} reshape(bf16[4,8,560,128]{3,2,1,0:T(8,128)(2,1)} %all-gather.23.cloned.1.call-done) | data formatting | bytes 9175040 | tf_op jit(solution)/shard_map/reshape | solution.py:60
  259.2 3.6 fusion.8
  262.9 9.3 %reshape.87 = bf16[640,3584]{1,0:T(8,128)(2,1)} reshape(bf16[4,8,560,128]{3,2,1,0:T(8,128)(2,1)} %all-gather.19.cloned.1.call-done) | data formatting | bytes 9175040 | tf_op jit(solution)/shard_map/reshape | solution.py:60
  272.1 4.3 fusion.15
  276.4 3.6 convolution_convert_fusion
  280.0 9.5 %reshape.90 = bf16[2,2,8,560,128]{4,3,2,1,0:T(8,128)(2,1)} reshape(bf16[640,3584]{1,0:T(8,128)(2,1)} %convolution_convert_fusion) | data formatting | bytes 9175040 | tf_op jit(solution)/shard_map/reshape | solution.py:51
  289.5 5.8 %all-to-all-start.6 = ((bf16[2,2,8,560,128]{4,3,2,1,0:T(8,128)(2,1)}), bf16[2,2,8,560,128]{4,3,2,1,0:T(8,128)(2,1)}, u32[]{:S(2)}, u32[]{:S(2)}) async-start(bf16[2,2,8,560,128]{4,3,2,1,0:T(8,128)(2,1)} %reshape.90), calls=%async_computation.6 | async-start | bytes 9175040 | tf_op jit(solution)/shard_map/all_to_all | solution.py:66
  295.4 5.7 %convert_reduce_fusion.1 = f32[2,8,560,128]{3,2,1,0:T(8,128)} fusion(bf16[2,2,8,560,128]{4,3,2,1,0:T(8,128)(2,1)} %all-to-all-done.1), kind=kLoop, calls=%fused_computation.1 | loop fusion | flops 3440640 | bytes 9175040 | tf_op jit(solution)/shard_map/reduce_sum | solution.py:67
  301.1 5.7 %all-to-all-start.2 = ((f32[2,8,560,128]{3,2,1,0:T(8,128)}), f32[2,8,560,128]{3,2,1,0:T(8,128)}, u32[]{:S(2)}, u32[]{:S(2)}) async-start(f32[2,8,560,128]{3,2,1,0:T(8,128)} %convert_reduce_fusion.1), calls=%async_computation.2 | async-start | bytes 9175040 | tf_op jit(solution)/shard_map/all_to_all | solution.py:68
  306.8 5.7 %convert_reduce_fusion = f32[2,8,560,128]{3,2,1,0:T(8,128)} fusion(bf16[2,2,8,560,128]{4,3,2,1,0:T(8,128)(2,1)} %all-to-all-done.6), kind=kLoop, calls=%fused_computation | loop fusion | flops 3440640 | bytes 9175040 | tf_op jit(solution)/shard_map/reduce_sum | solution.py:67
  312.5 46.1 %all-to-all-done.2 = f32[2,8,560,128]{3,2,1,0:T(8,128)} async-done(((f32[2,8,560,128]{3,2,1,0:T(8,128)}), f32[2,8,560,128]{3,2,1,0:T(8,128)}, u32[]{:S(2)}, u32[]{:S(2)}) %all-to-all-start.2) | async-done | bytes 4587552 | tf_op jit(solution)/shard_map/all_to_all | solution.py:68
  358.6 5.7 %all-to-all-start.7 = ((f32[2,8,560,128]{3,2,1,0:T(8,128)}), f32[2,8,560,128]{3,2,1,0:T(8,128)}, u32[]{:S(2)}, u32[]{:S(2)}) async-start(f32[2,8,560,128]{3,2,1,0:T(8,128)} %convert_reduce_fusion), calls=%async_computation.7 | async-start | bytes 9175040 | tf_op jit(solution)/shard_map/all_to_all | solution.py:68
  364.3 4.0 reduce_sum.99
  368.3 47.0 %all-to-all-done.7 = f32[2,8,560,128]{3,2,1,0:T(8,128)} async-done(((f32[2,8,560,128]{3,2,1,0:T(8,128)}), f32[2,8,560,128]{3,2,1,0:T(8,128)}, u32[]{:S(2)}, u32[]{:S(2)}) %all-to-all-start.7) | async-done | bytes 4587552 | tf_op jit(solution)/shard_map/all_to_all | solution.py:68
  415.3 5.5 %all-to-all-start.3 = ((bf16[8,560,128]{2,1,0:T(8,128)(2,1)}), bf16[8,560,128]{2,1,0:T(8,128)(2,1)S(1)}, u32[]{:S(2)}, u32[]{:S(2)}) async-start(bf16[8,560,128]{2,1,0:T(8,128)(2,1)} %reduce_sum.99), calls=%async_computation.3 | async-start | bytes 2293760 | tf_op jit(solution)/shard_map/all_to_all | solution.py:70
  420.8 4.0 reduce_sum.105
  424.8 26.4 %all-to-all-done.3 = bf16[8,560,128]{2,1,0:T(8,128)(2,1)S(1)} async-done(((bf16[8,560,128]{2,1,0:T(8,128)(2,1)}), bf16[8,560,128]{2,1,0:T(8,128)(2,1)S(1)}, u32[]{:S(2)}, u32[]{:S(2)}) %all-to-all-start.3) | async-done | bytes 1146912 | tf_op jit(solution)/shard_map/all_to_all | solution.py:70
  451.1 3.8 all-to-all-start.8
  454.9 5.8 %convolution_bitcast_fusion.1 = f32[1,1,3584,256]{3,2,1,0:T(8,128)} fusion(bf16[640,3584]{1,0:T(8,128)(2,1)} %reshape.89, bf16[640,256]{1,0:T(8,128)(2,1)S(1)} %copy-done.7), kind=kOutput, calls=%fused_computation.5 | convolution fusion | flops 1174405120 | bytes 8585216 | tf_op jit(solution)/shard_map/rd,rf->df/dot_general | solution.py:90
  460.7 2.1 reshape.85
  462.8 2.6 fusion.3
  465.4 3.6 collective-permute-start
  469.1 31.3 %all-to-all-done.8 = bf16[8,560,128]{2,1,0:T(8,128)(2,1)S(1)} async-done(((bf16[8,560,128]{2,1,0:T(8,128)(2,1)}), bf16[8,560,128]{2,1,0:T(8,128)(2,1)S(1)}, u32[]{:S(2)}, u32[]{:S(2)}) %all-to-all-start.8) | async-done | bytes 1146912 | tf_op jit(solution)/shard_map/all_to_all | solution.py:70
  500.4 1.3 reshape.91
  501.7 0.6 fusion.2
  502.3 22.0 %collective-permute-start.1 = (bf16[1,64,3584]{2,1,0:T(8,128)(2,1)S(1)}, bf16[1,64,3584]{2,1,0:T(8,128)(2,1)S(1)}, u32[]{:S(2)}, u32[]{:S(2)}) collective-permute-start(bf16[1,64,3584]{2,1,0:T(8,128)(2,1)S(1)} %fusion.2), channel_id=1, source_target_pairs={{0,224},{32,0},{64,32},{96,64},{128,96},{160,128},{192,160},{224,1... | collective-permute-start | bytes 1376264 | tf_op jit(solution)/shard_map/ppermute | solution.py:15
  524.3 6.1 %convolution_bitcast_fusion = f32[1,1,256,3584]{3,2,1,0:T(8,128)} fusion(bf16[640,3584]{1,0:T(8,128)(2,1)} %reshape.87, f32[640,256]{1,0:T(8,128)} %copy-done.5), kind=kOutput, calls=%fused_computation.4 | convolution fusion | flops 1175224320 | bytes 8912896 | tf_op jit(solution)/shard_map/rf,rd->fd/dot_general | solution.py:91
  530.4 8.6 %collective-permute-done.1 = bf16[1,64,3584]{2,1,0:T(8,128)(2,1)S(1)} collective-permute-done((bf16[1,64,3584]{2,1,0:T(8,128)(2,1)S(1)}, bf16[1,64,3584]{2,1,0:T(8,128)(2,1)S(1)}, u32[]{:S(2)}, u32[]{:S(2)}) %collective-permute-start.1) | collective-permute-done | bytes 458784 | tf_op jit(solution)/shard_map/ppermute | solution.py:15
  539.0 1.8 copy.43
  540.8 0.8 copy.44
  (43 shorter events, 0.6 us)
Async XLA Ops:
  7.2 217.0 %copy-start = (bf16[1,1,3584,256]{3,2,1,0:T(8,128)(2,1)S(1)}, bf16[1,1,3584,256]{3,2,1,0:T(8,128)(2,1)}, u32[]{:S(2)}) copy-start(bf16[1,1,3584,256]{3,2,1,0:T(8,128)(2,1)} %param.16) | copy-start | bytes 5505028
  12.5 10.2 %copy-start.10 = (s32[1,64,2]{1,2,0:T(2,128)S(1)}, s32[1,64,2]{1,2,0:T(2,128)}, u32[]{:S(2)}) copy-start(s32[1,64,2]{1,2,0:T(2,128)} %param.13) | copy-start | bytes 1540
  14.8 38.0 %copy-start.11 = (f32[1,64,2]{1,2,0:T(2,128)S(1)}, f32[1,64,2]{1,2,0:T(2,128)}, u32[]{:S(2)}) copy-start(f32[1,64,2]{1,2,0:T(2,128)} %param.14) | copy-start | bytes 1540
  14.8 38.7 %copy-start.8 = (bf16[1,64,3584]{2,1,0:T(8,128)(2,1)S(1)}, bf16[1,64,3584]{2,1,0:T(8,128)(2,1)}, u32[]{:S(2)}) copy-start(bf16[1,64,3584]{2,1,0:T(8,128)(2,1)} %param.12) | copy-start | bytes 1376260
  14.8 36.9 %all-to-all-start = ((bf16[8,560,128]{2,1,0:T(8,128)(2,1)}), bf16[8,560,128]{2,1,0:T(8,128)(2,1)S(1)}, u32[]{:S(2)}, u32[]{:S(2)}) async-start(bf16[8,560,128]{2,1,0:T(8,128)(2,1)} %reshape.82), calls=%async_computation | async-start | bytes 2293760 | tf_op jit(solution)/shard_map/all_to_all | solution.py:57
  22.7 105.5 %all-gather.13.cloned.1.call-start = ((), (), s32[]{:S(2)}) async-start(), calls=%async_computation.9 | async-start | bytes 3440640 | tf_op jit(solution)/shard_map/all_gather | solution.py:58
  51.7 1.0 copy-start.2
  52.7 97.9 %all-gather.21.cloned.1.call-start = ((), (), s32[]{:S(2)}) async-start(), calls=%async_computation.13 | async-start | bytes 3440640 | tf_op jit(solution)/shard_map/all_gather | solution.py:58
  56.3 34.8 %copy-start.4 = (bf16[1,64,3584]{2,1,0:T(8,128)(2,1)S(1)}, bf16[1,64,3584]{2,1,0:T(8,128)(2,1)}, u32[]{:S(2)}) copy-start(bf16[1,64,3584]{2,1,0:T(8,128)(2,1)} %param.15) | copy-start | bytes 1376260
  91.1 101.6 %all-gather.17.cloned.1.call-start = ((), (), s32[]{:S(2)}) async-start(), calls=%async_computation.11 | async-start | bytes 3440640 | tf_op jit(solution)/shard_map/all_gather | solution.py:58
  128.1 87.0 %all-gather.15.cloned.1.call-start = ((), (), s32[]{:S(2)}) async-start(), calls=%async_computation.10 | async-start | bytes 6881280 | tf_op jit(solution)/shard_map/all_gather | solution.py:59
  128.6 121.2 %all-gather.23.cloned.1.call-start = ((), (), s32[]{:S(2)}) async-start(), calls=%async_computation.14 | async-start | bytes 6881280 | tf_op jit(solution)/shard_map/all_gather | solution.py:59
  150.6 112.2 %all-gather.19.cloned.1.call-start = ((), (), s32[]{:S(2)}) async-start(), calls=%async_computation.12 | async-start | bytes 6881280 | tf_op jit(solution)/shard_map/all_gather | solution.py:59
  243.9 45.7 %all-to-all-start.1 = ((bf16[2,2,8,560,128]{4,3,2,1,0:T(8,128)(2,1)}), bf16[2,2,8,560,128]{4,3,2,1,0:T(8,128)(2,1)}, u32[]{:S(2)}, u32[]{:S(2)}) async-start(bf16[2,2,8,560,128]{4,3,2,1,0:T(8,128)(2,1)} %reshape.84), calls=%async_computation.1 | async-start | bytes 9175040 | tf_op jit(solution)/shard_map/all_to_all | solution.py:66
  262.8 9.3 %copy-start.5 = (f32[640,256]{1,0:T(8,128)}, f32[640,256]{1,0:T(8,128)S(1)}, u32[]{:S(2)}) copy-start(f32[640,256]{1,0:T(8,128)S(1)} %fusion.8) | copy-start | bytes 1966084
  276.4 3.6 copy-start.6
  289.5 11.5 %all-to-all-start.6 = ((bf16[2,2,8,560,128]{4,3,2,1,0:T(8,128)(2,1)}), bf16[2,2,8,560,128]{4,3,2,1,0:T(8,128)(2,1)}, u32[]{:S(2)}, u32[]{:S(2)}) async-start(bf16[2,2,8,560,128]{4,3,2,1,0:T(8,128)(2,1)} %reshape.90), calls=%async_computation.6 | async-start | bytes 9175040 | tf_op jit(solution)/shard_map/all_to_all | solution.py:66
  301.1 57.6 %all-to-all-start.2 = ((f32[2,8,560,128]{3,2,1,0:T(8,128)}), f32[2,8,560,128]{3,2,1,0:T(8,128)}, u32[]{:S(2)}, u32[]{:S(2)}) async-start(f32[2,8,560,128]{3,2,1,0:T(8,128)} %convert_reduce_fusion.1), calls=%async_computation.2 | async-start | bytes 9175040 | tf_op jit(solution)/shard_map/all_to_all | solution.py:68
  358.6 56.7 %all-to-all-start.7 = ((f32[2,8,560,128]{3,2,1,0:T(8,128)}), f32[2,8,560,128]{3,2,1,0:T(8,128)}, u32[]{:S(2)}, u32[]{:S(2)}) async-start(f32[2,8,560,128]{3,2,1,0:T(8,128)} %convert_reduce_fusion), calls=%async_computation.7 | async-start | bytes 9175040 | tf_op jit(solution)/shard_map/all_to_all | solution.py:68
  415.3 35.9 %all-to-all-start.3 = ((bf16[8,560,128]{2,1,0:T(8,128)(2,1)}), bf16[8,560,128]{2,1,0:T(8,128)(2,1)S(1)}, u32[]{:S(2)}, u32[]{:S(2)}) async-start(bf16[8,560,128]{2,1,0:T(8,128)(2,1)} %reduce_sum.99), calls=%async_computation.3 | async-start | bytes 2293760 | tf_op jit(solution)/shard_map/all_to_all | solution.py:70
  424.8 30.2 %copy-start.7 = (bf16[640,256]{1,0:T(8,128)(2,1)S(1)}, bf16[640,256]{1,0:T(8,128)(2,1)}, u32[]{:S(2)}) copy-start(bf16[640,256]{1,0:T(8,128)(2,1)} %copy-done.6) | copy-start | bytes 983044
  451.1 49.3 %all-to-all-start.8 = ((bf16[8,560,128]{2,1,0:T(8,128)(2,1)}), bf16[8,560,128]{2,1,0:T(8,128)(2,1)S(1)}, u32[]{:S(2)}, u32[]{:S(2)}) async-start(bf16[8,560,128]{2,1,0:T(8,128)(2,1)} %reduce_sum.105), calls=%async_computation.8 | async-start | bytes 2293760 | tf_op jit(solution)/shard_map/all_to_all | solution.py:70
  460.7 2.1 copy-start.3
  460.7 2.1 copy-start.9
  465.4 65.0 %collective-permute-start = (bf16[1,64,3584]{2,1,0:T(8,128)(2,1)}, bf16[1,64,3584]{2,1,0:T(8,128)(2,1)}, u32[]{:S(2)}, u32[]{:S(2)}) collective-permute-start(bf16[1,64,3584]{2,1,0:T(8,128)(2,1)} %fusion.3), channel_id=1, source_target_pairs={{0,32},{32,64},{64,96},{96,128},{128,160},{160,192},{192,224},{224... | collective-permute-start | bytes 1376264 | tf_op jit(solution)/shard_map/ppermute | solution.py:15
  502.3 36.7 %collective-permute-start.1 = (bf16[1,64,3584]{2,1,0:T(8,128)(2,1)S(1)}, bf16[1,64,3584]{2,1,0:T(8,128)(2,1)S(1)}, u32[]{:S(2)}, u32[]{:S(2)}) collective-permute-start(bf16[1,64,3584]{2,1,0:T(8,128)(2,1)S(1)} %fusion.2), channel_id=1, source_target_pairs={{0,224},{32,0},{64,32},{96,64},{128,96},{160,128},{192,160},{224,1... | collective-permute-start | bytes 1376264 | tf_op jit(solution)/shard_map/ppermute | solution.py:15
  524.3 17.3 %copy-start.1 = (bf16[1,1,3584,256]{3,2,1,0:T(8,128)(2,1)S(1)}, bf16[1,1,3584,256]{3,2,1,0:T(8,128)(2,1)}, u32[]{:S(2)}) copy-start(bf16[1,1,3584,256]{3,2,1,0:T(8,128)(2,1)} %param.16) | copy-start | bytes 5505028
Sparse Core Ops, SparseCore 0:
  52.8 53.3 all-gather.12
  108.0 42.5 all-gather.20
  152.4 40.2 all-gather.16
  194.3 20.6 all-gather.14
  216.7 20.8 all-gather.22
  239.3 20.8 all-gather.18

commit v3 on v2

--- a/solution.py
+++ b/solution.py
@@ -2,6 +2,9 @@
 import jax.numpy as jnp
 from jax import lax
 from jax.sharding import PartitionSpec as P
+from jax.experimental import pallas as pl
+from jax.experimental.pallas import tpu as pltpu
+import functools
 
 GROUP = 4
 
@@ -51,22 +54,115 @@
     return rows.reshape(*lead, -1, 128)
 
 
-def send_rows(rows, experts, slot_cap):
-    model_width = rows.shape[-1]
-    chunks = to_wire(rows, experts)
-    received = lax.all_to_all(chunks, "eg", split_axis=0, concat_axis=0, tiled=True)
-    across = lax.all_gather(received, "ez", axis=0)
-    gathered = lax.all_gather(across, "ec", axis=0)
-    return gathered.reshape(-1, model_width)
+def dispatch_kernel(groups, *refs):
+    sources = refs[:3]
+    out, local_sem, send1, recv1, xs_send, xs_recv, cs_send, cs_recv, fw_send, fw_recv = refs[3:]
+    mesh_kind = pl.DeviceIdType.MESH
+    pipe = lax.axis_index("pipe")
+    me = lax.axis_index("eg")
+    chip = lax.axis_index("ez")
+    core = lax.axis_index("ec")
+    across = (pipe, me, 1 - chip, core)
+    partner = (pipe, me, chip, 1 - core)
+    peers = [(pipe, lax.rem(me + step, groups), chip, core) for step in range(1, groups)]
+    barrier = pltpu.get_barrier_semaphore()
+    for peer in peers + [across, partner]:
+        pl.semaphore_signal(barrier, 1, device_id=peer, device_id_type=mesh_kind)
+    pl.semaphore_wait(barrier, len(peers) + 2)
+    first = []
+    for index, source in enumerate(sources):
+        own = pltpu.make_async_copy(source.at[me], out.at[index, core, chip, me], local_sem.at[index])
+        own.start()
+        copies = []
+        for step in range(1, groups):
+            copy = pltpu.make_async_remote_copy(
+                src_ref=source.at[peers[step - 1][1]],
+                dst_ref=out.at[index, core, chip, me],
+                send_sem=send1.at[index, step],
+                recv_sem=recv1.at[index, step],
+                device_id=peers[step - 1],
+                device_id_type=mesh_kind,
+            )
+            copy.start()
+            copies.append(copy)
+        first.append((own, copies))
+    second = []
+    for index in range(len(sources)):
+        own, copies = first[index]
+        own.wait()
+        for copy in copies:
+            copy.wait_recv()
+        block = out.at[index, core, chip]
+        far = pltpu.make_async_remote_copy(
+            src_ref=block, dst_ref=block, send_sem=xs_send.at[index], recv_sem=xs_recv.at[index],
+            device_id=across, device_id_type=mesh_kind,
+        )
+        far.start()
+        near = pltpu.make_async_remote_copy(
+            src_ref=block, dst_ref=block, send_sem=cs_send.at[index], recv_sem=cs_recv.at[index],
+            device_id=partner, device_id_type=mesh_kind,
+        )
+        near.start()
+        second.append((far, near))
+    third = []
+    for index in range(len(sources)):
+        far, near = second[index]
+        far.wait_recv()
+        relay = out.at[index, core, 1 - chip]
+        onward = pltpu.make_async_remote_copy(
+            src_ref=relay, dst_ref=relay, send_sem=fw_send.at[index], recv_sem=fw_recv.at[index],
+            device_id=partner, device_id_type=mesh_kind,
+        )
+        onward.start()
+        third.append(onward)
+    for index in range(len(sources)):
+        own, copies = first[index]
+        for copy in copies:
+            copy.wait_send()
+        far, near = second[index]
+        far.wait_send()
+        near.wait_send()
+        near.wait_recv()
+        third[index].wait_send()
+        third[index].wait_recv()
+
+
+def dispatch(wires):
+    groups = wires[0].shape[0]
+    count = len(wires)
+    tail = wires[0].shape[1:]
+    dma = pltpu.SemaphoreType.DMA
+    return pl.pallas_call(
+        functools.partial(dispatch_kernel, groups),
+        out_shape=jax.ShapeDtypeStruct((count, 2, 2, groups) + tail, wires[0].dtype),
+        in_specs=[pl.BlockSpec(memory_space=pl.ANY)] * count,
+        out_specs=pl.BlockSpec(memory_space=pl.ANY),
+        scratch_shapes=[
+            dma((count,)),
+            dma((count, groups)),
+            dma((count, groups)),
+            dma((count,)),
+            dma((count,)),
+            dma((count,)),
+            dma((count,)),
+            dma((count,)),
+            dma((count,)),
+        ],
+        compiler_params=pltpu.CompilerParams(collective_id=0, has_side_effects=True),
+    )(*wires)
+
+
+def to_wire(rows, *lead):
+    return rows.reshape(*lead, -1, 128)
 
 
 def send_back(parts, experts):
     model_width = parts.shape[-1]
     wire = to_wire(parts, 2, 2, experts)
     mine = lax.all_to_all(wire, "ec", split_axis=0, concat_axis=0, tiled=True)
-    pair = jnp.sum(mine.astype(jnp.float32), axis=0)
+    pair = jnp.sum(mine.astype(jnp.float32), axis=0).astype(jnp.bfloat16)
     other = lax.all_to_all(pair, "ez", split_axis=0, concat_axis=0, tiled=True)
-    summed = jnp.sum(other, axis=0).astype(jnp.bfloat16)
+    summed = jnp.sum(other.astype(jnp.float32), axis=0).astype(jnp.bfloat16)
     back = lax.all_to_all(summed, "eg", split_axis=0, concat_axis=0, tiled=True)
     return back.reshape(-1, model_width).astype(jnp.float32)
 
@@ -112,11 +208,11 @@
     buffer_g = lax.dot_general(
         gated_b, out_grad.astype(jnp.float32), (((0,), (0,)), ((), ())), precision=HIGH
     ).astype(jnp.bfloat16)
-    got_f = send_rows(buffer_f, experts, slot_cap)
+    model_width = fwd_input.shape[-1]
+    got = dispatch([to_wire(b, experts) for b in (buffer_f, buffer_x, buffer_g)])
+    got_f, got_x, got_g = [got[index].reshape(-1, model_width) for index in range(3)]
     part = expert_forward(got_f, up_proj, down_proj)
     summed_f = send_back(part, experts)
-    got_x = send_rows(buffer_x, experts, slot_cap)
-    got_g = send_rows(buffer_g, experts, slot_cap)
     dpart, grad_up, grad_down = expert_backward(got_x, got_g, up_proj, down_proj)
     summed_b = send_back(dpart, experts)
     merged = jnp.dot(gated_f, summed_f, precision=HIGH)

time: 553 us -> 444 us (0.80)
  waiting for transfers between devices: 273 us -> 133 us
  Pallas kernels: 0 us -> 138 us
  blocking collectives: 67.4 us -> 0 us
  starting transfers between devices: 66.2 us -> 38.8 us
  between operations: 14.4 us -> 0.85 us
  local copies, waits for them, and re-layouts: 62.3 us -> 72.9 us
    pallas_call x0 -> x1, Pallas kernels: none -> 138 us  [dispatch(): pl.pallas_call(functools.partial(dispatch_kernel, groups), out_shape=jax....]
    all_gather x6 -> x0, waiting for transfers between devices: 86.4 us -> none  [the longest x3 64 us: send_rows(): across = lax.all_gather(received, 'ez', axis=0)]
    all_to_all x2 -> x0, blocking collectives: 67.4 us -> none  [send_rows(): lax.all_to_all(chunks, 'eg', split_axis=0, concat_axis=0, tiled=True)]
    all_to_all x2, waiting for transfers between devices: 93.1 us -> 44.9 us  [send_back(): other = lax.all_to_all(pair, 'ez', split_axis=0, concat_axis=0, tiled=True)]
    reshape x3 -> x0, local copies, waits for them, and re-layouts: 27.7 us -> none  [send_rows(): return gathered.reshape(-1, model_width)]
    another operation x0 -> x3, local copies, waits for them, and re-layouts: none -> 27.1 us  [local(): got[index].reshape(-1, model_width)]
    all_to_all x1 -> x0, waiting for transfers between devices: 26.6 us -> none  [send_rows(): lax.all_to_all(chunks, 'eg', split_axis=0, concat_axis=0, tiled=True)]
    ppermute x2, starting transfers between devices: 25.6 us -> 8.18 us  [passed_along(): return lax.ppermute(value, axis, pairs)]
  transfers between devices with their start and end apart: 15 -> 8, of which waited for: 9 -> 5; matrix products, arithmetic and copies ran while one was open for 21% -> 14% of each run, Pallas kernels for 0% -> 0%
where the time goes in v3:
time: 444 us; the launch traced here: 442 us
  Pallas kernels  138 us (31%)
  waiting for transfers between devices  133 us (30%)
  local copies, waits for them, and re-layouts  72.9 us (16%)
  starting transfers between devices  38.8 us (9%)
  matrix products  38 us (9%)
  other arithmetic  20.9 us (5%)
    pallas_call x1, Pallas kernels, dispatch(): pl.pallas_call(functools.partial(dispatch_kernel, groups), out_shape=jax....  138 us
    all_to_all x2, waiting for transfers between devices, send_back(): back = lax.all_to_all(summed, 'eg', split_axis=0, concat_axis=0, tiled=True)  70.2 us
    all_to_all x2, waiting for transfers between devices, send_back(): other = lax.all_to_all(pair, 'ez', split_axis=0, concat_axis=0, tiled=True)  44.9 us
    another operation x3, local copies, waits for them, and re-layouts, local(): got[index].reshape(-1, model_width)  27.1 us
    reshape x5, local copies, waits for them, and re-layouts, to_wire(): return rows.reshape(*lead, -1, 128)  25.8 us
    ppermute x2, waiting for transfers between devices, passed_along(): return lax.ppermute(value, axis, pairs)  18.2 us
    all_to_all x2, starting transfers between devices, send_back(): mine = lax.all_to_all(wire, 'ec', split_axis=0, concat_axis=0, tiled=True)  11.8 us
    reduce_sum x2, other arithmetic, send_back(): pair = jnp.sum(mine.astype(jnp.float32), axis=0).astype(jnp.bfloat16)  10.3 us
  transfers between devices with their start and end apart: 8, of which 5 were waited for; matrix products, arithmetic and copies ran while one was open for 14% of the time, Pallas kernels for 0%

profile of v3, /device:TPU:1, one launch (start us, length us, event | category | flops | bytes accessed | tf_op | source)
XLA Modules:
  0.0 442.5 jit_solution(17617443527628224814)
XLA Ops:
  0.6 0.0 copy-start
  0.6 0.9 copy.29
  1.6 0.1 eq.58
  1.7 0.8 copy.31
  2.5 0.1 eq.65
  2.6 0.1 fusion.27
  2.7 0.2 reduce_window_sum.18
  2.9 0.2 select_reduce_fusion.2
  3.0 0.1 reduce_sum.111
  3.2 0.0 copy-start.4
  3.2 0.1 copy.32
  3.3 0.7 bitcast_add_fusion
  4.0 0.1 fusion.28
  4.1 0.2 reduce_window_sum.17
  4.3 0.2 select_reduce_fusion.3
  4.5 0.1 reduce_sum.107
  4.6 0.1 copy.30
  4.7 0.7 bitcast_add_fusion.1
  5.4 0.8 select_reduce_fusion
  6.2 2.1 convolution_convert_fusion.2
  8.3 2.3 reshape.75.refs_2_
  10.6 0.7 convert_reduce_fusion.1
  11.3 0.5 convolution_convert_fusion.4
  11.8 2.3 reshape.73.refs_0_
  14.1 1.5 convolution_convert_fusion.3
  15.6 2.3 reshape.74.refs_1_
  17.9 137.7 %shard_map.120 = bf16[3,2,2,8,560,128]{5,4,3,2,1,0:T(8,128)(2,1)} custom-call(bf16[8,560,128]{2,1,0:T(8,128)(2,1)} %reshape.73.refs_0_, bf16[8,560,128]{2,1,0:T(8,128)(2,1)} %reshape.74.refs_1_, bf16[8,560,128]{2,1,0:T(8,128)(2,1)} %reshape.75.refs_2_), custom_call_target="tpu_custom_call" | custom-call | tf_op jit(solution)/shard_map/pallas_call | solution.py:135
  155.6 10.0 %fusion.33 = (bf16[1,2,2,8,560,128]{5,4,3,2,1,0:T(8,128)(2,1)}, bf16[1,2,2,8,560,128]{5,4,3,2,1,0:T(8,128)(2,1)}, bf16[1,2,2,8,560,128]{5,4,3,2,1,0:T(8,128)(2,1)}) fusion(bf16[3,2,2,8,560,128]{5,4,3,2,1,0:T(8,128)(2,1)} %shard_map.120), kind=kLoop, calls=%fused_computation.49 | loop fusion | bytes 27525120 | tf_op jit(solution)/shard_map/slice | solution.py:213
  165.6 9.1 %reshape_squeeze.13 = bf16[640,3584]{1,0:T(8,128)(2,1)} reshape(bf16[1,2,2,8,560,128]{5,4,3,2,1,0:T(8,128)(2,1)} %get-tuple-element.8) | data formatting | bytes 9175040 | tf_op jit(solution)/shard_map/reshape;squeeze | solution.py:213
  174.6 9.0 %reshape_squeeze.12 = bf16[640,3584]{1,0:T(8,128)(2,1)} reshape(bf16[1,2,2,8,560,128]{5,4,3,2,1,0:T(8,128)(2,1)} %get-tuple-element.9) | data formatting | bytes 9175040 | tf_op jit(solution)/shard_map/reshape;squeeze | solution.py:213
  183.7 3.8 fusion.8
  187.5 0.8 copy-done.5
  188.3 1.4 fusion.15
  189.7 0.7 copy-done.6
  190.5 3.6 convolution_convert_fusion
  194.0 9.5 %reshape.78 = bf16[2,2,8,560,128]{4,3,2,1,0:T(8,128)(2,1)} reshape(bf16[640,3584]{1,0:T(8,128)(2,1)} %convolution_convert_fusion) | data formatting | bytes 9175040 | tf_op jit(solution)/shard_map/reshape | solution.py:156
  203.5 6.0 %all-to-all-start.3 = ((bf16[2,2,8,560,128]{4,3,2,1,0:T(8,128)(2,1)}), bf16[2,2,8,560,128]{4,3,2,1,0:T(8,128)(2,1)}, u32[]{:S(2)}, u32[]{:S(2)}) async-start(bf16[2,2,8,560,128]{4,3,2,1,0:T(8,128)(2,1)} %reshape.78), calls=%async_computation.3 | async-start | bytes 9175040 | tf_op jit(solution)/shard_map/all_to_all | solution.py:162
  209.5 9.0 %reshape_squeeze.11 = bf16[640,3584]{1,0:T(8,128)(2,1)} reshape(bf16[1,2,2,8,560,128]{5,4,3,2,1,0:T(8,128)(2,1)} %get-tuple-element.10) | data formatting | bytes 9175040 | tf_op jit(solution)/shard_map/reshape;squeeze | solution.py:213
  218.5 9.9 %convolution_convert_fusion.1 = bf16[640,3584]{1,0:T(8,128)(2,1)} fusion(bf16[1,1,256,3584]{3,2,1,0:T(8,128)(2,1)} %param.17, bf16[640,3584]{1,0:T(8,128)(2,1)} %reshape_squeeze.11, bf16[1,1,3584,256]{3,2,1,0:T(8,128)(2,1)S(1)} %copy-done), kind=kOutput, calls=%fused_computation.1 | convolution fusion | flops 2351923200 | bytes 12845056 | tf_op jit(solution)/shard_map/...f,fd->...d/dot_general | solution.py:173
  228.5 9.5 %reshape.76 = bf16[2,2,8,560,128]{4,3,2,1,0:T(8,128)(2,1)} reshape(bf16[640,3584]{1,0:T(8,128)(2,1)} %convolution_convert_fusion.1) | data formatting | bytes 9175040 | tf_op jit(solution)/shard_map/reshape | solution.py:156
  238.0 5.8 %all-to-all-start = ((bf16[2,2,8,560,128]{4,3,2,1,0:T(8,128)(2,1)}), bf16[2,2,8,560,128]{4,3,2,1,0:T(8,128)(2,1)}, u32[]{:S(2)}, u32[]{:S(2)}) async-start(bf16[2,2,8,560,128]{4,3,2,1,0:T(8,128)(2,1)} %reshape.76), calls=%async_computation | async-start | bytes 9175040 | tf_op jit(solution)/shard_map/all_to_all | solution.py:162
  243.7 5.2 %reduce_sum.116 = bf16[2,8,560,128]{3,2,1,0:T(8,128)(2,1)} reduce(bf16[2,2,8,560,128]{4,3,2,1,0:T(8,128)(2,1)} %all-to-all-done.3, bf16[]{:T(256)} %constant.23.clone.1), dimensions={0}, to_apply=%region_10.11 | reduce | flops 1146880 | bytes 6881282 | tf_op jit(solution)/shard_map/reduce_sum | solution.py:163
  248.9 4.9 %all-to-all-start.4 = ((bf16[2,8,560,128]{3,2,1,0:T(8,128)(2,1)}), bf16[2,8,560,128]{3,2,1,0:T(8,128)(2,1)}, u32[]{:S(2)}, u32[]{:S(2)}) async-start(bf16[2,8,560,128]{3,2,1,0:T(8,128)(2,1)} %reduce_sum.116), calls=%async_computation.4 | async-start | bytes 4587520 | tf_op jit(solution)/shard_map/all_to_all | solution.py:164
  253.8 5.2 %reduce_sum.114 = bf16[2,8,560,128]{3,2,1,0:T(8,128)(2,1)} reduce(bf16[2,2,8,560,128]{4,3,2,1,0:T(8,128)(2,1)} %all-to-all-done, bf16[]{:T(256)} %constant.23.clone.1), dimensions={0}, to_apply=%region_8.9 | reduce | flops 1146880 | bytes 6881282 | tf_op jit(solution)/shard_map/reduce_sum | solution.py:163
  259.0 22.0 %all-to-all-done.4 = bf16[2,8,560,128]{3,2,1,0:T(8,128)(2,1)} async-done(((bf16[2,8,560,128]{3,2,1,0:T(8,128)(2,1)}), bf16[2,8,560,128]{3,2,1,0:T(8,128)(2,1)}, u32[]{:S(2)}, u32[]{:S(2)}) %all-to-all-start.4) | async-done | bytes 2293792 | tf_op jit(solution)/shard_map/all_to_all | solution.py:164
  281.0 4.9 %all-to-all-start.1 = ((bf16[2,8,560,128]{3,2,1,0:T(8,128)(2,1)}), bf16[2,8,560,128]{3,2,1,0:T(8,128)(2,1)}, u32[]{:S(2)}, u32[]{:S(2)}) async-start(bf16[2,8,560,128]{3,2,1,0:T(8,128)(2,1)} %reduce_sum.114), calls=%async_computation.1 | async-start | bytes 4587520 | tf_op jit(solution)/shard_map/all_to_all | solution.py:164
  285.9 3.4 reduce_sum.117
  289.2 22.9 %all-to-all-done.1 = bf16[2,8,560,128]{3,2,1,0:T(8,128)(2,1)} async-done(((bf16[2,8,560,128]{3,2,1,0:T(8,128)(2,1)}), bf16[2,8,560,128]{3,2,1,0:T(8,128)(2,1)}, u32[]{:S(2)}, u32[]{:S(2)}) %all-to-all-start.1) | async-done | bytes 2293792 | tf_op jit(solution)/shard_map/all_to_all | solution.py:164
  312.1 5.3 %all-to-all-start.5 = ((bf16[8,560,128]{2,1,0:T(8,128)(2,1)}), bf16[8,560,128]{2,1,0:T(8,128)(2,1)S(1)}, u32[]{:S(2)}, u32[]{:S(2)}) async-start(bf16[8,560,128]{2,1,0:T(8,128)(2,1)} %reduce_sum.117), calls=%async_computation.5 | async-start | bytes 2293760 | tf_op jit(solution)/shard_map/all_to_all | solution.py:166
  317.5 3.4 reduce_sum.115
  320.8 27.0 %all-to-all-done.5 = bf16[8,560,128]{2,1,0:T(8,128)(2,1)S(1)} async-done(((bf16[8,560,128]{2,1,0:T(8,128)(2,1)}), bf16[8,560,128]{2,1,0:T(8,128)(2,1)S(1)}, u32[]{:S(2)}, u32[]{:S(2)}) %all-to-all-start.5) | async-done | bytes 1146912 | tf_op jit(solution)/shard_map/all_to_all | solution.py:166
  347.8 3.8 all-to-all-start.2
  351.6 5.8 %convolution_bitcast_fusion.1 = f32[1,1,3584,256]{3,2,1,0:T(8,128)} fusion(bf16[640,3584]{1,0:T(8,128)(2,1)} %reshape_squeeze.13, bf16[640,256]{1,0:T(8,128)(2,1)S(1)} %copy-done.7), kind=kOutput, calls=%fused_computation.3 | convolution fusion | flops 1174405120 | bytes 8585216 | tf_op jit(solution)/shard_map/rd,rf->df/dot_general | solution.py:186
  357.4 2.1 reshape.79
  359.5 2.7 fusion.2
  362.2 6.4 %collective-permute-start.1 = (bf16[1,64,3584]{2,1,0:T(8,128)(2,1)}, bf16[1,64,3584]{2,1,0:T(8,128)(2,1)}, u32[]{:S(2)}, u32[]{:S(2)}) collective-permute-start(bf16[1,64,3584]{2,1,0:T(8,128)(2,1)} %fusion.2), channel_id=1, source_target_pairs={{0,224},{32,0},{64,32},{96,64},{128,96},{160,128},{192,160},{224,1... | collective-permute-start | bytes 1376264 | tf_op jit(solution)/shard_map/ppermute | solution.py:18
  368.5 43.2 %all-to-all-done.2 = bf16[8,560,128]{2,1,0:T(8,128)(2,1)S(1)} async-done(((bf16[8,560,128]{2,1,0:T(8,128)(2,1)}), bf16[8,560,128]{2,1,0:T(8,128)(2,1)S(1)}, u32[]{:S(2)}, u32[]{:S(2)}) %all-to-all-start.2) | async-done | bytes 1146912 | tf_op jit(solution)/shard_map/all_to_all | solution.py:166
  411.8 1.3 reshape.77
  413.1 0.6 fusion.3
  413.7 1.8 collective-permute-start
  415.5 6.1 %convolution_bitcast_fusion = f32[1,1,256,3584]{3,2,1,0:T(8,128)} fusion(bf16[640,3584]{1,0:T(8,128)(2,1)} %reshape_squeeze.12, f32[640,256]{1,0:T(8,128)} %copy-done.5), kind=kOutput, calls=%fused_computation.2 | convolution fusion | flops 1175224320 | bytes 8912896 | tf_op jit(solution)/shard_map/rf,rd->fd/dot_general | solution.py:187
  421.6 18.2 %collective-permute-done = bf16[1,64,3584]{2,1,0:T(8,128)(2,1)S(1)} collective-permute-done((bf16[1,64,3584]{2,1,0:T(8,128)(2,1)S(1)}, bf16[1,64,3584]{2,1,0:T(8,128)(2,1)S(1)}, u32[]{:S(2)}, u32[]{:S(2)}) %collective-permute-start) | collective-permute-done | bytes 458784 | tf_op jit(solution)/shard_map/ppermute | solution.py:18
  439.9 0.8 copy.35
  440.6 1.8 copy.36
  (21 shorter events, 0.0 us)
Async XLA Ops:
  0.6 183.0 %copy-start = (bf16[1,1,3584,256]{3,2,1,0:T(8,128)(2,1)S(1)}, bf16[1,1,3584,256]{3,2,1,0:T(8,128)(2,1)}, u32[]{:S(2)}) copy-start(bf16[1,1,3584,256]{3,2,1,0:T(8,128)(2,1)} %param.16) | copy-start | bytes 5505028
  2.9 7.7 %copy-start.9 = (f32[1,64,2]{1,2,0:T(2,128)S(1)}, f32[1,64,2]{1,2,0:T(2,128)}, u32[]{:S(2)}) copy-start(f32[1,64,2]{1,2,0:T(2,128)} %param.11) | copy-start | bytes 1540
  3.2 8.1 %copy-start.4 = (bf16[1,64,3584]{2,1,0:T(8,128)(2,1)S(1)}, bf16[1,64,3584]{2,1,0:T(8,128)(2,1)}, u32[]{:S(2)}) copy-start(bf16[1,64,3584]{2,1,0:T(8,128)(2,1)} %param.9) | copy-start | bytes 1376260
  183.7 4.7 %copy-start.2 = (bf16[640,3584]{1,0:T(8,128)(2,1)S(1)}, bf16[640,3584]{1,0:T(8,128)(2,1)}, u32[]{:S(2)}) copy-start(bf16[640,3584]{1,0:T(8,128)(2,1)} %reshape_squeeze.12) | copy-start | bytes 13762564
  183.7 4.7 %copy-start.10 = (bf16[1,1,256,3584]{3,2,1,0:T(8,128)(2,1)S(1)}, bf16[1,1,256,3584]{3,2,1,0:T(8,128)(2,1)}, u32[]{:S(2)}) copy-start(bf16[1,1,256,3584]{3,2,1,0:T(8,128)(2,1)} %param.17) | copy-start | bytes 5505028
  187.5 0.9 copy-start.5
  189.7 0.7 copy-start.6
  203.5 34.5 %all-to-all-start.3 = ((bf16[2,2,8,560,128]{4,3,2,1,0:T(8,128)(2,1)}), bf16[2,2,8,560,128]{4,3,2,1,0:T(8,128)(2,1)}, u32[]{:S(2)}, u32[]{:S(2)}) async-start(bf16[2,2,8,560,128]{4,3,2,1,0:T(8,128)(2,1)} %reshape.78), calls=%async_computation.3 | async-start | bytes 9175040 | tf_op jit(solution)/shard_map/all_to_all | solution.py:162
  238.0 10.9 %all-to-all-start = ((bf16[2,2,8,560,128]{4,3,2,1,0:T(8,128)(2,1)}), bf16[2,2,8,560,128]{4,3,2,1,0:T(8,128)(2,1)}, u32[]{:S(2)}, u32[]{:S(2)}) async-start(bf16[2,2,8,560,128]{4,3,2,1,0:T(8,128)(2,1)} %reshape.76), calls=%async_computation | async-start | bytes 9175040 | tf_op jit(solution)/shard_map/all_to_all | solution.py:162
  248.9 32.1 %all-to-all-start.4 = ((bf16[2,8,560,128]{3,2,1,0:T(8,128)(2,1)}), bf16[2,8,560,128]{3,2,1,0:T(8,128)(2,1)}, u32[]{:S(2)}, u32[]{:S(2)}) async-start(bf16[2,8,560,128]{3,2,1,0:T(8,128)(2,1)} %reduce_sum.116), calls=%async_computation.4 | async-start | bytes 4587520 | tf_op jit(solution)/shard_map/all_to_all | solution.py:164
  281.0 31.2 %all-to-all-start.1 = ((bf16[2,8,560,128]{3,2,1,0:T(8,128)(2,1)}), bf16[2,8,560,128]{3,2,1,0:T(8,128)(2,1)}, u32[]{:S(2)}, u32[]{:S(2)}) async-start(bf16[2,8,560,128]{3,2,1,0:T(8,128)(2,1)} %reduce_sum.114), calls=%async_computation.1 | async-start | bytes 4587520 | tf_op jit(solution)/shard_map/all_to_all | solution.py:164
  312.1 35.7 %all-to-all-start.5 = ((bf16[8,560,128]{2,1,0:T(8,128)(2,1)}), bf16[8,560,128]{2,1,0:T(8,128)(2,1)S(1)}, u32[]{:S(2)}, u32[]{:S(2)}) async-start(bf16[8,560,128]{2,1,0:T(8,128)(2,1)} %reduce_sum.117), calls=%async_computation.5 | async-start | bytes 2293760 | tf_op jit(solution)/shard_map/all_to_all | solution.py:166
  317.5 34.1 %copy-start.7 = (bf16[640,256]{1,0:T(8,128)(2,1)S(1)}, bf16[640,256]{1,0:T(8,128)(2,1)}, u32[]{:S(2)}) copy-start(bf16[640,256]{1,0:T(8,128)(2,1)} %copy-done.6) | copy-start | bytes 983044
  347.8 64.0 %all-to-all-start.2 = ((bf16[8,560,128]{2,1,0:T(8,128)(2,1)}), bf16[8,560,128]{2,1,0:T(8,128)(2,1)S(1)}, u32[]{:S(2)}, u32[]{:S(2)}) async-start(bf16[8,560,128]{2,1,0:T(8,128)(2,1)} %reduce_sum.115), calls=%async_computation.2 | async-start | bytes 2293760 | tf_op jit(solution)/shard_map/all_to_all | solution.py:166
  357.4 2.1 copy-start.3
  359.5 53.6 %copy-start.8 = (f32[64,160]{1,0:T(8,128)S(1)}, f32[64,160]{1,0:T(8,128)}, u32[]{:S(2)}) copy-start(f32[64,160]{1,0:T(8,128)} %get-tuple-element.7) | copy-start | bytes 122884
  362.2 59.5 %collective-permute-start.1 = (bf16[1,64,3584]{2,1,0:T(8,128)(2,1)}, bf16[1,64,3584]{2,1,0:T(8,128)(2,1)}, u32[]{:S(2)}, u32[]{:S(2)}) collective-permute-start(bf16[1,64,3584]{2,1,0:T(8,128)(2,1)} %fusion.2), channel_id=1, source_target_pairs={{0,224},{32,0},{64,32},{96,64},{128,96},{160,128},{192,160},{224,1... | collective-permute-start | bytes 1376264 | tf_op jit(solution)/shard_map/ppermute | solution.py:18
  413.7 26.2 %collective-permute-start = (bf16[1,64,3584]{2,1,0:T(8,128)(2,1)S(1)}, bf16[1,64,3584]{2,1,0:T(8,128)(2,1)S(1)}, u32[]{:S(2)}, u32[]{:S(2)}) collective-permute-start(bf16[1,64,3584]{2,1,0:T(8,128)(2,1)S(1)} %fusion.3), channel_id=1, source_target_pairs={{0,32},{32,64},{64,96},{96,128},{128,160},{160,192},{192,224},{224... | collective-permute-start | bytes 1376264 | tf_op jit(solution)/shard_map/ppermute | solution.py:18
  415.5 26.9 %copy-start.1 = (bf16[1,1,3584,256]{3,2,1,0:T(8,128)(2,1)S(1)}, bf16[1,1,3584,256]{3,2,1,0:T(8,128)(2,1)}, u32[]{:S(2)}) copy-start(bf16[1,1,3584,256]{3,2,1,0:T(8,128)(2,1)} %param.16) | copy-start | bytes 5505028

commit v4 on v3

--- a/solution.py
+++ b/solution.py
@@ -156,15 +156,66 @@
     return rows.reshape(*lead, -1, 128)
 
 
-def send_back(parts, experts):
+def return_kernel(groups, *refs):
+    count = len(refs) - 4
+    sources = refs[:count]
+    out, local_sem, send1, recv1 = refs[count:]
+    mesh_kind = pl.DeviceIdType.MESH
+    pipe = lax.axis_index("pipe")
+    me = lax.axis_index("eg")
+    chip = lax.axis_index("ez")
+    core = lax.axis_index("ec")
+    peers = [(pipe, lax.rem(me + step, groups), chip, core) for step in range(1, groups)]
+    barrier = pltpu.get_barrier_semaphore()
+    for peer in peers:
+        pl.semaphore_signal(barrier, 1, device_id=peer, device_id_type=mesh_kind)
+    pl.semaphore_wait(barrier, len(peers))
+    started = []
+    for index, source in enumerate(sources):
+        own = pltpu.make_async_copy(source.at[me], out.at[index, me], local_sem.at[index])
+        own.start()
+        copies = []
+        for step in range(1, groups):
+            copy = pltpu.make_async_remote_copy(
+                src_ref=source.at[peers[step - 1][1]],
+                dst_ref=out.at[index, me],
+                send_sem=send1.at[index, step],
+                recv_sem=recv1.at[index, step],
+                device_id=peers[step - 1],
+                device_id_type=mesh_kind,
+            )
+            copy.start()
+            copies.append(copy)
+        started.append((own, copies))
+    for own, copies in started:
+        own.wait()
+        for copy in copies:
+            copy.wait_send()
+            copy.wait_recv()
+
+
+def send_home(wires):
+    groups = wires[0].shape[0]
+    count = len(wires)
+    dma = pltpu.SemaphoreType.DMA
+    return pl.pallas_call(
+        functools.partial(return_kernel, groups),
+        out_shape=jax.ShapeDtypeStruct((count,) + wires[0].shape, wires[0].dtype),
+        in_specs=[pl.BlockSpec(memory_space=pl.ANY)] * count,
+        out_specs=pl.BlockSpec(memory_space=pl.ANY),
+        scratch_shapes=[dma((count,)), dma((count, groups)), dma((count, groups))],
+        compiler_params=pltpu.CompilerParams(collective_id=1, has_side_effects=True),
+    )(*wires)
+
+
+def group_sum(parts, experts):
     model_width = parts.shape[-1]
-    wire = to_wire(parts, 2, 2, experts)
-    mine = lax.all_to_all(wire, "ec", split_axis=0, concat_axis=0, tiled=True)
+    blocks = parts.reshape(2, 2, -1, model_width)
+    mine = lax.all_to_all(blocks, "ec", split_axis=0, concat_axis=0, tiled=True)
     pair = jnp.sum(mine.astype(jnp.float32), axis=0).astype(jnp.bfloat16)
     other = lax.all_to_all(pair, "ez", split_axis=0, concat_axis=0, tiled=True)
     summed = jnp.sum(other.astype(jnp.float32), axis=0).astype(jnp.bfloat16)
-    back = lax.all_to_all(summed, "eg", split_axis=0, concat_axis=0, tiled=True)
-    return back.reshape(-1, model_width).astype(jnp.float32)
+    return to_wire(summed, experts)
 
 
 def expert_forward(rows, up_proj, down_proj):
@@ -212,9 +263,12 @@
     got = dispatch([to_wire(b, experts) for b in (buffer_f, buffer_x, buffer_g)])
     got_f, got_x, got_g = [got[index].reshape(-1, model_width) for index in range(3)]
     part = expert_forward(got_f, up_proj, down_proj)
-    summed_f = send_back(part, experts)
+    wire_f = group_sum(part, experts)
     dpart, grad_up, grad_down = expert_backward(got_x, got_g, up_proj, down_proj)
-    summed_b = send_back(dpart, experts)
+    wire_b = group_sum(dpart, experts)
+    home = send_home([wire_f, wire_b])
+    summed_f = home[0].reshape(-1, model_width).astype(jnp.float32)
+    summed_b = home[1].reshape(-1, model_width).astype(jnp.float32)
     merged = jnp.dot(gated_f, summed_f, precision=HIGH)
     section_out = (fwd_input.astype(jnp.float32) + merged).astype(jnp.bfloat16)
     spread_back = jnp.dot(plain_b, summed_b, precision=HIGH)

time: 444 us -> 410 us (0.923)
  waiting for transfers between devices: 133 us -> 70.8 us
  Pallas kernels: 138 us -> 193 us
  local copies, waits for them, and re-layouts: 72.9 us -> 59.5 us
  starting transfers between devices: 38.8 us -> 28.1 us
    all_to_all x6 -> x4, waiting for transfers between devices: 115 us -> 37.9 us  [the longest x2 37.9 us: group_sum(): other = lax.all_to_all(pair, 'ez', split_axis=0, concat_axis=0, tiled=True)]
    pallas_call x0 -> x1, Pallas kernels: none -> 55.6 us  [send_home(): pl.pallas_call(functools.partial(return_kernel, groups), out_shape=jax.Sh...]
    ppermute x2, waiting for transfers between devices: 18.2 us -> 32.8 us  [passed_along(): return lax.ppermute(value, axis, pairs)]
    reshape x5, local copies, waits for them, and re-layouts: 25.8 us -> 11.4 us  [to_wire(): return rows.reshape(*lead, -1, 128)]
    all_to_all x6 -> x4, starting transfers between devices: 30.6 us -> 21.7 us  [the longest x2 11.8 us: group_sum(): mine = lax.all_to_all(blocks, 'ec', split_axis=0, concat_axis=0, tiled=True)]
  transfers between devices with their start and end apart: 8 -> 6, of which waited for: 5 -> 4; matrix products, arithmetic and copies ran while one was open for 14% -> 12% of each run, Pallas kernels for 0% -> 0%
where the time goes in v4:
time: 410 us; the launch traced here: 409 us
  Pallas kernels  193 us (47%)
  waiting for transfers between devices  70.8 us (17%)
  local copies, waits for them, and re-layouts  59.5 us (15%)
  matrix products  37.8 us (9%)
  starting transfers between devices  28.1 us (7%)
  other arithmetic  18.3 us (4%)
    pallas_call x1, Pallas kernels, dispatch(): pl.pallas_call(functools.partial(dispatch_kernel, groups), out_shape=jax....  138 us
    pallas_call x1, Pallas kernels, send_home(): pl.pallas_call(functools.partial(return_kernel, groups), out_shape=jax.Sh...  55.6 us
    all_to_all x2, waiting for transfers between devices, group_sum(): other = lax.all_to_all(pair, 'ez', split_axis=0, concat_axis=0, tiled=True)  37.9 us
    ppermute x2, waiting for transfers between devices, passed_along(): return lax.ppermute(value, axis, pairs)  32.8 us
    another operation x3, local copies, waits for them, and re-layouts, local(): got[index].reshape(-1, model_width)  27.1 us
    all_to_all x2, starting transfers between devices, group_sum(): mine = lax.all_to_all(blocks, 'ec', split_axis=0, concat_axis=0, tiled=True)  11.8 us
    reshape x5, local copies, waits for them, and re-layouts, to_wire(): return rows.reshape(*lead, -1, 128)  11.4 us
    reduce_sum x2, other arithmetic, group_sum(): pair = jnp.sum(mine.astype(jnp.float32), axis=0).astype(jnp.bfloat16)  10.2 us
  transfers between devices with their start and end apart: 6, of which 4 were waited for; matrix products, arithmetic and copies ran while one was open for 12% of the time, Pallas kernels for 0%

profile of v4, /device:TPU:1, one launch (start us, length us, event | category | flops | bytes accessed | tf_op | source)
XLA Modules:
  0.0 408.6 jit_solution(17381091814491796352)
XLA Ops:
  0.6 0.0 copy-start
  0.6 0.9 copy.29
  1.6 0.1 eq.58
  1.7 0.8 copy.31
  2.5 0.1 eq.65
  2.6 0.1 fusion.27
  2.7 0.2 reduce_window_sum.18
  2.9 0.2 select_reduce_fusion.2
  3.0 0.1 reduce_sum.111
  3.2 0.0 copy-start.4
  3.2 0.1 copy.32
  3.3 0.7 bitcast_add_fusion
  4.0 0.1 fusion.28
  4.1 0.2 reduce_window_sum.17
  4.3 0.2 select_reduce_fusion.3
  4.5 0.1 reduce_sum.107
  4.6 0.1 copy.30
  4.7 0.7 bitcast_add_fusion.1
  5.4 0.8 select_reduce_fusion
  6.2 2.1 convolution_convert_fusion.2
  8.3 2.3 reshape.75.refs_2_
  10.6 0.7 convert_reduce_fusion.1
  11.3 0.5 convolution_convert_fusion.4
  11.8 2.3 reshape.73.refs_0_
  14.1 1.5 convolution_convert_fusion.3
  15.6 2.3 reshape.74.refs_1_
  17.9 137.7 %shard_map.120 = bf16[3,2,2,8,560,128]{5,4,3,2,1,0:T(8,128)(2,1)} custom-call(bf16[8,560,128]{2,1,0:T(8,128)(2,1)} %reshape.73.refs_0_, bf16[8,560,128]{2,1,0:T(8,128)(2,1)} %reshape.74.refs_1_, bf16[8,560,128]{2,1,0:T(8,128)(2,1)} %reshape.75.refs_2_), custom_call_target="tpu_custom_call" | custom-call | tf_op jit(solution)/shard_map/pallas_call | solution.py:135
  155.6 10.0 %fusion.33 = (bf16[1,2,2,8,560,128]{5,4,3,2,1,0:T(8,128)(2,1)}, bf16[1,2,2,8,560,128]{5,4,3,2,1,0:T(8,128)(2,1)}, bf16[1,2,2,8,560,128]{5,4,3,2,1,0:T(8,128)(2,1)}) fusion(bf16[3,2,2,8,560,128]{5,4,3,2,1,0:T(8,128)(2,1)} %shard_map.120), kind=kLoop, calls=%fused_computation.49 | loop fusion | bytes 27525120 | tf_op jit(solution)/shard_map/slice | solution.py:264
  165.6 9.1 %reshape_squeeze.19 = bf16[640,3584]{1,0:T(8,128)(2,1)} reshape(bf16[1,2,2,8,560,128]{5,4,3,2,1,0:T(8,128)(2,1)} %get-tuple-element.8) | data formatting | bytes 9175040 | tf_op jit(solution)/shard_map/reshape;squeeze | solution.py:264
  174.6 9.0 %reshape_squeeze.18 = bf16[640,3584]{1,0:T(8,128)(2,1)} reshape(bf16[1,2,2,8,560,128]{5,4,3,2,1,0:T(8,128)(2,1)} %get-tuple-element.9) | data formatting | bytes 9175040 | tf_op jit(solution)/shard_map/reshape;squeeze | solution.py:264
  183.7 3.8 fusion.8
  187.5 0.8 copy-done.5
  188.3 1.4 fusion.15
  189.7 3.5 convolution_convert_fusion
  193.2 6.0 %all-to-all-start.2 = ((bf16[2,2,160,3584]{3,2,1,0:T(8,128)(2,1)}), bf16[2,2,160,3584]{3,2,1,0:T(8,128)(2,1)}, u32[]{:S(2)}, u32[]{:S(2)}) async-start(bf16[2,2,160,3584]{3,2,1,0:T(8,128)(2,1)} %bitcast.70), calls=%async_computation.2 | async-start | bytes 9175040 | tf_op jit(solution)/shard_map/all_to_all | solution.py:214
  199.2 9.0 %reshape_squeeze.17 = bf16[640,3584]{1,0:T(8,128)(2,1)} reshape(bf16[1,2,2,8,560,128]{5,4,3,2,1,0:T(8,128)(2,1)} %get-tuple-element.10) | data formatting | bytes 9175040 | tf_op jit(solution)/shard_map/reshape;squeeze | solution.py:264
  208.3 9.8 %convolution_convert_fusion.1 = bf16[640,3584]{1,0:T(8,128)(2,1)} fusion(bf16[1,1,256,3584]{3,2,1,0:T(8,128)(2,1)} %param.17, bf16[640,3584]{1,0:T(8,128)(2,1)} %reshape_squeeze.17, bf16[1,1,3584,256]{3,2,1,0:T(8,128)(2,1)S(1)} %copy-done), kind=kOutput, calls=%fused_computation.1 | convolution fusion | flops 2351923200 | bytes 12845056 | tf_op jit(solution)/shard_map/...f,fd->...d/dot_general | solution.py:224
  218.1 5.8 %all-to-all-start = ((bf16[2,2,160,3584]{3,2,1,0:T(8,128)(2,1)}), bf16[2,2,160,3584]{3,2,1,0:T(8,128)(2,1)}, u32[]{:S(2)}, u32[]{:S(2)}) async-start(bf16[2,2,160,3584]{3,2,1,0:T(8,128)(2,1)} %bitcast.71), calls=%async_computation | async-start | bytes 9175040 | tf_op jit(solution)/shard_map/all_to_all | solution.py:214
  223.9 5.1 %reduce_sum.116 = bf16[2,160,3584]{2,1,0:T(8,128)(2,1)} reduce(bf16[2,2,160,3584]{3,2,1,0:T(8,128)(2,1)} %all-to-all-done.2, bf16[]{:T(256)} %constant.23.clone.1), dimensions={0}, to_apply=%region_10.11 | reduce | flops 1146880 | bytes 6881282 | tf_op jit(solution)/shard_map/reduce_sum | solution.py:215
  229.0 4.9 %all-to-all-start.3 = ((bf16[2,160,3584]{2,1,0:T(8,128)(2,1)}), bf16[2,160,3584]{2,1,0:T(8,128)(2,1)}, u32[]{:S(2)}, u32[]{:S(2)}) async-start(bf16[2,160,3584]{2,1,0:T(8,128)(2,1)} %reduce_sum.116), calls=%async_computation.3 | async-start | bytes 4587520 | tf_op jit(solution)/shard_map/all_to_all | solution.py:216
  233.9 5.1 %reduce_sum.114 = bf16[2,160,3584]{2,1,0:T(8,128)(2,1)} reduce(bf16[2,2,160,3584]{3,2,1,0:T(8,128)(2,1)} %all-to-all-done, bf16[]{:T(256)} %constant.23.clone.1), dimensions={0}, to_apply=%region_8.9 | reduce | flops 1146880 | bytes 6881282 | tf_op jit(solution)/shard_map/reduce_sum | solution.py:215
  239.0 22.1 %all-to-all-done.3 = bf16[2,160,3584]{2,1,0:T(8,128)(2,1)} async-done(((bf16[2,160,3584]{2,1,0:T(8,128)(2,1)}), bf16[2,160,3584]{2,1,0:T(8,128)(2,1)}, u32[]{:S(2)}, u32[]{:S(2)}) %all-to-all-start.3) | async-done | bytes 2293792 | tf_op jit(solution)/shard_map/all_to_all | solution.py:216
  261.0 5.1 %all-to-all-start.1 = ((bf16[2,160,3584]{2,1,0:T(8,128)(2,1)}), bf16[2,160,3584]{2,1,0:T(8,128)(2,1)}, u32[]{:S(2)}, u32[]{:S(2)}) async-start(bf16[2,160,3584]{2,1,0:T(8,128)(2,1)} %reduce_sum.114), calls=%async_computation.1 | async-start | bytes 4587520 | tf_op jit(solution)/shard_map/all_to_all | solution.py:216
  266.1 5.8 %convolution_bitcast_fusion.1 = f32[1,1,3584,256]{3,2,1,0:T(8,128)} fusion(bf16[640,3584]{1,0:T(8,128)(2,1)} %reshape_squeeze.19, bf16[640,256]{1,0:T(8,128)(2,1)S(1)} %fusion.15), kind=kOutput, calls=%fused_computation.3 | convolution fusion | flops 1174405120 | bytes 8585216 | tf_op jit(solution)/shard_map/rd,rf->df/dot_general | solution.py:237
  271.9 2.1 reduce_sum.117
  274.1 2.3 reshape.79.refs_1_
  276.3 15.9 %all-to-all-done.1 = bf16[2,160,3584]{2,1,0:T(8,128)(2,1)} async-done(((bf16[2,160,3584]{2,1,0:T(8,128)(2,1)}), bf16[2,160,3584]{2,1,0:T(8,128)(2,1)}, u32[]{:S(2)}, u32[]{:S(2)}) %all-to-all-start.1) | async-done | bytes 2293792 | tf_op jit(solution)/shard_map/all_to_all | solution.py:216
  292.2 2.1 reduce_sum.115
  294.3 2.3 reshape.77.refs_0_
  296.6 55.6 %shard_map.121 = bf16[2,8,560,128]{3,2,1,0:T(8,128)(2,1)} custom-call(bf16[8,560,128]{2,1,0:T(8,128)(2,1)} %reshape.77.refs_0_, bf16[8,560,128]{2,1,0:T(8,128)(2,1)} %reshape.79.refs_1_), custom_call_target="tpu_custom_call" | custom-call | tf_op jit(solution)/shard_map/pallas_call | solution.py:201
  352.2 1.8 fusion.34
  354.0 0.0 copy-start.3
  354.0 2.1 reshape_squeeze.21
  356.1 2.7 fusion.2
  358.8 6.2 %collective-permute-start.1 = (bf16[1,64,3584]{2,1,0:T(8,128)(2,1)}, bf16[1,64,3584]{2,1,0:T(8,128)(2,1)}, u32[]{:S(2)}, u32[]{:S(2)}) collective-permute-start(bf16[1,64,3584]{2,1,0:T(8,128)(2,1)} %fusion.2), channel_id=1, source_target_pairs={{0,224},{32,0},{64,32},{96,64},{128,96},{160,128},{192,160},{224,1... | collective-permute-start | bytes 1376264 | tf_op jit(solution)/shard_map/ppermute | solution.py:18
  365.0 1.3 reshape_squeeze.20
  366.4 0.6 fusion.3
  367.0 0.1 collective-permute-start
  367.1 0.0 copy-start.1
  367.1 6.1 %convolution_bitcast_fusion = f32[1,1,256,3584]{3,2,1,0:T(8,128)} fusion(bf16[640,3584]{1,0:T(8,128)(2,1)} %reshape_squeeze.18, f32[640,256]{1,0:T(8,128)} %copy-done.5), kind=kOutput, calls=%fused_computation.2 | convolution fusion | flops 1175224320 | bytes 8912896 | tf_op jit(solution)/shard_map/rf,rd->fd/dot_general | solution.py:238
  373.2 10.4 %collective-permute-done.1 = bf16[1,64,3584]{2,1,0:T(8,128)(2,1)} collective-permute-done((bf16[1,64,3584]{2,1,0:T(8,128)(2,1)}, bf16[1,64,3584]{2,1,0:T(8,128)(2,1)}, u32[]{:S(2)}, u32[]{:S(2)}) %collective-permute-start.1) | collective-permute-done | bytes 458784 | tf_op jit(solution)/shard_map/ppermute | solution.py:18
  383.6 22.4 %collective-permute-done = bf16[1,64,3584]{2,1,0:T(8,128)(2,1)S(1)} collective-permute-done((bf16[1,64,3584]{2,1,0:T(8,128)(2,1)S(1)}, bf16[1,64,3584]{2,1,0:T(8,128)(2,1)S(1)}, u32[]{:S(2)}, u32[]{:S(2)}) %collective-permute-start) | collective-permute-done | bytes 458784 | tf_op jit(solution)/shard_map/ppermute | solution.py:18
  406.0 0.8 copy.35
  406.8 1.8 copy.36
  (15 shorter events, 0.0 us)
Async XLA Ops:
  0.6 183.0 %copy-start = (bf16[1,1,3584,256]{3,2,1,0:T(8,128)(2,1)S(1)}, bf16[1,1,3584,256]{3,2,1,0:T(8,128)(2,1)}, u32[]{:S(2)}) copy-start(bf16[1,1,3584,256]{3,2,1,0:T(8,128)(2,1)} %param.16) | copy-start | bytes 5505028
  2.9 7.7 %copy-start.7 = (f32[1,64,2]{1,2,0:T(2,128)S(1)}, f32[1,64,2]{1,2,0:T(2,128)}, u32[]{:S(2)}) copy-start(f32[1,64,2]{1,2,0:T(2,128)} %param.11) | copy-start | bytes 1540
  3.2 8.1 %copy-start.4 = (bf16[1,64,3584]{2,1,0:T(8,128)(2,1)S(1)}, bf16[1,64,3584]{2,1,0:T(8,128)(2,1)}, u32[]{:S(2)}) copy-start(bf16[1,64,3584]{2,1,0:T(8,128)(2,1)} %param.9) | copy-start | bytes 1376260
  183.7 4.6 %copy-start.2 = (bf16[640,3584]{1,0:T(8,128)(2,1)S(1)}, bf16[640,3584]{1,0:T(8,128)(2,1)}, u32[]{:S(2)}) copy-start(bf16[640,3584]{1,0:T(8,128)(2,1)} %reshape_squeeze.18) | copy-start | bytes 13762564
  183.7 4.6 %copy-start.8 = (bf16[1,1,256,3584]{3,2,1,0:T(8,128)(2,1)S(1)}, bf16[1,1,256,3584]{3,2,1,0:T(8,128)(2,1)}, u32[]{:S(2)}) copy-start(bf16[1,1,256,3584]{3,2,1,0:T(8,128)(2,1)} %param.17) | copy-start | bytes 5505028
  187.5 0.8 copy-start.5
  193.2 24.9 %all-to-all-start.2 = ((bf16[2,2,160,3584]{3,2,1,0:T(8,128)(2,1)}), bf16[2,2,160,3584]{3,2,1,0:T(8,128)(2,1)}, u32[]{:S(2)}, u32[]{:S(2)}) async-start(bf16[2,2,160,3584]{3,2,1,0:T(8,128)(2,1)} %bitcast.70), calls=%async_computation.2 | async-start | bytes 9175040 | tf_op jit(solution)/shard_map/all_to_all | solution.py:214
  218.1 10.9 %all-to-all-start = ((bf16[2,2,160,3584]{3,2,1,0:T(8,128)(2,1)}), bf16[2,2,160,3584]{3,2,1,0:T(8,128)(2,1)}, u32[]{:S(2)}, u32[]{:S(2)}) async-start(bf16[2,2,160,3584]{3,2,1,0:T(8,128)(2,1)} %bitcast.71), calls=%async_computation | async-start | bytes 9175040 | tf_op jit(solution)/shard_map/all_to_all | solution.py:214
  229.0 32.1 %all-to-all-start.3 = ((bf16[2,160,3584]{2,1,0:T(8,128)(2,1)}), bf16[2,160,3584]{2,1,0:T(8,128)(2,1)}, u32[]{:S(2)}, u32[]{:S(2)}) async-start(bf16[2,160,3584]{2,1,0:T(8,128)(2,1)} %reduce_sum.116), calls=%async_computation.3 | async-start | bytes 4587520 | tf_op jit(solution)/shard_map/all_to_all | solution.py:216
  261.0 31.2 %all-to-all-start.1 = ((bf16[2,160,3584]{2,1,0:T(8,128)(2,1)}), bf16[2,160,3584]{2,1,0:T(8,128)(2,1)}, u32[]{:S(2)}, u32[]{:S(2)}) async-start(bf16[2,160,3584]{2,1,0:T(8,128)(2,1)} %reduce_sum.114), calls=%async_computation.1 | async-start | bytes 4587520 | tf_op jit(solution)/shard_map/all_to_all | solution.py:216
  354.0 2.1 copy-start.3
  356.1 10.2 %copy-start.6 = (f32[64,160]{1,0:T(8,128)S(1)}, f32[64,160]{1,0:T(8,128)}, u32[]{:S(2)}) copy-start(f32[64,160]{1,0:T(8,128)} %get-tuple-element.7) | copy-start | bytes 122884
  358.8 24.8 %collective-permute-start.1 = (bf16[1,64,3584]{2,1,0:T(8,128)(2,1)}, bf16[1,64,3584]{2,1,0:T(8,128)(2,1)}, u32[]{:S(2)}, u32[]{:S(2)}) collective-permute-start(bf16[1,64,3584]{2,1,0:T(8,128)(2,1)} %fusion.2), channel_id=1, source_target_pairs={{0,224},{32,0},{64,32},{96,64},{128,96},{160,128},{192,160},{224,1... | collective-permute-start | bytes 1376264 | tf_op jit(solution)/shard_map/ppermute | solution.py:18
  367.0 39.1 %collective-permute-start = (bf16[1,64,3584]{2,1,0:T(8,128)(2,1)S(1)}, bf16[1,64,3584]{2,1,0:T(8,128)(2,1)S(1)}, u32[]{:S(2)}, u32[]{:S(2)}) collective-permute-start(bf16[1,64,3584]{2,1,0:T(8,128)(2,1)S(1)} %fusion.3), channel_id=1, source_target_pairs={{0,32},{32,64},{64,96},{96,128},{128,160},{160,192},{192,224},{224... | collective-permute-start | bytes 1376264 | tf_op jit(solution)/shard_map/ppermute | solution.py:18
  367.1 41.6 %copy-start.1 = (bf16[1,1,3584,256]{3,2,1,0:T(8,128)(2,1)S(1)}, bf16[1,1,3584,256]{3,2,1,0:T(8,128)(2,1)}, u32[]{:S(2)}) copy-start(bf16[1,1,3584,256]{3,2,1,0:T(8,128)(2,1)} %param.16) | copy-start | bytes 5505028

commit v5 on v4

--- a/solution.py
+++ b/solution.py
@@ -56,7 +56,8 @@
 
 def dispatch_kernel(groups, *refs):
     sources = refs[:3]
-    out, local_sem, send1, recv1, xs_send, xs_recv, cs_send, cs_recv, fw_send, fw_recv = refs[3:]
+    outs = refs[3:6]
+    local_sem, send1, recv1, xs_send, xs_recv, cs_send, cs_recv, fw_send, fw_recv = refs[6:]
     mesh_kind = pl.DeviceIdType.MESH
     pipe = lax.axis_index("pipe")
     me = lax.axis_index("eg")
@@ -71,13 +72,13 @@
     pl.semaphore_wait(barrier, len(peers) + 2)
     first = []
     for index, source in enumerate(sources):
-        own = pltpu.make_async_copy(source.at[me], out.at[index, core, chip, me], local_sem.at[index])
+        own = pltpu.make_async_copy(source.at[me], outs[index].at[core, chip, me], local_sem.at[index])
         own.start()
         copies = []
         for step in range(1, groups):
             copy = pltpu.make_async_remote_copy(
                 src_ref=source.at[peers[step - 1][1]],
-                dst_ref=out.at[index, core, chip, me],
+                dst_ref=outs[index].at[core, chip, me],
                 send_sem=send1.at[index, step],
                 recv_sem=recv1.at[index, step],
                 device_id=peers[step - 1],
@@ -92,7 +93,7 @@
         own.wait()
         for copy in copies:
             copy.wait_recv()
-        block = out.at[index, core, chip]
+        block = outs[index].at[core, chip]
         far = pltpu.make_async_remote_copy(
             src_ref=block, dst_ref=block, send_sem=xs_send.at[index], recv_sem=xs_recv.at[index],
             device_id=across, device_id_type=mesh_kind,
@@ -108,7 +109,7 @@
     for index in range(len(sources)):
         far, near = second[index]
         far.wait_recv()
-        relay = out.at[index, core, 1 - chip]
+        relay = outs[index].at[core, 1 - chip]
         onward = pltpu.make_async_remote_copy(
             src_ref=relay, dst_ref=relay, send_sem=fw_send.at[index], recv_sem=fw_recv.at[index],
             device_id=partner, device_id_type=mesh_kind,
@@ -134,9 +135,9 @@
     dma = pltpu.SemaphoreType.DMA
     return pl.pallas_call(
         functools.partial(dispatch_kernel, groups),
-        out_shape=jax.ShapeDtypeStruct((count, 2, 2, groups) + tail, wires[0].dtype),
+        out_shape=[jax.ShapeDtypeStruct((2, 2, groups) + tail, wires[0].dtype)] * count,
         in_specs=[pl.BlockSpec(memory_space=pl.ANY)] * count,
-        out_specs=pl.BlockSpec(memory_space=pl.ANY),
+        out_specs=[pl.BlockSpec(memory_space=pl.ANY)] * count,
         scratch_shapes=[
             dma((count,)),
             dma((count, groups)),
@@ -194,7 +195,7 @@
             copy.wait_recv()
 
 
-def send_home(wires):
+def send_home(wires, tag):
     groups = wires[0].shape[0]
     count = len(wires)
     dma = pltpu.SemaphoreType.DMA
@@ -204,7 +205,7 @@
         in_specs=[pl.BlockSpec(memory_space=pl.ANY)] * count,
         out_specs=pl.BlockSpec(memory_space=pl.ANY),
         scratch_shapes=[dma((count,)), dma((count, groups)), dma((count, groups))],
-        compiler_params=pltpu.CompilerParams(collective_id=1, has_side_effects=True),
+        compiler_params=pltpu.CompilerParams(collective_id=tag, has_side_effects=True),
     )(*wires)
 
 
@@ -266,9 +267,8 @@
     wire_f = group_sum(part, experts)
     dpart, grad_up, grad_down = expert_backward(got_x, got_g, up_proj, down_proj)
     wire_b = group_sum(dpart, experts)
-    home = send_home([wire_f, wire_b])
-    summed_f = home[0].reshape(-1, model_width).astype(jnp.float32)
-    summed_b = home[1].reshape(-1, model_width).astype(jnp.float32)
+    summed_f = send_home([wire_f], 1)[0].reshape(-1, model_width).astype(jnp.float32)
+    summed_b = send_home([wire_b], 2)[0].reshape(-1, model_width).astype(jnp.float32)
     merged = jnp.dot(gated_f, summed_f, precision=HIGH)
     section_out = (fwd_input.astype(jnp.float32) + merged).astype(jnp.bfloat16)
     spread_back = jnp.dot(plain_b, summed_b, precision=HIGH)

time: 410 us -> 385 us (0.939)
  waiting for transfers between devices: 70.8 us -> 38.7 us
  Pallas kernels: 193 us -> 211 us
  local copies, waits for them, and re-layouts: 59.5 us -> 47.7 us
    reshape x0 -> x3, local copies, waits for them, and re-layouts: none -> 27.1 us  [local(): got[index].reshape(-1, model_width)]
    another operation x5 -> x2, local copies, waits for them, and re-layouts: 30.5 us -> 4.72 us  [the longest x1 2.36 us: local(): send_home([wire_f], 1)[0].reshape(-1, model_width).astype(jnp.float32)]
    pallas_call x1 -> x2, Pallas kernels: 55.6 us -> 73.2 us  [send_home(): pl.pallas_call(functools.partial(return_kernel, groups), out_shape=jax.Sh...]
    ppermute x2, waiting for transfers between devices: 32.8 us -> 16.7 us  [passed_along(): return lax.ppermute(value, axis, pairs)]
    all_to_all x2, waiting for transfers between devices: 37.9 us -> 22 us  [group_sum(): other = lax.all_to_all(pair, 'ez', split_axis=0, concat_axis=0, tiled=True)]
    slice x2 -> x0, local copies, waits for them, and re-layouts: 11.7 us -> none  [the longest x1 9.98 us: local(): got[index].reshape(-1, model_width)]
  transfers between devices with their start and end apart: 6 -> 6, of which waited for: 4 -> 2; matrix products, arithmetic and copies ran while one was open for 12% -> 17% of each run, Pallas kernels for 0% -> 19%
where the time goes in v5:
time: 385 us; the launch traced here: 383 us
  Pallas kernels  211 us (55%)
  local copies, waits for them, and re-layouts  47.7 us (12%)
  waiting for transfers between devices  38.7 us (10%)
  matrix products  36.4 us (9%)
  starting transfers between devices  29.7 us (8%)
  other arithmetic  18.3 us (5%)
    pallas_call x1, Pallas kernels, dispatch(): pl.pallas_call(functools.partial(dispatch_kernel, groups), out_shape=[jax...  138 us
    pallas_call x2, Pallas kernels, send_home(): pl.pallas_call(functools.partial(return_kernel, groups), out_shape=jax.Sh...  73.2 us
    reshape x3, local copies, waits for them, and re-layouts, local(): got[index].reshape(-1, model_width)  27.1 us
    all_to_all x2, waiting for transfers between devices, group_sum(): other = lax.all_to_all(pair, 'ez', split_axis=0, concat_axis=0, tiled=True)  22 us
    ppermute x2, waiting for transfers between devices, passed_along(): return lax.ppermute(value, axis, pairs)  16.7 us
    all_to_all x2, starting transfers between devices, group_sum(): mine = lax.all_to_all(blocks, 'ec', split_axis=0, concat_axis=0, tiled=True)  11.7 us
    reshape x5, local copies, waits for them, and re-layouts, to_wire(): return rows.reshape(*lead, -1, 128)  11.4 us
    reduce_sum x2, other arithmetic, group_sum(): pair = jnp.sum(mine.astype(jnp.float32), axis=0).astype(jnp.bfloat16)  10.3 us
  transfers between devices with their start and end apart: 6, of which 2 were waited for; matrix products, arithmetic and copies ran while one was open for 17% of the time, Pallas kernels for 19%

profile of v5, /device:TPU:1, one launch (start us, length us, event | category | flops | bytes accessed | tf_op | source)
XLA Modules:
  0.0 382.7 jit_solution(9968308262471893836)
XLA Ops:
  0.6 0.0 copy-start
  0.6 0.9 copy.29
  1.6 0.1 eq.58
  1.7 0.8 copy.31
  2.5 0.1 eq.65
  2.6 0.1 fusion.27
  2.7 0.2 reduce_window_sum.18
  2.9 0.2 select_reduce_fusion.2
  3.0 0.1 reduce_sum.111
  3.2 0.0 copy-start.3
  3.2 0.1 copy.32
  3.3 0.7 bitcast_add_fusion
  4.0 0.1 fusion.28
  4.1 0.2 reduce_window_sum.17
  4.3 0.2 select_reduce_fusion.3
  4.5 0.1 reduce_sum.107
  4.6 0.1 copy.30
  4.7 0.7 bitcast_add_fusion.1
  5.4 0.8 select_reduce_fusion
  6.2 2.1 convolution_convert_fusion.2
  8.3 2.3 reshape.84.refs_2_
  10.6 0.0 copy-done.6
  10.6 0.7 convert_reduce_fusion.1
  11.3 0.5 convolution_convert_fusion.4
  11.8 2.3 reshape.82.refs_0_
  14.1 1.5 convolution_convert_fusion.3
  15.6 2.3 reshape.83.refs_1_
  17.9 137.7 %shard_map.120 = (bf16[2,2,8,560,128]{4,3,2,1,0:T(8,128)(2,1)}, bf16[2,2,8,560,128]{4,3,2,1,0:T(8,128)(2,1)}, bf16[2,2,8,560,128]{4,3,2,1,0:T(8,128)(2,1)}) custom-call(bf16[8,560,128]{2,1,0:T(8,128)(2,1)} %reshape.82.refs_0_, bf16[8,560,128]{2,1,0:T(8,128)(2,1)} %reshape.83.refs_1_, bf16[8,560,128]{2,1,0:T(8,128)(2,1)} %reshape.84.refs_2_), custom_call_target="tpu_custom_call" | custom-call | tf_op jit(solution)/shard_map/pallas_call | solution.py:136
  155.6 9.0 %reshape.85 = bf16[640,3584]{1,0:T(8,128)(2,1)} reshape(bf16[2,2,8,560,128]{4,3,2,1,0:T(8,128)(2,1)} %get-tuple-element.7) | data formatting | bytes 9175040 | tf_op jit(solution)/shard_map/reshape | solution.py:265
  164.7 9.9 %convolution_convert_fusion.1 = bf16[640,3584]{1,0:T(8,128)(2,1)} fusion(bf16[1,1,256,3584]{3,2,1,0:T(8,128)(2,1)} %param.17, bf16[640,3584]{1,0:T(8,128)(2,1)} %reshape.85, bf16[1,1,3584,256]{3,2,1,0:T(8,128)(2,1)S(1)} %copy-done), kind=kOutput, calls=%fused_computation.1 | convolution fusion | flops 2351923200 | bytes 12845056 | tf_op jit(solution)/shard_map/...f,fd->...d/dot_general | solution.py:225
  174.5 5.9 %all-to-all-start = ((bf16[2,2,160,3584]{3,2,1,0:T(8,128)(2,1)}), bf16[2,2,160,3584]{3,2,1,0:T(8,128)(2,1)}, u32[]{:S(2)}, u32[]{:S(2)}) async-start(bf16[2,2,160,3584]{3,2,1,0:T(8,128)(2,1)} %bitcast.71), calls=%async_computation | async-start | bytes 9175040 | tf_op jit(solution)/shard_map/all_to_all | solution.py:215
  180.4 9.0 %reshape.88 = bf16[640,3584]{1,0:T(8,128)(2,1)} reshape(bf16[2,2,8,560,128]{4,3,2,1,0:T(8,128)(2,1)} %get-tuple-element.8) | data formatting | bytes 9175040 | tf_op jit(solution)/shard_map/reshape | solution.py:265
  189.5 9.1 %reshape.89 = bf16[640,3584]{1,0:T(8,128)(2,1)} reshape(bf16[2,2,8,560,128]{4,3,2,1,0:T(8,128)(2,1)} %get-tuple-element.9) | data formatting | bytes 9175040 | tf_op jit(solution)/shard_map/reshape | solution.py:265
  198.5 3.8 fusion.8
  202.3 0.5 copy-done.7
  202.8 1.4 fusion.15
  204.2 3.6 convolution_convert_fusion
  207.8 0.0 all-to-all-done
  207.8 5.8 %all-to-all-start.2 = ((bf16[2,2,160,3584]{3,2,1,0:T(8,128)(2,1)}), bf16[2,2,160,3584]{3,2,1,0:T(8,128)(2,1)}, u32[]{:S(2)}, u32[]{:S(2)}) async-start(bf16[2,2,160,3584]{3,2,1,0:T(8,128)(2,1)} %bitcast.70), calls=%async_computation.2 | async-start | bytes 9175040 | tf_op jit(solution)/shard_map/all_to_all | solution.py:215
  213.6 5.1 %reduce_sum.114 = bf16[2,160,3584]{2,1,0:T(8,128)(2,1)} reduce(bf16[2,2,160,3584]{3,2,1,0:T(8,128)(2,1)} %all-to-all-done, bf16[]{:T(256)} %constant.23.clone.1), dimensions={0}, to_apply=%region_8.9 | reduce | flops 1146880 | bytes 6881282 | tf_op jit(solution)/shard_map/reduce_sum | solution.py:216
  218.7 0.0 all-to-all-done.2
  218.7 4.9 %all-to-all-start.1 = ((bf16[2,160,3584]{2,1,0:T(8,128)(2,1)}), bf16[2,160,3584]{2,1,0:T(8,128)(2,1)}, u32[]{:S(2)}, u32[]{:S(2)}) async-start(bf16[2,160,3584]{2,1,0:T(8,128)(2,1)} %reduce_sum.114), calls=%async_computation.1 | async-start | bytes 4587520 | tf_op jit(solution)/shard_map/all_to_all | solution.py:217
  223.6 5.1 %reduce_sum.116 = bf16[2,160,3584]{2,1,0:T(8,128)(2,1)} reduce(bf16[2,2,160,3584]{3,2,1,0:T(8,128)(2,1)} %all-to-all-done.2, bf16[]{:T(256)} %constant.23.clone.1), dimensions={0}, to_apply=%region_10.11 | reduce | flops 1146880 | bytes 6881282 | tf_op jit(solution)/shard_map/reduce_sum | solution.py:216
  228.8 22.0 %all-to-all-done.1 = bf16[2,160,3584]{2,1,0:T(8,128)(2,1)} async-done(((bf16[2,160,3584]{2,1,0:T(8,128)(2,1)}), bf16[2,160,3584]{2,1,0:T(8,128)(2,1)}, u32[]{:S(2)}, u32[]{:S(2)}) %all-to-all-start.1) | async-done | bytes 2293792 | tf_op jit(solution)/shard_map/all_to_all | solution.py:217
  250.8 5.1 %all-to-all-start.3 = ((bf16[2,160,3584]{2,1,0:T(8,128)(2,1)}), bf16[2,160,3584]{2,1,0:T(8,128)(2,1)}, u32[]{:S(2)}, u32[]{:S(2)}) async-start(bf16[2,160,3584]{2,1,0:T(8,128)(2,1)} %reduce_sum.116), calls=%async_computation.3 | async-start | bytes 4587520 | tf_op jit(solution)/shard_map/all_to_all | solution.py:217
  255.9 5.8 %convolution_bitcast_fusion.1 = f32[1,1,3584,256]{3,2,1,0:T(8,128)} fusion(bf16[640,3584]{1,0:T(8,128)(2,1)} %reshape.89, bf16[640,256]{1,0:T(8,128)(2,1)S(1)} %fusion.15), kind=kOutput, calls=%fused_computation.3 | convolution fusion | flops 1174405120 | bytes 8585216 | tf_op jit(solution)/shard_map/rd,rf->df/dot_general | solution.py:238
  261.7 2.1 reduce_sum.115
  263.8 2.3 reshape.87.refs_0_
  266.1 26.7 %shard_map.121 = bf16[1,8,560,128]{3,2,1,0:T(8,128)(2,1)} custom-call(bf16[8,560,128]{2,1,0:T(8,128)(2,1)} %reshape.87.refs_0_), custom_call_target="tpu_custom_call" | custom-call | tf_op jit(solution)/shard_map/pallas_call | solution.py:202
  292.8 2.4 reshape_squeeze.8
  295.2 1.4 fusion.3
  296.6 4.6 %collective-permute-start = (bf16[1,64,3584]{2,1,0:T(8,128)(2,1)}, bf16[1,64,3584]{2,1,0:T(8,128)(2,1)S(1)}, u32[]{:S(2)}, u32[]{:S(2)}) collective-permute-start(bf16[1,64,3584]{2,1,0:T(8,128)(2,1)} %fusion.3), channel_id=1, source_target_pairs={{0,32},{32,64},{64,96},{96,128},{128,160},{160,192},{192,224},{224... | collective-permute-start | bytes 1376264 | tf_op jit(solution)/shard_map/ppermute | solution.py:18
  301.2 0.0 all-to-all-done.3
  301.2 2.1 reduce_sum.117
  303.4 2.3 reshape.91.refs_0_
  305.6 46.5 %shard_map.122 = bf16[1,8,560,128]{3,2,1,0:T(8,128)(2,1)} custom-call(bf16[8,560,128]{2,1,0:T(8,128)(2,1)} %reshape.91.refs_0_), custom_call_target="tpu_custom_call" | custom-call | tf_op jit(solution)/shard_map/pallas_call | solution.py:202
  352.1 2.4 reshape_squeeze.9
  354.5 0.6 fusion.2
  355.1 3.4 collective-permute-start.1
  358.5 5.9 %convolution_bitcast_fusion = f32[1,1,256,3584]{3,2,1,0:T(8,128)} fusion(bf16[640,3584]{1,0:T(8,128)(2,1)} %reshape.88, f32[640,256]{1,0:T(8,128)S(1)} %fusion.8), kind=kOutput, calls=%fused_computation.2 | convolution fusion | flops 1175224320 | bytes 8912896 | tf_op jit(solution)/shard_map/rf,rd->fd/dot_general | solution.py:239
  364.4 0.0 collective-permute-done
  364.4 16.7 %collective-permute-done.1 = bf16[1,64,3584]{2,1,0:T(8,128)(2,1)S(1)} collective-permute-done((bf16[1,64,3584]{2,1,0:T(8,128)(2,1)S(1)}, bf16[1,64,3584]{2,1,0:T(8,128)(2,1)S(1)}, u32[]{:S(2)}, u32[]{:S(2)}) %collective-permute-start.1) | collective-permute-done | bytes 458784 | tf_op jit(solution)/shard_map/ppermute | solution.py:18
  381.1 0.8 copy.35
  381.9 0.8 copy.36
  (12 shorter events, 0.0 us)
Async XLA Ops:
  0.6 164.0 %copy-start = (bf16[1,1,3584,256]{3,2,1,0:T(8,128)(2,1)S(1)}, bf16[1,1,3584,256]{3,2,1,0:T(8,128)(2,1)}, u32[]{:S(2)}) copy-start(bf16[1,1,3584,256]{3,2,1,0:T(8,128)(2,1)} %param.16) | copy-start | bytes 5505028
  2.9 7.7 %copy-start.6 = (f32[1,64,2]{1,2,0:T(2,128)S(1)}, f32[1,64,2]{1,2,0:T(2,128)}, u32[]{:S(2)}) copy-start(f32[1,64,2]{1,2,0:T(2,128)} %param.11) | copy-start | bytes 1540
  3.2 8.1 %copy-start.3 = (bf16[1,64,3584]{2,1,0:T(8,128)(2,1)S(1)}, bf16[1,64,3584]{2,1,0:T(8,128)(2,1)}, u32[]{:S(2)}) copy-start(bf16[1,64,3584]{2,1,0:T(8,128)(2,1)} %param.9) | copy-start | bytes 1376260
  174.5 33.2 %all-to-all-start = ((bf16[2,2,160,3584]{3,2,1,0:T(8,128)(2,1)}), bf16[2,2,160,3584]{3,2,1,0:T(8,128)(2,1)}, u32[]{:S(2)}, u32[]{:S(2)}) async-start(bf16[2,2,160,3584]{3,2,1,0:T(8,128)(2,1)} %bitcast.71), calls=%async_computation | async-start | bytes 9175040 | tf_op jit(solution)/shard_map/all_to_all | solution.py:215
  198.5 3.8 copy-start.2
  198.5 4.3 %copy-start.7 = (bf16[1,1,256,3584]{3,2,1,0:T(8,128)(2,1)S(1)}, bf16[1,1,256,3584]{3,2,1,0:T(8,128)(2,1)}, u32[]{:S(2)}) copy-start(bf16[1,1,256,3584]{3,2,1,0:T(8,128)(2,1)} %param.17) | copy-start | bytes 5505028
  207.8 11.0 %all-to-all-start.2 = ((bf16[2,2,160,3584]{3,2,1,0:T(8,128)(2,1)}), bf16[2,2,160,3584]{3,2,1,0:T(8,128)(2,1)}, u32[]{:S(2)}, u32[]{:S(2)}) async-start(bf16[2,2,160,3584]{3,2,1,0:T(8,128)(2,1)} %bitcast.70), calls=%async_computation.2 | async-start | bytes 9175040 | tf_op jit(solution)/shard_map/all_to_all | solution.py:215
  218.7 32.1 %all-to-all-start.1 = ((bf16[2,160,3584]{2,1,0:T(8,128)(2,1)}), bf16[2,160,3584]{2,1,0:T(8,128)(2,1)}, u32[]{:S(2)}, u32[]{:S(2)}) async-start(bf16[2,160,3584]{2,1,0:T(8,128)(2,1)} %reduce_sum.114), calls=%async_computation.1 | async-start | bytes 4587520 | tf_op jit(solution)/shard_map/all_to_all | solution.py:217
  250.8 50.4 %all-to-all-start.3 = ((bf16[2,160,3584]{2,1,0:T(8,128)(2,1)}), bf16[2,160,3584]{2,1,0:T(8,128)(2,1)}, u32[]{:S(2)}, u32[]{:S(2)}) async-start(bf16[2,160,3584]{2,1,0:T(8,128)(2,1)} %reduce_sum.116), calls=%async_computation.3 | async-start | bytes 4587520 | tf_op jit(solution)/shard_map/all_to_all | solution.py:217
  266.1 29.1 %copy-start.5 = (f32[64,160]{1,0:T(8,128)S(1)}, f32[64,160]{1,0:T(8,128)}, u32[]{:S(2)}) copy-start(f32[64,160]{1,0:T(8,128)} %get-tuple-element.13) | copy-start | bytes 122884
  296.6 67.8 %collective-permute-start = (bf16[1,64,3584]{2,1,0:T(8,128)(2,1)}, bf16[1,64,3584]{2,1,0:T(8,128)(2,1)S(1)}, u32[]{:S(2)}, u32[]{:S(2)}) collective-permute-start(bf16[1,64,3584]{2,1,0:T(8,128)(2,1)} %fusion.3), channel_id=1, source_target_pairs={{0,32},{32,64},{64,96},{96,128},{128,160},{160,192},{192,224},{224... | collective-permute-start | bytes 1376264 | tf_op jit(solution)/shard_map/ppermute | solution.py:18
  305.6 48.8 %copy-start.4 = (bf16[1,64,3584]{2,1,0:T(8,128)(2,1)S(1)}, bf16[1,64,3584]{2,1,0:T(8,128)(2,1)}, u32[]{:S(2)}) copy-start(bf16[1,64,3584]{2,1,0:T(8,128)(2,1)} %param.15) | copy-start | bytes 1376260
  355.1 26.0 %collective-permute-start.1 = (bf16[1,64,3584]{2,1,0:T(8,128)(2,1)S(1)}, bf16[1,64,3584]{2,1,0:T(8,128)(2,1)S(1)}, u32[]{:S(2)}, u32[]{:S(2)}) collective-permute-start(bf16[1,64,3584]{2,1,0:T(8,128)(2,1)S(1)} %fusion.2), channel_id=1, source_target_pairs={{0,224},{32,0},{64,32},{96,64},{128,96},{160,128},{192,160},{224,1... | collective-permute-start | bytes 1376264 | tf_op jit(solution)/shard_map/ppermute | solution.py:18
  358.5 24.2 %copy-start.1 = (bf16[1,1,3584,256]{3,2,1,0:T(8,128)(2,1)S(1)}, bf16[1,1,3584,256]{3,2,1,0:T(8,128)(2,1)}, u32[]{:S(2)}) copy-start(bf16[1,1,3584,256]{3,2,1,0:T(8,128)(2,1)} %param.16) | copy-start | bytes 5505028

commit v6 on v5

--- a/solution.py
+++ b/solution.py
@@ -72,13 +72,13 @@
     pl.semaphore_wait(barrier, len(peers) + 2)
     first = []
     for index, source in enumerate(sources):
-        own = pltpu.make_async_copy(source.at[me], outs[index].at[core, chip, me], local_sem.at[index])
+        own = pltpu.make_async_copy(source.at[me], outs[index].at[chip, core, me], local_sem.at[index])
         own.start()
         copies = []
         for step in range(1, groups):
             copy = pltpu.make_async_remote_copy(
                 src_ref=source.at[peers[step - 1][1]],
-                dst_ref=outs[index].at[core, chip, me],
+                dst_ref=outs[index].at[chip, core, me],
                 send_sem=send1.at[index, step],
                 recv_sem=recv1.at[index, step],
                 device_id=peers[step - 1],
@@ -93,7 +93,7 @@
         own.wait()
         for copy in copies:
             copy.wait_recv()
-        block = outs[index].at[core, chip]
+        block = outs[index].at[chip, core]
         far = pltpu.make_async_remote_copy(
             src_ref=block, dst_ref=block, send_sem=xs_send.at[index], recv_sem=xs_recv.at[index],
             device_id=across, device_id_type=mesh_kind,
@@ -109,7 +109,7 @@
     for index in range(len(sources)):
         far, near = second[index]
         far.wait_recv()
-        relay = outs[index].at[core, 1 - chip]
+        relay = outs[index].at[1 - chip, core]
         onward = pltpu.make_async_remote_copy(
             src_ref=relay, dst_ref=relay, send_sem=fw_send.at[index], recv_sem=fw_recv.at[index],
             device_id=partner, device_id_type=mesh_kind,
@@ -211,12 +211,9 @@
 
 def group_sum(parts, experts):
     model_width = parts.shape[-1]
-    blocks = parts.reshape(2, 2, -1, model_width)
-    mine = lax.all_to_all(blocks, "ec", split_axis=0, concat_axis=0, tiled=True)
-    pair = jnp.sum(mine.astype(jnp.float32), axis=0).astype(jnp.bfloat16)
-    other = lax.all_to_all(pair, "ez", split_axis=0, concat_axis=0, tiled=True)
-    summed = jnp.sum(other.astype(jnp.float32), axis=0).astype(jnp.bfloat16)
-    return to_wire(summed, experts)
+    blocks = parts.reshape(GROUP, -1, model_width)
+    summed = lax.psum_scatter(blocks, ("ez", "ec"), scatter_dimension=0, tiled=True)
+    return to_wire(summed.reshape(-1, model_width), experts)
 
 
 def expert_forward(rows, up_proj, down_proj):

time: 385 us -> 391 us (1.016)
  waiting for transfers between devices: 38.7 us -> 72.8 us
  starting transfers between devices: 29.7 us -> 10.6 us
  other arithmetic: 18.3 us -> 3.77 us
  between operations: 0.85 us -> 14.2 us
  Pallas kernels: 211 us -> 199 us
    reduce_scatter x0 -> x2, waiting for transfers between devices: none -> 60.5 us  [group_sum(): lax.psum_scatter(blocks, ('ez', 'ec'), scatter_dimension=0, tiled=True)]
    all_to_all x4 -> x0, waiting for transfers between devices: 22 us -> none  [the longest x2 22 us: group_sum(): other = lax.all_to_all(pair, 'ez', split_axis=0, concat_axis=0, tiled=True)]
    all_to_all x4 -> x0, starting transfers between devices: 21.7 us -> none  [the longest x2 11.7 us: group_sum(): mine = lax.all_to_all(blocks, 'ec', split_axis=0, concat_axis=0, tiled=True)]
    reduce_sum x4 -> x0, other arithmetic: 14.5 us -> none  [the longest x2 10.3 us: group_sum(): pair = jnp.sum(mine.astype(jnp.float32), axis=0).astype(jnp.bfloat16)]
    pallas_call x2, Pallas kernels: 73.2 us -> 61.3 us  [send_home(): pl.pallas_call(functools.partial(return_kernel, groups), out_shape=jax.Sh...]
    another operation x0 -> x2, local copies, waits for them, and re-layouts: none -> 6.65 us  [to_wire(): return rows.reshape(*lead, -1, 128)]
    reshape x5 -> x3, local copies, waits for them, and re-layouts: 11.4 us -> 6.86 us  [to_wire(): return rows.reshape(*lead, -1, 128)]
    ppermute x2, waiting for transfers between devices: 16.7 us -> 12.3 us  [passed_along(): return lax.ppermute(value, axis, pairs)]
  transfers between devices with their start and end apart: 6 -> 4, of which waited for: 2 -> 3; matrix products, arithmetic and copies ran while one was open for 17% -> 14% of each run, Pallas kernels for 19% -> 16%
where the time goes in v6:
time: 391 us; the launch traced here: 389 us
  Pallas kernels  199 us (51%)
  waiting for transfers between devices  72.8 us (19%)
  local copies, waits for them, and re-layouts  51.2 us (13%)
  matrix products  37.2 us (10%)
  between operations  14.2 us (4%)
  starting transfers between devices  10.6 us (3%)
    pallas_call x1, Pallas kernels, dispatch(): pl.pallas_call(functools.partial(dispatch_kernel, groups), out_shape=[jax...  138 us
    pallas_call x2, Pallas kernels, send_home(): pl.pallas_call(functools.partial(return_kernel, groups), out_shape=jax.Sh...  61.3 us
    reduce_scatter x2, waiting for transfers between devices, group_sum(): lax.psum_scatter(blocks, ('ez', 'ec'), scatter_dimension=0, tiled=True)  60.5 us
    reshape x3, local copies, waits for them, and re-layouts, local(): got[index].reshape(-1, model_width)  27.2 us
    ppermute x2, waiting for transfers between devices, passed_along(): return lax.ppermute(value, axis, pairs)  12.3 us
    ppermute x2, starting transfers between devices, passed_along(): return lax.ppermute(value, axis, pairs)  10.3 us
    dot_general x1, matrix products, expert_forward(): jnp.einsum('...f,fd->...d', act, down_proj, preferred_element_type=jnp.fl...  9.91 us
  transfers between devices with their start and end apart: 4, of which 3 were waited for; matrix products, arithmetic and copies ran while one was open for 14% of the time, Pallas kernels for 16%

profile of v6, /device:TPU:1, one launch (start us, length us, event | category | flops | bytes accessed | tf_op | source)
XLA Modules:
  0.0 388.9 jit_solution(493631364988745920)
XLA Ops:
  7.2 0.0 copy-start
  7.2 0.0 reduce-scatter.3.cloned.1.call-start
  7.2 0.9 copy.29
  8.1 0.1 eq.58
  8.3 0.8 copy.31
  9.0 0.1 eq.65
  9.2 0.1 fusion.27
  9.3 0.2 reduce_window_sum.18
  9.4 0.2 select_reduce_fusion.2
  9.6 0.1 reduce_sum.63
  9.8 0.1 copy.32
  9.8 0.7 bitcast_add_fusion
  10.5 0.1 fusion.28
  10.6 0.2 reduce_window_sum.17
  10.8 0.2 select_reduce_fusion.3
  11.0 0.1 reduce_sum.59
  11.1 0.1 copy.30
  11.2 0.7 bitcast_add_fusion.1
  11.9 0.8 select_reduce_fusion
  12.7 0.0 copy-start.6
  12.7 0.0 copy-start.2
  12.7 2.2 convolution_convert_fusion.2
  14.9 2.3 reshape.78.refs_2_
  17.2 0.0 copy-done.6
  17.2 0.7 convert_reduce_fusion.1
  17.9 0.0 copy-done.2
  17.9 0.5 convolution_convert_fusion.4
  18.4 2.3 reshape.76.refs_0_
  20.7 1.5 convolution_convert_fusion.3
  22.2 2.3 reshape.77.refs_1_
  24.5 137.7 %shard_map.120 = (bf16[2,2,8,560,128]{4,3,2,1,0:T(8,128)(2,1)}, bf16[2,2,8,560,128]{4,3,2,1,0:T(8,128)(2,1)}, bf16[2,2,8,560,128]{4,3,2,1,0:T(8,128)(2,1)}) custom-call(bf16[8,560,128]{2,1,0:T(8,128)(2,1)} %reshape.76.refs_0_, bf16[8,560,128]{2,1,0:T(8,128)(2,1)} %reshape.77.refs_1_, bf16[8,560,128]{2,1,0:T(8,128)(2,1)} %reshape.78.refs_2_), custom_call_target="tpu_custom_call" | custom-call | tf_op jit(solution)/shard_map/pallas_call | solution.py:136
  162.2 9.0 %reshape.79 = bf16[640,3584]{1,0:T(8,128)(2,1)} reshape(bf16[2,2,8,560,128]{4,3,2,1,0:T(8,128)(2,1)} %get-tuple-element.7) | data formatting | bytes 9175040 | tf_op jit(solution)/shard_map/reshape | solution.py:262
  171.2 0.0 copy-done
  171.2 9.9 %convolution_convert_fusion.1 = bf16[640,3584]{1,0:T(8,128)(2,1)} fusion(bf16[1,1,256,3584]{3,2,1,0:T(8,128)(2,1)} %param.17, bf16[640,3584]{1,0:T(8,128)(2,1)} %reshape.79, bf16[1,1,3584,256]{3,2,1,0:T(8,128)(2,1)S(1)} %copy-done), kind=kOutput, calls=%fused_computation.1 | convolution fusion | flops 2351923200 | bytes 12845056 | tf_op jit(solution)/shard_map/...f,fd->...d/dot_general | solution.py:222
  181.1 0.0 reduce-scatter.3.cloned.1.call-update
  181.2 0.2 reduce-scatter.5.cloned.1.call-start
  181.4 9.0 %reshape.81 = bf16[640,3584]{1,0:T(8,128)(2,1)} reshape(bf16[2,2,8,560,128]{4,3,2,1,0:T(8,128)(2,1)} %get-tuple-element.8) | data formatting | bytes 9175040 | tf_op jit(solution)/shard_map/reshape | solution.py:262
  190.4 9.1 %reshape.82 = bf16[640,3584]{1,0:T(8,128)(2,1)} reshape(bf16[2,2,8,560,128]{4,3,2,1,0:T(8,128)(2,1)} %get-tuple-element.9) | data formatting | bytes 9175040 | tf_op jit(solution)/shard_map/reshape | solution.py:262
  199.5 3.8 fusion.8
  203.3 0.0 copy-start.4
  203.4 0.8 copy-done.4
  204.2 0.0 copy-done.7
  204.2 1.4 fusion.15
  205.6 3.6 convolution_convert_fusion
  209.2 0.0 reduce-scatter.5.cloned.1.call-update
  209.2 5.8 %convolution_bitcast_fusion.1 = f32[1,1,3584,256]{3,2,1,0:T(8,128)} fusion(bf16[640,3584]{1,0:T(8,128)(2,1)} %reshape.82, bf16[640,256]{1,0:T(8,128)(2,1)S(1)} %fusion.15), kind=kOutput, calls=%fused_computation.3 | convolution fusion | flops 1174405120 | bytes 8585216 | tf_op jit(solution)/shard_map/rd,rf->df/dot_general | solution.py:235
  215.0 17.2 %reduce-scatter.3.cloned.1.call-done = bf16[1,160,3584]{2,1,0:T(8,128)(2,1)} async-done(((bf16[4,160,3584]{2,1,0:T(8,128)(2,1)}), bf16[1,160,3584]{2,1,0:T(8,128)(2,1)}) %reduce-scatter.3.cloned.1.call-update) | async-done | bytes 1146896 | tf_op jit(solution)/shard_map/reduce_scatter | solution.py:215
  232.2 3.3 reshape_reshape.6.refs_0_
  235.6 31.1 %shard_map.121 = bf16[1,8,560,128]{3,2,1,0:T(8,128)(2,1)} custom-call(bf16[8,560,128]{2,1,0:T(8,128)(2,1)} %reshape_reshape.6.refs_0_), custom_call_target="tpu_custom_call" | custom-call | tf_op jit(solution)/shard_map/pallas_call | solution.py:202
  266.7 2.4 reshape_squeeze.8
  269.1 2.2 fusion.3
  271.3 3.7 collective-permute-start
  274.9 43.3 %reduce-scatter.5.cloned.1.call-done = bf16[1,160,3584]{2,1,0:T(8,128)(2,1)} async-done(((bf16[4,160,3584]{2,1,0:T(8,128)(2,1)}), bf16[1,160,3584]{2,1,0:T(8,128)(2,1)}) %reduce-scatter.5.cloned.1.call-update) | async-done | bytes 1146896 | tf_op jit(solution)/shard_map/reduce_scatter | solution.py:215
  318.2 3.3 reshape_reshape.7.refs_0_
  321.6 30.2 %shard_map.122 = bf16[1,8,560,128]{3,2,1,0:T(8,128)(2,1)} custom-call(bf16[8,560,128]{2,1,0:T(8,128)(2,1)} %reshape_reshape.7.refs_0_), custom_call_target="tpu_custom_call" | custom-call | tf_op jit(solution)/shard_map/pallas_call | solution.py:202
  351.8 2.4 reshape_squeeze.9
  354.2 0.6 fusion.2
  354.8 6.6 %collective-permute-start.1 = (bf16[1,64,3584]{2,1,0:T(8,128)(2,1)S(1)}, bf16[1,64,3584]{2,1,0:T(8,128)(2,1)S(1)}, u32[]{:S(2)}, u32[]{:S(2)}) collective-permute-start(bf16[1,64,3584]{2,1,0:T(8,128)(2,1)S(1)} %fusion.2), channel_id=1, source_target_pairs={{0,224},{32,0},{64,32},{96,64},{128,96},{160,128},{192,160},{224,1... | collective-permute-start | bytes 1376264 | tf_op jit(solution)/shard_map/ppermute | solution.py:18
  361.4 0.0 copy-done.5
  361.4 5.8 %convolution_bitcast_fusion = f32[1,1,256,3584]{3,2,1,0:T(8,128)} fusion(bf16[640,3584]{1,0:T(8,128)(2,1)} %reshape.81, f32[640,256]{1,0:T(8,128)S(1)} %copy-done.5), kind=kOutput, calls=%fused_computation.2 | convolution fusion | flops 1175224320 | bytes 8912896 | tf_op jit(solution)/shard_map/rf,rd->fd/dot_general | solution.py:236
  367.2 0.0 collective-permute-done
  367.2 12.3 %collective-permute-done.1 = bf16[1,64,3584]{2,1,0:T(8,128)(2,1)S(1)} collective-permute-done((bf16[1,64,3584]{2,1,0:T(8,128)(2,1)S(1)}, bf16[1,64,3584]{2,1,0:T(8,128)(2,1)S(1)}, u32[]{:S(2)}, u32[]{:S(2)}) %collective-permute-start.1) | collective-permute-done | bytes 458784 | tf_op jit(solution)/shard_map/ppermute | solution.py:18
  379.5 1.8 copy.35
  381.3 0.8 copy.36
  (6 shorter events, 0.0 us)
Async XLA Ops:
  7.2 164.1 %copy-start = (bf16[1,1,3584,256]{3,2,1,0:T(8,128)(2,1)S(1)}, bf16[1,1,3584,256]{3,2,1,0:T(8,128)(2,1)}, u32[]{:S(2)}) copy-start(bf16[1,1,3584,256]{3,2,1,0:T(8,128)(2,1)} %param.16) | copy-start | bytes 5505028
  7.2 225.0 %reduce-scatter.3.cloned.1.call-start = ((), (), s32[]{:S(2)}) async-start(), calls=%async_computation.2 | async-start | bytes 5734400 | tf_op jit(solution)/shard_map/reduce_scatter | solution.py:215
  12.7 4.5 %copy-start.6 = (f32[1,64,2]{1,2,0:T(2,128)S(1)}, f32[1,64,2]{1,2,0:T(2,128)}, u32[]{:S(2)}) copy-start(f32[1,64,2]{1,2,0:T(2,128)} %param.11) | copy-start | bytes 1540
  12.7 5.2 %copy-start.2 = (bf16[1,64,3584]{2,1,0:T(8,128)(2,1)S(1)}, bf16[1,64,3584]{2,1,0:T(8,128)(2,1)}, u32[]{:S(2)}) copy-start(bf16[1,64,3584]{2,1,0:T(8,128)(2,1)} %param.9) | copy-start | bytes 1376260
  181.2 137.1 %reduce-scatter.5.cloned.1.call-start = ((), (), s32[]{:S(2)}) async-start(), calls=%async_computation.3 | async-start | bytes 5734400 | tf_op jit(solution)/shard_map/reduce_scatter | solution.py:215
  199.5 4.6 %copy-start.1 = (bf16[640,3584]{1,0:T(8,128)(2,1)S(1)}, bf16[640,3584]{1,0:T(8,128)(2,1)}, u32[]{:S(2)}) copy-start(bf16[640,3584]{1,0:T(8,128)(2,1)} %reshape.81) | copy-start | bytes 13762564
  199.5 4.6 %copy-start.7 = (bf16[1,1,256,3584]{3,2,1,0:T(8,128)(2,1)S(1)}, bf16[1,1,256,3584]{3,2,1,0:T(8,128)(2,1)}, u32[]{:S(2)}) copy-start(bf16[1,1,256,3584]{3,2,1,0:T(8,128)(2,1)} %param.17) | copy-start | bytes 5505028
  203.3 0.8 copy-start.4
  271.3 95.9 %collective-permute-start = (bf16[1,64,3584]{2,1,0:T(8,128)(2,1)}, bf16[1,64,3584]{2,1,0:T(8,128)(2,1)}, u32[]{:S(2)}, u32[]{:S(2)}) collective-permute-start(bf16[1,64,3584]{2,1,0:T(8,128)(2,1)} %fusion.3), channel_id=1, source_target_pairs={{0,32},{32,64},{64,96},{96,128},{128,160},{160,192},{192,224},{224... | collective-permute-start | bytes 1376264 | tf_op jit(solution)/shard_map/ppermute | solution.py:18
  321.6 32.6 %copy-start.3 = (bf16[1,64,3584]{2,1,0:T(8,128)(2,1)S(1)}, bf16[1,64,3584]{2,1,0:T(8,128)(2,1)}, u32[]{:S(2)}) copy-start(bf16[1,64,3584]{2,1,0:T(8,128)(2,1)} %param.15) | copy-start | bytes 1376260
  354.1 7.3 %copy-start.5 = (f32[640,256]{1,0:T(8,128)S(1)}, f32[640,256]{1,0:T(8,128)}, u32[]{:S(2)}) copy-start(f32[640,256]{1,0:T(8,128)} %copy-done.4) | copy-start | bytes 1966084
  354.8 24.7 %collective-permute-start.1 = (bf16[1,64,3584]{2,1,0:T(8,128)(2,1)S(1)}, bf16[1,64,3584]{2,1,0:T(8,128)(2,1)S(1)}, u32[]{:S(2)}, u32[]{:S(2)}) collective-permute-start(bf16[1,64,3584]{2,1,0:T(8,128)(2,1)S(1)} %fusion.2), channel_id=1, source_target_pairs={{0,224},{32,0},{64,32},{96,64},{128,96},{160,128},{192,160},{224,1... | collective-permute-start | bytes 1376264 | tf_op jit(solution)/shard_map/ppermute | solution.py:18
Sparse Core Ops, SparseCore 0:
  181.3 50.8 reduce-scatter.2
  234.8 83.3 reduce-scatter.4

commit v7 on v5

--- a/solution.py
+++ b/solution.py
@@ -70,8 +70,8 @@
     for peer in peers + [across, partner]:
         pl.semaphore_signal(barrier, 1, device_id=peer, device_id_type=mesh_kind)
     pl.semaphore_wait(barrier, len(peers) + 2)
-    first = []
-    for index, source in enumerate(sources):
+    def launch(index):
+        source = sources[index]
         own = pltpu.make_async_copy(source.at[me], outs[index].at[core, chip, me], local_sem.at[index])
         own.start()
         copies = []
@@ -86,13 +86,29 @@
             )
             copy.start()
             copies.append(copy)
-        first.append((own, copies))
+        return own, copies
+
+    def relay(index, far):
+        far.wait_recv()
+        held = outs[index].at[core, 1 - chip]
+        onward = pltpu.make_async_remote_copy(
+            src_ref=held, dst_ref=held, send_sem=fw_send.at[index], recv_sem=fw_recv.at[index],
+            device_id=partner, device_id_type=mesh_kind,
+        )
+        onward.start()
+        return onward
+
+    count = len(sources)
+    first = [launch(0)]
     second = []
-    for index in range(len(sources)):
+    third = []
+    for index in range(count):
         own, copies = first[index]
         own.wait()
         for copy in copies:
             copy.wait_recv()
+        if index + 1 < count:
+            first.append(launch(index + 1))
         block = outs[index].at[core, chip]
         far = pltpu.make_async_remote_copy(
             src_ref=block, dst_ref=block, send_sem=xs_send.at[index], recv_sem=xs_recv.at[index],
@@ -105,18 +121,10 @@
         )
         near.start()
         second.append((far, near))
-    third = []
-    for index in range(len(sources)):
-        far, near = second[index]
-        far.wait_recv()
-        relay = outs[index].at[core, 1 - chip]
-        onward = pltpu.make_async_remote_copy(
-            src_ref=relay, dst_ref=relay, send_sem=fw_send.at[index], recv_sem=fw_recv.at[index],
-            device_id=partner, device_id_type=mesh_kind,
-        )
-        onward.start()
-        third.append(onward)
-    for index in range(len(sources)):
+        if index >= 1:
+            third.append(relay(index - 1, second[index - 1][0]))
+    third.append(relay(count - 1, second[count - 1][0]))
+    for index in range(count):
         own, copies = first[index]
         for copy in copies:
             copy.wait_send()

time: 385 us -> 383 us (level)
  no operation moved by 1% of the time
where the time goes in v7:
time: 383 us; the launch traced here: 382 us
  Pallas kernels  208 us (54%)
  local copies, waits for them, and re-layouts  47.7 us (12%)
  waiting for transfers between devices  38.4 us (10%)
  matrix products  36.4 us (10%)
  starting transfers between devices  32.3 us (8%)
  other arithmetic  18.3 us (5%)
    pallas_call x1, Pallas kernels, dispatch(): pl.pallas_call(functools.partial(dispatch_kernel, groups), out_shape=[jax...  135 us
    pallas_call x2, Pallas kernels, send_home(): pl.pallas_call(functools.partial(return_kernel, groups), out_shape=jax.Sh...  73.3 us
    reshape x3, local copies, waits for them, and re-layouts, local(): got[index].reshape(-1, model_width)  27.1 us
    all_to_all x2, waiting for transfers between devices, group_sum(): other = lax.all_to_all(pair, 'ez', split_axis=0, concat_axis=0, tiled=True)  22.7 us
    ppermute x2, waiting for transfers between devices, passed_along(): return lax.ppermute(value, axis, pairs)  15.7 us
    all_to_all x2, starting transfers between devices, group_sum(): mine = lax.all_to_all(blocks, 'ec', split_axis=0, concat_axis=0, tiled=True)  11.7 us
    reshape x5, local copies, waits for them, and re-layouts, to_wire(): return rows.reshape(*lead, -1, 128)  11.4 us
    ppermute x2, starting transfers between devices, passed_along(): return lax.ppermute(value, axis, pairs)  10.6 us
  transfers between devices with their start and end apart: 6, of which 2 were waited for; matrix products, arithmetic and copies ran while one was open for 17% of the time, Pallas kernels for 19%

profile of v7, /device:TPU:1, one launch (start us, length us, event | category | flops | bytes accessed | tf_op | source)
XLA Modules:
  0.0 382.1 jit_solution(8269866332539250272)
XLA Ops:
  0.6 0.0 copy-start
  0.6 0.9 copy.29
  1.6 0.1 eq.58
  1.7 0.8 copy.31
  2.5 0.1 eq.65
  2.6 0.1 fusion.27
  2.7 0.2 reduce_window_sum.18
  2.9 0.2 select_reduce_fusion.2
  3.0 0.1 reduce_sum.111
  3.2 0.0 copy-start.3
  3.2 0.1 copy.32
  3.3 0.7 bitcast_add_fusion
  4.0 0.1 fusion.28
  4.1 0.2 reduce_window_sum.17
  4.3 0.2 select_reduce_fusion.3
  4.5 0.1 reduce_sum.107
  4.6 0.1 copy.30
  4.7 0.7 bitcast_add_fusion.1
  5.4 0.8 select_reduce_fusion
  6.2 2.1 convolution_convert_fusion.2
  8.3 2.3 reshape.84.refs_2_
  10.6 0.0 copy-done.6
  10.6 0.7 convert_reduce_fusion.1
  11.3 0.5 convolution_convert_fusion.4
  11.8 2.3 reshape.82.refs_0_
  14.1 1.5 convolution_convert_fusion.3
  15.6 2.3 reshape.83.refs_1_
  17.9 134.8 %shard_map.120 = (bf16[2,2,8,560,128]{4,3,2,1,0:T(8,128)(2,1)}, bf16[2,2,8,560,128]{4,3,2,1,0:T(8,128)(2,1)}, bf16[2,2,8,560,128]{4,3,2,1,0:T(8,128)(2,1)}) custom-call(bf16[8,560,128]{2,1,0:T(8,128)(2,1)} %reshape.82.refs_0_, bf16[8,560,128]{2,1,0:T(8,128)(2,1)} %reshape.83.refs_1_, bf16[8,560,128]{2,1,0:T(8,128)(2,1)} %reshape.84.refs_2_), custom_call_target="tpu_custom_call" | custom-call | tf_op jit(solution)/shard_map/pallas_call | solution.py:144
  152.7 9.0 %reshape.85 = bf16[640,3584]{1,0:T(8,128)(2,1)} reshape(bf16[2,2,8,560,128]{4,3,2,1,0:T(8,128)(2,1)} %get-tuple-element.7) | data formatting | bytes 9175040 | tf_op jit(solution)/shard_map/reshape | solution.py:273
  161.7 9.9 %convolution_convert_fusion.1 = bf16[640,3584]{1,0:T(8,128)(2,1)} fusion(bf16[1,1,256,3584]{3,2,1,0:T(8,128)(2,1)} %param.17, bf16[640,3584]{1,0:T(8,128)(2,1)} %reshape.85, bf16[1,1,3584,256]{3,2,1,0:T(8,128)(2,1)S(1)} %copy-done), kind=kOutput, calls=%fused_computation.1 | convolution fusion | flops 2351923200 | bytes 12845056 | tf_op jit(solution)/shard_map/...f,fd->...d/dot_general | solution.py:233
  171.6 5.9 %all-to-all-start = ((bf16[2,2,160,3584]{3,2,1,0:T(8,128)(2,1)}), bf16[2,2,160,3584]{3,2,1,0:T(8,128)(2,1)}, u32[]{:S(2)}, u32[]{:S(2)}) async-start(bf16[2,2,160,3584]{3,2,1,0:T(8,128)(2,1)} %bitcast.71), calls=%async_computation | async-start | bytes 9175040 | tf_op jit(solution)/shard_map/all_to_all | solution.py:223
  177.5 9.0 %reshape.88 = bf16[640,3584]{1,0:T(8,128)(2,1)} reshape(bf16[2,2,8,560,128]{4,3,2,1,0:T(8,128)(2,1)} %get-tuple-element.8) | data formatting | bytes 9175040 | tf_op jit(solution)/shard_map/reshape | solution.py:273
  186.6 9.1 %reshape.89 = bf16[640,3584]{1,0:T(8,128)(2,1)} reshape(bf16[2,2,8,560,128]{4,3,2,1,0:T(8,128)(2,1)} %get-tuple-element.9) | data formatting | bytes 9175040 | tf_op jit(solution)/shard_map/reshape | solution.py:273
  195.6 3.8 fusion.8
  199.4 0.5 copy-done.7
  199.9 1.4 fusion.15
  201.3 3.6 convolution_convert_fusion
  204.9 0.0 all-to-all-done
  204.9 5.9 %all-to-all-start.2 = ((bf16[2,2,160,3584]{3,2,1,0:T(8,128)(2,1)}), bf16[2,2,160,3584]{3,2,1,0:T(8,128)(2,1)}, u32[]{:S(2)}, u32[]{:S(2)}) async-start(bf16[2,2,160,3584]{3,2,1,0:T(8,128)(2,1)} %bitcast.70), calls=%async_computation.2 | async-start | bytes 9175040 | tf_op jit(solution)/shard_map/all_to_all | solution.py:223
  210.7 5.1 %reduce_sum.114 = bf16[2,160,3584]{2,1,0:T(8,128)(2,1)} reduce(bf16[2,2,160,3584]{3,2,1,0:T(8,128)(2,1)} %all-to-all-done, bf16[]{:T(256)} %constant.23.clone.1), dimensions={0}, to_apply=%region_8.9 | reduce | flops 1146880 | bytes 6881282 | tf_op jit(solution)/shard_map/reduce_sum | solution.py:224
  215.8 0.0 all-to-all-done.2
  215.8 4.9 %all-to-all-start.1 = ((bf16[2,160,3584]{2,1,0:T(8,128)(2,1)}), bf16[2,160,3584]{2,1,0:T(8,128)(2,1)}, u32[]{:S(2)}, u32[]{:S(2)}) async-start(bf16[2,160,3584]{2,1,0:T(8,128)(2,1)} %reduce_sum.114), calls=%async_computation.1 | async-start | bytes 4587520 | tf_op jit(solution)/shard_map/all_to_all | solution.py:225
  220.7 5.1 %reduce_sum.116 = bf16[2,160,3584]{2,1,0:T(8,128)(2,1)} reduce(bf16[2,2,160,3584]{3,2,1,0:T(8,128)(2,1)} %all-to-all-done.2, bf16[]{:T(256)} %constant.23.clone.1), dimensions={0}, to_apply=%region_10.11 | reduce | flops 1146880 | bytes 6881282 | tf_op jit(solution)/shard_map/reduce_sum | solution.py:224
  225.9 22.7 %all-to-all-done.1 = bf16[2,160,3584]{2,1,0:T(8,128)(2,1)} async-done(((bf16[2,160,3584]{2,1,0:T(8,128)(2,1)}), bf16[2,160,3584]{2,1,0:T(8,128)(2,1)}, u32[]{:S(2)}, u32[]{:S(2)}) %all-to-all-start.1) | async-done | bytes 2293792 | tf_op jit(solution)/shard_map/all_to_all | solution.py:225
  248.6 5.1 %all-to-all-start.3 = ((bf16[2,160,3584]{2,1,0:T(8,128)(2,1)}), bf16[2,160,3584]{2,1,0:T(8,128)(2,1)}, u32[]{:S(2)}, u32[]{:S(2)}) async-start(bf16[2,160,3584]{2,1,0:T(8,128)(2,1)} %reduce_sum.116), calls=%async_computation.3 | async-start | bytes 4587520 | tf_op jit(solution)/shard_map/all_to_all | solution.py:225
  253.7 5.8 %convolution_bitcast_fusion.1 = f32[1,1,3584,256]{3,2,1,0:T(8,128)} fusion(bf16[640,3584]{1,0:T(8,128)(2,1)} %reshape.89, bf16[640,256]{1,0:T(8,128)(2,1)S(1)} %fusion.15), kind=kOutput, calls=%fused_computation.3 | convolution fusion | flops 1174405120 | bytes 8585216 | tf_op jit(solution)/shard_map/rd,rf->df/dot_general | solution.py:246
  259.5 2.1 reduce_sum.115
  261.6 2.3 reshape.87.refs_0_
  263.9 26.9 %shard_map.121 = bf16[1,8,560,128]{3,2,1,0:T(8,128)(2,1)} custom-call(bf16[8,560,128]{2,1,0:T(8,128)(2,1)} %reshape.87.refs_0_), custom_call_target="tpu_custom_call" | custom-call | tf_op jit(solution)/shard_map/pallas_call | solution.py:210
  290.8 2.4 reshape_squeeze.8
  293.2 1.4 fusion.3
  294.6 6.7 %collective-permute-start = (bf16[1,64,3584]{2,1,0:T(8,128)(2,1)}, bf16[1,64,3584]{2,1,0:T(8,128)(2,1)S(1)}, u32[]{:S(2)}, u32[]{:S(2)}) collective-permute-start(bf16[1,64,3584]{2,1,0:T(8,128)(2,1)} %fusion.3), channel_id=1, source_target_pairs={{0,32},{32,64},{64,96},{96,128},{128,160},{160,192},{192,224},{224... | collective-permute-start | bytes 1376264 | tf_op jit(solution)/shard_map/ppermute | solution.py:18
  301.3 0.0 all-to-all-done.3
  301.3 2.1 reduce_sum.117
  303.4 2.3 reshape.91.refs_0_
  305.7 46.4 %shard_map.122 = bf16[1,8,560,128]{3,2,1,0:T(8,128)(2,1)} custom-call(bf16[8,560,128]{2,1,0:T(8,128)(2,1)} %reshape.91.refs_0_), custom_call_target="tpu_custom_call" | custom-call | tf_op jit(solution)/shard_map/pallas_call | solution.py:210
  352.0 2.4 reshape_squeeze.9
  354.4 0.6 fusion.2
  355.0 3.9 %collective-permute-start.1 = (bf16[1,64,3584]{2,1,0:T(8,128)(2,1)S(1)}, bf16[1,64,3584]{2,1,0:T(8,128)(2,1)S(1)}, u32[]{:S(2)}, u32[]{:S(2)}) collective-permute-start(bf16[1,64,3584]{2,1,0:T(8,128)(2,1)S(1)} %fusion.2), channel_id=1, source_target_pairs={{0,224},{32,0},{64,32},{96,64},{128,96},{160,128},{192,160},{224,1... | collective-permute-start | bytes 1376264 | tf_op jit(solution)/shard_map/ppermute | solution.py:18
  359.0 5.9 %convolution_bitcast_fusion = f32[1,1,256,3584]{3,2,1,0:T(8,128)} fusion(bf16[640,3584]{1,0:T(8,128)(2,1)} %reshape.88, f32[640,256]{1,0:T(8,128)S(1)} %fusion.8), kind=kOutput, calls=%fused_computation.2 | convolution fusion | flops 1175224320 | bytes 8912896 | tf_op jit(solution)/shard_map/rf,rd->fd/dot_general | solution.py:247
  364.9 0.0 collective-permute-done
  364.9 15.7 %collective-permute-done.1 = bf16[1,64,3584]{2,1,0:T(8,128)(2,1)S(1)} collective-permute-done((bf16[1,64,3584]{2,1,0:T(8,128)(2,1)S(1)}, bf16[1,64,3584]{2,1,0:T(8,128)(2,1)S(1)}, u32[]{:S(2)}, u32[]{:S(2)}) %collective-permute-start.1) | collective-permute-done | bytes 458784 | tf_op jit(solution)/shard_map/ppermute | solution.py:18
  380.5 0.8 copy.35
  381.3 0.8 copy.36
  (12 shorter events, 0.0 us)
Async XLA Ops:
  0.6 161.1 %copy-start = (bf16[1,1,3584,256]{3,2,1,0:T(8,128)(2,1)S(1)}, bf16[1,1,3584,256]{3,2,1,0:T(8,128)(2,1)}, u32[]{:S(2)}) copy-start(bf16[1,1,3584,256]{3,2,1,0:T(8,128)(2,1)} %param.16) | copy-start | bytes 5505028
  2.9 7.7 %copy-start.6 = (f32[1,64,2]{1,2,0:T(2,128)S(1)}, f32[1,64,2]{1,2,0:T(2,128)}, u32[]{:S(2)}) copy-start(f32[1,64,2]{1,2,0:T(2,128)} %param.11) | copy-start | bytes 1540
  3.2 8.1 %copy-start.3 = (bf16[1,64,3584]{2,1,0:T(8,128)(2,1)S(1)}, bf16[1,64,3584]{2,1,0:T(8,128)(2,1)}, u32[]{:S(2)}) copy-start(bf16[1,64,3584]{2,1,0:T(8,128)(2,1)} %param.9) | copy-start | bytes 1376260
  171.6 33.2 %all-to-all-start = ((bf16[2,2,160,3584]{3,2,1,0:T(8,128)(2,1)}), bf16[2,2,160,3584]{3,2,1,0:T(8,128)(2,1)}, u32[]{:S(2)}, u32[]{:S(2)}) async-start(bf16[2,2,160,3584]{3,2,1,0:T(8,128)(2,1)} %bitcast.71), calls=%async_computation | async-start | bytes 9175040 | tf_op jit(solution)/shard_map/all_to_all | solution.py:223
  195.6 3.8 copy-start.2
  195.6 4.3 %copy-start.7 = (bf16[1,1,256,3584]{3,2,1,0:T(8,128)(2,1)S(1)}, bf16[1,1,256,3584]{3,2,1,0:T(8,128)(2,1)}, u32[]{:S(2)}) copy-start(bf16[1,1,256,3584]{3,2,1,0:T(8,128)(2,1)} %param.17) | copy-start | bytes 5505028
  204.9 11.0 %all-to-all-start.2 = ((bf16[2,2,160,3584]{3,2,1,0:T(8,128)(2,1)}), bf16[2,2,160,3584]{3,2,1,0:T(8,128)(2,1)}, u32[]{:S(2)}, u32[]{:S(2)}) async-start(bf16[2,2,160,3584]{3,2,1,0:T(8,128)(2,1)} %bitcast.70), calls=%async_computation.2 | async-start | bytes 9175040 | tf_op jit(solution)/shard_map/all_to_all | solution.py:223
  215.8 32.8 %all-to-all-start.1 = ((bf16[2,160,3584]{2,1,0:T(8,128)(2,1)}), bf16[2,160,3584]{2,1,0:T(8,128)(2,1)}, u32[]{:S(2)}, u32[]{:S(2)}) async-start(bf16[2,160,3584]{2,1,0:T(8,128)(2,1)} %reduce_sum.114), calls=%async_computation.1 | async-start | bytes 4587520 | tf_op jit(solution)/shard_map/all_to_all | solution.py:225
  248.6 52.7 %all-to-all-start.3 = ((bf16[2,160,3584]{2,1,0:T(8,128)(2,1)}), bf16[2,160,3584]{2,1,0:T(8,128)(2,1)}, u32[]{:S(2)}, u32[]{:S(2)}) async-start(bf16[2,160,3584]{2,1,0:T(8,128)(2,1)} %reduce_sum.116), calls=%async_computation.3 | async-start | bytes 4587520 | tf_op jit(solution)/shard_map/all_to_all | solution.py:225
  263.9 29.3 %copy-start.5 = (f32[64,160]{1,0:T(8,128)S(1)}, f32[64,160]{1,0:T(8,128)}, u32[]{:S(2)}) copy-start(f32[64,160]{1,0:T(8,128)} %get-tuple-element.13) | copy-start | bytes 122884
  294.6 70.3 %collective-permute-start = (bf16[1,64,3584]{2,1,0:T(8,128)(2,1)}, bf16[1,64,3584]{2,1,0:T(8,128)(2,1)S(1)}, u32[]{:S(2)}, u32[]{:S(2)}) collective-permute-start(bf16[1,64,3584]{2,1,0:T(8,128)(2,1)} %fusion.3), channel_id=1, source_target_pairs={{0,32},{32,64},{64,96},{96,128},{128,160},{160,192},{192,224},{224... | collective-permute-start | bytes 1376264 | tf_op jit(solution)/shard_map/ppermute | solution.py:18
  305.7 48.7 %copy-start.4 = (bf16[1,64,3584]{2,1,0:T(8,128)(2,1)S(1)}, bf16[1,64,3584]{2,1,0:T(8,128)(2,1)}, u32[]{:S(2)}) copy-start(bf16[1,64,3584]{2,1,0:T(8,128)(2,1)} %param.15) | copy-start | bytes 1376260
  355.0 25.5 %collective-permute-start.1 = (bf16[1,64,3584]{2,1,0:T(8,128)(2,1)S(1)}, bf16[1,64,3584]{2,1,0:T(8,128)(2,1)S(1)}, u32[]{:S(2)}, u32[]{:S(2)}) collective-permute-start(bf16[1,64,3584]{2,1,0:T(8,128)(2,1)S(1)} %fusion.2), channel_id=1, source_target_pairs={{0,224},{32,0},{64,32},{96,64},{128,96},{160,128},{192,160},{224,1... | collective-permute-start | bytes 1376264 | tf_op jit(solution)/shard_map/ppermute | solution.py:18
  359.0 23.1 %copy-start.1 = (bf16[1,1,3584,256]{3,2,1,0:T(8,128)(2,1)S(1)}, bf16[1,1,3584,256]{3,2,1,0:T(8,128)(2,1)}, u32[]{:S(2)}) copy-start(bf16[1,1,3584,256]{3,2,1,0:T(8,128)(2,1)} %param.16) | copy-start | bytes 5505028

commit v8 on v7

--- a/solution.py
+++ b/solution.py
@@ -50,14 +50,21 @@
     ).astype(jnp.bfloat16)
 
 
+def split_slots(table, experts, slot_cap, main):
+    lead = table.shape[0]
+    shaped = table.reshape(lead, experts, slot_cap)
+    return (shaped[:, :, :main].reshape(lead, -1), shaped[:, :, main:].reshape(lead, -1))
+
+
 def to_wire(rows, *lead):
     return rows.reshape(*lead, -1, 128)
 
 
 def dispatch_kernel(groups, *refs):
-    sources = refs[:3]
-    outs = refs[3:6]
-    local_sem, send1, recv1, xs_send, xs_recv, cs_send, cs_recv, fw_send, fw_recv = refs[6:]
+    count = (len(refs) - 9) // 2
+    sources = refs[:count]
+    outs = refs[count:2 * count]
+    local_sem, send1, recv1, xs_send, xs_recv, cs_send, cs_recv, fw_send, fw_recv = refs[2 * count:]
     mesh_kind = pl.DeviceIdType.MESH
     pipe = lax.axis_index("pipe")
     me = lax.axis_index("eg")
@@ -139,11 +146,10 @@
 def dispatch(wires):
     groups = wires[0].shape[0]
     count = len(wires)
-    tail = wires[0].shape[1:]
     dma = pltpu.SemaphoreType.DMA
     return pl.pallas_call(
         functools.partial(dispatch_kernel, groups),
-        out_shape=[jax.ShapeDtypeStruct((2, 2, groups) + tail, wires[0].dtype)] * count,
+        out_shape=[jax.ShapeDtypeStruct((2, 2) + wire.shape, wire.dtype) for wire in wires],
         in_specs=[pl.BlockSpec(memory_space=pl.ANY)] * count,
         out_specs=[pl.BlockSpec(memory_space=pl.ANY)] * count,
         scratch_shapes=[
@@ -161,14 +167,21 @@
     )(*wires)
 
 
+def split_slots(table, experts, slot_cap, main):
+    lead = table.shape[0]
+    shaped = table.reshape(lead, experts, slot_cap)
+    return (shaped[:, :, :main].reshape(lead, -1), shaped[:, :, main:].reshape(lead, -1))
+
+
 def to_wire(rows, *lead):
     return rows.reshape(*lead, -1, 128)
 
 
 def return_kernel(groups, *refs):
-    count = len(refs) - 4
+    count = (len(refs) - 3) // 2
     sources = refs[:count]
-    out, local_sem, send1, recv1 = refs[count:]
+    outs = refs[count:2 * count]
+    local_sem, send1, recv1 = refs[2 * count:]
     mesh_kind = pl.DeviceIdType.MESH
     pipe = lax.axis_index("pipe")
     me = lax.axis_index("eg")
@@ -181,13 +194,13 @@
     pl.semaphore_wait(barrier, len(peers))
     started = []
     for index, source in enumerate(sources):
-        own = pltpu.make_async_copy(source.at[me], out.at[index, me], local_sem.at[index])
+        own = pltpu.make_async_copy(source.at[me], outs[index].at[me], local_sem.at[index])
         own.start()
         copies = []
         for step in range(1, groups):
             copy = pltpu.make_async_remote_copy(
                 src_ref=source.at[peers[step - 1][1]],
-                dst_ref=out.at[index, me],
+                dst_ref=outs[index].at[me],
                 send_sem=send1.at[index, step],
                 recv_sem=recv1.at[index, step],
                 device_id=peers[step - 1],
@@ -209,22 +222,21 @@
     dma = pltpu.SemaphoreType.DMA
     return pl.pallas_call(
         functools.partial(return_kernel, groups),
-        out_shape=jax.ShapeDtypeStruct((count,) + wires[0].shape, wires[0].dtype),
+        out_shape=[jax.ShapeDtypeStruct(wire.shape, wire.dtype) for wire in wires],
         in_specs=[pl.BlockSpec(memory_space=pl.ANY)] * count,
-        out_specs=pl.BlockSpec(memory_space=pl.ANY),
+        out_specs=[pl.BlockSpec(memory_space=pl.ANY)] * count,
         scratch_shapes=[dma((count,)), dma((count, groups)), dma((count, groups))],
         compiler_params=pltpu.CompilerParams(collective_id=tag, has_side_effects=True),
     )(*wires)
 
 
-def group_sum(parts, experts):
+def group_sum(parts):
     model_width = parts.shape[-1]
     blocks = parts.reshape(2, 2, -1, model_width)
     mine = lax.all_to_all(blocks, "ec", split_axis=0, concat_axis=0, tiled=True)
     pair = jnp.sum(mine.astype(jnp.float32), axis=0).astype(jnp.bfloat16)
     other = lax.all_to_all(pair, "ez", split_axis=0, concat_axis=0, tiled=True)
-    summed = jnp.sum(other.astype(jnp.float32), axis=0).astype(jnp.bfloat16)
-    return to_wire(summed, experts)
+    return jnp.sum(other.astype(jnp.float32), axis=0).astype(jnp.bfloat16)
 
 
 def expert_forward(rows, up_proj, down_proj):
@@ -263,24 +275,47 @@
     out_grad = back_grads[0]
     plain_f, gated_f = tables(fwd_routes[0], fwd_gates[0], experts, slot_cap)
     plain_b, gated_b = tables(back_routes[0], back_gates[0], experts, slot_cap)
-    buffer_f = gather_rows(plain_f, fwd_input)
-    buffer_x = gather_rows(plain_b, back_input)
-    buffer_g = lax.dot_general(
-        gated_b, out_grad.astype(jnp.float32), (((0,), (0,)), ((), ())), precision=HIGH
-    ).astype(jnp.bfloat16)
+    main = slot_cap // 8 * 8
     model_width = fwd_input.shape[-1]
-    got = dispatch([to_wire(b, experts) for b in (buffer_f, buffer_x, buffer_g)])
-    got_f, got_x, got_g = [got[index].reshape(-1, model_width) for index in range(3)]
-    part = expert_forward(got_f, up_proj, down_proj)
-    wire_f = group_sum(part, experts)
-    dpart, grad_up, grad_down = expert_backward(got_x, got_g, up_proj, down_proj)
-    wire_b = group_sum(dpart, experts)
-    summed_f = send_home([wire_f], 1)[0].reshape(-1, model_width).astype(jnp.float32)
-    summed_b = send_home([wire_b], 2)[0].reshape(-1, model_width).astype(jnp.float32)
-    merged = jnp.dot(gated_f, summed_f, precision=HIGH)
+    split = functools.partial(split_slots, experts=experts, slot_cap=slot_cap, main=main)
+    plain_f, gated_f, plain_b, gated_b = [split(table) for table in (plain_f, gated_f, plain_b, gated_b)]
+    grads_wide = out_grad.astype(jnp.float32)
+    wires = []
+    for index in range(2):
+        rows_f = gather_rows(plain_f[index], fwd_input)
+        rows_x = gather_rows(plain_b[index], back_input)
+        rows_g = lax.dot_general(
+            gated_b[index], grads_wide, (((0,), (0,)), ((), ())), precision=HIGH
+        ).astype(jnp.bfloat16)
+        if index == 0:
+            wires.append([rows.reshape(experts, main, model_width) for rows in (rows_f, rows_x, rows_g)])
+        else:
+            wires.append([to_wire(rows, experts) for rows in (rows_f, rows_x, rows_g)])
+    got = dispatch(wires[0] + wires[1])
+    got = [got[:3], got[3:]]
+    summed_f = []
+    summed_b = []
+    grad_up = 0.0
+    grad_down = 0.0
+    for index in range(2):
+        got_f, got_x, got_g = [block.reshape(-1, model_width) for block in got[index]]
+        part = expert_forward(got_f, up_proj, down_proj)
+        summed_f.append(group_sum(part))
+        dpart, more_up, more_down = expert_backward(got_x, got_g, up_proj, down_proj)
+        grad_up = grad_up + more_up
+        grad_down = grad_down + more_down
+        summed_b.append(group_sum(dpart))
+
+    def home(summed, tag):
+        shaped = [summed[0].reshape(experts, main, model_width), to_wire(summed[1], experts)]
+        return [block.reshape(-1, model_width).astype(jnp.float32) for block in send_home(shaped, tag)]
+
+    back_f = home(summed_f, 1)
+    back_b = home(summed_b, 2)
+    merged = jnp.dot(gated_f[0], back_f[0], precision=HIGH) + jnp.dot(gated_f[1], back_f[1], precision=HIGH)
     section_out = (fwd_input.astype(jnp.float32) + merged).astype(jnp.bfloat16)
-    spread_back = jnp.dot(plain_b, summed_b, precision=HIGH)
-    section_grad = (out_grad.astype(jnp.float32) + spread_back).astype(jnp.bfloat16)
+    spread_back = jnp.dot(plain_b[0], back_b[0], precision=HIGH) + jnp.dot(plain_b[1], back_b[1], precision=HIGH)
+    section_grad = (grads_wide + spread_back).astype(jnp.bfloat16)
     fwd_next = passed_along(section_out[None], "pipe", 1)
     back_next = passed_along(section_grad[None], "pipe", -1)
     return (fwd_next, back_next, grad_up[None, None], grad_down[None, None])

time: 383 us -> 411 us (1.073)
  matrix products: 36.4 us -> 54.9 us
  local copies, waits for them, and re-layouts: 47.7 us -> 29.6 us
  blocking collectives: 0 us -> 15.7 us
  other arithmetic: 18.3 us -> 24 us
    reshape x3 -> x8, local copies, waits for them, and re-layouts: 27.1 us -> 10 us  [the longest x3 7.87 us: local(): block.reshape(-1, model_width)]
    all_to_all x0 -> x2, blocking collectives: none -> 15.7 us  [group_sum(): mine = lax.all_to_all(blocks, 'ec', split_axis=0, concat_axis=0, tiled=True)]
    reshape x5, local copies, waits for them, and re-layouts: 11.4 us -> 4.98 us  [to_wire(): return rows.reshape(*lead, -1, 128)]
    pallas_call x2, Pallas kernels: 73.3 us -> 79.3 us  [send_home(): pl.pallas_call(functools.partial(return_kernel, groups), out_shape=[jax.S...]
    all_to_all x2 -> x4, starting transfers between devices: 9.98 us -> 14.6 us  [group_sum(): other = lax.all_to_all(pair, 'ez', split_axis=0, concat_axis=0, tiled=True)]
    another operation x2, local copies, waits for them, and re-layouts: 4.72 us -> 0.13 us  [the longest x1 2.36 us: local(): send_home([wire_b], 2)[0].reshape(-1, model_width).astype(jnp.float32)]
    slice x0 -> x9, local copies, waits for them, and re-layouts: none -> 4.57 us  [the longest x5 3.95 us: split_slots(): shaped[:, :, main:].reshape(lead, -1)]
    dot_general x3 -> x6, matrix products: 4.1 us -> 8.37 us  [the longest x2 2.84 us: local(): lax.dot_general(gated_b[index], grads_wide, (((0,), (0,)), ((), ())), pre...]
  transfers between devices with their start and end apart: 6 -> 8, of which waited for: 2 -> 5; matrix products, arithmetic and copies ran while one was open for 17% -> 18% of each run, Pallas kernels for 19% -> 19%
where the time goes in v8:
time: 411 us; the launch traced here: 409 us
  Pallas kernels  212 us (52%)
  matrix products  54.9 us (13%)
  waiting for transfers between devices  37.6 us (9%)
  starting transfers between devices  34 us (8%)
  local copies, waits for them, and re-layouts  29.6 us (7%)
  other arithmetic  24 us (6%)
  blocking collectives  15.7 us (4%)
    pallas_call x1, Pallas kernels, dispatch(): pl.pallas_call(functools.partial(dispatch_kernel, groups), out_shape=[jax...  133 us
    pallas_call x2, Pallas kernels, send_home(): pl.pallas_call(functools.partial(return_kernel, groups), out_shape=[jax.S...  79.3 us
    all_to_all x4, waiting for transfers between devices, group_sum(): other = lax.all_to_all(pair, 'ez', split_axis=0, concat_axis=0, tiled=True)  23.1 us
    all_to_all x2, blocking collectives, group_sum(): mine = lax.all_to_all(blocks, 'ec', split_axis=0, concat_axis=0, tiled=True)  15.7 us
    all_to_all x4, starting transfers between devices, group_sum(): other = lax.all_to_all(pair, 'ez', split_axis=0, concat_axis=0, tiled=True)  14.6 us
    ppermute x2, waiting for transfers between devices, passed_along(): return lax.ppermute(value, axis, pairs)  13 us
    dot_general x2, matrix products, expert_forward(): jnp.einsum('...f,fd->...d', act, down_proj, preferred_element_type=jnp.fl...  12.3 us
    reduce_sum x4, other arithmetic, group_sum(): pair = jnp.sum(mine.astype(jnp.float32), axis=0).astype(jnp.bfloat16)  12.2 us
  transfers between devices with their start and end apart: 8, of which 5 were waited for; matrix products, arithmetic and copies ran while one was open for 18% of the time, Pallas kernels for 19%

profile of v8, /device:TPU:1, one launch (start us, length us, event | category | flops | bytes accessed | tf_op | source)
XLA Modules:
  0.0 408.8 jit_solution(11118739433125236150)
XLA Ops:
  0.7 0.9 copy.29
  3.1 1.4 select_reduce_fusion.1
  5.3 0.8 copy.33
  7.5 1.4 select_reduce_fusion
  9.7 0.9 copy.35
  11.9 1.0 convolution_convert_fusion.7
  12.9 1.0 reshape.163.refs_5_
  13.9 0.9 convolution_convert_fusion.8
  14.8 1.0 reshape.161.refs_4_
  15.8 0.9 convolution_convert_fusion.9
  16.7 1.0 reshape.160.refs_3_
  17.7 1.8 convolution_convert_fusion.4
  19.5 2.1 convolution_convert_fusion.5
  21.6 1.3 convolution_convert_fusion.6
  22.9 132.7 %shard_map.120 = (bf16[2,2,8,16,3584]{4,3,2,1,0:T(8,128)(2,1)}, bf16[2,2,8,16,3584]{4,3,2,1,0:T(8,128)(2,1)}, bf16[2,2,8,16,3584]{4,3,2,1,0:T(8,128)(2,1)}, bf16...) custom-call(bf16[8,16,3584]{2,1,0:T(8,128)(2,1)} %bitcast.145, ...), custom_call_target="tpu_custom_call" | custom-call | tf_op jit(solution)/shard_map/pallas_call | solution.py:150
  155.6 2.9 reshape.176
  158.5 2.1 reshape.177
  163.8 1.7 convolution_convert_fusion.2
  165.5 4.5 %all-to-all-start.6 = ((bf16[2,2,32,3584]{3,2,1,0:T(8,128)(2,1)}), bf16[2,2,32,3584]{3,2,1,0:T(8,128)(2,1)}, u32[]{:S(2)}, u32[]{:S(2)}) async-start(bf16[2,2,32,3584]{3,2,1,0:T(8,128)(2,1)} %bitcast.139), calls=%async_computation.6 | async-start | bytes 1835008 | tf_op jit(solution)/shard_map/all_to_all | solution.py:236
  170.1 8.4 %convolution_convert_fusion.1 = bf16[512,3584]{1,0:T(8,128)(2,1)} fusion(bf16[1,1,256,3584]{3,2,1,0:T(8,128)(2,1)} %param.17, bf16[512,3584]{1,0:T(8,128)(2,1)} %bitcast.156, bf16[1,1,3584,256]{3,2,1,0:T(8,128)(2,1)S(1)} %copy-done), kind=kOutput, calls=%fused_computation.1 | convolution fusion | flops 1881538560 | bytes 11010048 | tf_op jit(solution)/shard_map/...f,fd->...d/dot_general | solution.py:245
  178.5 4.0 fusion.18
  182.4 2.9 reshape.167
  185.3 3.9 convolution_convert_fusion.3
  189.2 3.8 fusion.27
  193.0 3.0 convolution_convert_fusion
  196.0 5.6 %all-to-all-start = ((bf16[2,2,128,3584]{3,2,1,0:T(8,128)(2,1)}), bf16[2,2,128,3584]{3,2,1,0:T(8,128)(2,1)}, u32[]{:S(2)}, u32[]{:S(2)}) async-start(bf16[2,2,128,3584]{3,2,1,0:T(8,128)(2,1)} %bitcast.138), calls=%async_computation | async-start | bytes 7340032 | tf_op jit(solution)/shard_map/all_to_all | solution.py:236
  201.6 2.3 reduce_sum.168
  203.9 1.5 all-to-all-done
  205.4 4.5 %all_to_all.40 = bf16[2,2,32,3584]{3,2,1,0:T(8,128)(2,1)S(1)} all-to-all(bf16[2,2,32,3584]{3,2,1,0:T(8,128)(2,1)S(1)} %bitcast.142), channel_id=1, replica_groups=mesh['pipe'=8,'eg'=8,'ez'=2,'ec'=2] {'ec'}, dimensions={0} | all-to-all | bytes 1835008 | tf_op jit(solution)/shard_map/all_to_all | solution.py:236
  209.8 11.2 %all_to_all.41 = bf16[2,2,128,3584]{3,2,1,0:T(8,128)(2,1)} all-to-all(bf16[2,2,128,3584]{3,2,1,0:T(8,128)(2,1)} %bitcast.133), channel_id=1, replica_groups=mesh['pipe'=8,'eg'=8,'ez'=2,'ec'=2] {'ec'}, dimensions={0} | all-to-all | bytes 7340032 | tf_op jit(solution)/shard_map/all_to_all | solution.py:236
  221.1 3.5 all-to-all-start.7
  224.6 1.0 reduce_sum.164
  225.6 6.0 %all-to-all-done.7 = bf16[2,32,3584]{2,1,0:T(8,128)(2,1)S(1)} async-done(((bf16[2,32,3584]{2,1,0:T(8,128)(2,1)}), bf16[2,32,3584]{2,1,0:T(8,128)(2,1)S(1)}, u32[]{:S(2)}, u32[]{:S(2)}) %all-to-all-start.7) | async-done | bytes 458784 | tf_op jit(solution)/shard_map/all_to_all | solution.py:238
  231.6 3.5 all-to-all-start.3
  235.1 4.4 %reduce_sum.162 = bf16[2,128,3584]{2,1,0:T(8,128)(2,1)} reduce(bf16[2,2,128,3584]{3,2,1,0:T(8,128)(2,1)} %all-to-all-done, bf16[]{:T(256)} %constant.31.clone.1), dimensions={0}, to_apply=%region_8.9 | reduce | flops 917504 | bytes 5505026 | tf_op jit(solution)/shard_map/reduce_sum | solution.py:237
  239.4 1.7 all-to-all-done.3
  241.9 3.7 all-to-all-start.1
  245.6 4.5 %reduce_sum.166 = bf16[2,128,3584]{2,1,0:T(8,128)(2,1)} reduce(bf16[2,2,128,3584]{3,2,1,0:T(8,128)(2,1)} %all_to_all.41, bf16[]{:T(256)} %constant.31.clone.1), dimensions={0}, to_apply=%region_12.13 | reduce | flops 917504 | bytes 5505026 | tf_op jit(solution)/shard_map/reduce_sum | solution.py:237
  250.1 15.4 %all-to-all-done.1 = bf16[2,128,3584]{2,1,0:T(8,128)(2,1)S(1)} async-done(((bf16[2,128,3584]{2,1,0:T(8,128)(2,1)}), bf16[2,128,3584]{2,1,0:T(8,128)(2,1)S(1)}, u32[]{:S(2)}, u32[]{:S(2)}) %all-to-all-start.1) | async-done | bytes 1835040 | tf_op jit(solution)/shard_map/all_to_all | solution.py:238
  265.6 1.2 copy-done.4
  266.8 3.9 all-to-all-start.5
  270.7 1.4 slice.39
  272.1 0.9 copy.31
  274.4 5.2 %fusion.63 = f32[3584,256]{1,0:T(8,128)} fusion(bf16[512,3584]{1,0:T(8,128)(2,1)} %bitcast.137, bf16[512,256]{1,0:T(8,128)(2,1)S(1)} %fusion.27), kind=kOutput, calls=%fused_computation.83 | convolution fusion | flops 939524096 | bytes 7602176 | tf_op jit(solution)/shard_map/rd,rf->df/dot_general | solution.py:258
  279.6 3.0 fusion.46
  282.6 1.1 reduce_sum.169
  283.8 1.0 reshape.179.refs_1_
  284.8 1.1 reduce_sum.165
  285.9 1.0 reshape.169.refs_1_
  286.9 3.0 reduce_sum.163
  289.9 31.6 %shard_map.121 = (bf16[8,16,3584]{2,1,0:T(8,128)(2,1)}, bf16[8,112,128]{2,1,0:T(8,128)(2,1)}) custom-call(bf16[8,16,3584]{2,1,0:T(8,128)(2,1)} %bitcast.141, bf16[8,112,128]{2,1,0:T(8,128)(2,1)} %reshape.169.refs_1_), custom_call_target="tpu_custom_call" | custom-call | tf_op jit(solution)/shard_map/pallas_call | solution.py:223
  321.4 1.2 reshape.171
  322.7 1.8 convolution_bitcast_fusion.1
  324.4 1.4 fusion.7
  325.8 4.1 collective-permute-start
  329.9 1.5 reduce_sum.167
  331.4 47.7 %shard_map.122 = (bf16[8,16,3584]{2,1,0:T(8,128)(2,1)}, bf16[8,112,128]{2,1,0:T(8,128)(2,1)}) custom-call(bf16[8,16,3584]{2,1,0:T(8,128)(2,1)} %bitcast.140, bf16[8,112,128]{2,1,0:T(8,128)(2,1)} %reshape.179.refs_1_), custom_call_target="tpu_custom_call" | custom-call | tf_op jit(solution)/shard_map/pallas_call | solution.py:223
  379.1 1.8 convolution_bitcast_fusion
  381.8 5.2 %collective-permute-start.1 = (bf16[1,64,3584]{2,1,0:T(8,128)(2,1)S(1)}, bf16[1,64,3584]{2,1,0:T(8,128)(2,1)S(1)}, u32[]{:S(2)}, u32[]{:S(2)}) collective-permute-start(bf16[1,64,3584]{2,1,0:T(8,128)(2,1)S(1)} %fusion.6), channel_id=1, source_target_pairs={{0,224},{32,0},{64,32},{96,64},{128,96},{160,128},{192,160},{224,1... | collective-permute-start | bytes 1376264 | tf_op jit(solution)/shard_map/ppermute | solution.py:18
  387.0 4.7 %fusion = f32[1,1,3584,256]{3,2,1,0:T(8,128)} fusion(f32[3584,256]{1,0:T(8,128)} %fusion.63, bf16[128,3584]{1,0:T(8,128)(2,1)S(1)} %reshape.177, bf16[128,256]{1,0:T(8,128)(2,1)S(1)} %copy-done.22), kind=kOutput, calls=%fused_computation.4 | convolution fusion | flops 235798528 | bytes 8323072 | tf_op jit(solution)/shard_map/rd,rf->df/dot_general | solution.py:258
  391.7 2.5 fusion.1
  394.3 13.0 %collective-permute-done.1 = bf16[1,64,3584]{2,1,0:T(8,128)(2,1)S(1)} collective-permute-done((bf16[1,64,3584]{2,1,0:T(8,128)(2,1)S(1)}, bf16[1,64,3584]{2,1,0:T(8,128)(2,1)S(1)}, u32[]{:S(2)}, u32[]{:S(2)}) %collective-permute-start.1) | collective-permute-done | bytes 458784 | tf_op jit(solution)/shard_map/ppermute | solution.py:18
  407.3 0.8 copy.39
  408.0 0.8 copy.40
  (86 shorter events, 11.9 us)
Async XLA Ops:
  0.6 160.0 %copy-start = (bf16[1,1,3584,256]{3,2,1,0:T(8,128)(2,1)S(1)}, bf16[1,1,3584,256]{3,2,1,0:T(8,128)(2,1)}, u32[]{:S(2)}) copy-start(bf16[1,1,3584,256]{3,2,1,0:T(8,128)(2,1)} %param.16) | copy-start | bytes 5505028
  0.6 11.2 %copy-start.6 = (bf16[1,64,3584]{2,1,0:T(8,128)(2,1)S(1)}, bf16[1,64,3584]{2,1,0:T(8,128)(2,1)}, u32[]{:S(2)}) copy-start(bf16[1,64,3584]{2,1,0:T(8,128)(2,1)} %param.15) | copy-start | bytes 1376260
  0.7 13.3 %copy-start.13 = (bf16[1,64,3584]{2,1,0:T(8,128)(2,1)S(1)}, bf16[1,64,3584]{2,1,0:T(8,128)(2,1)}, u32[]{:S(2)}) copy-start(bf16[1,64,3584]{2,1,0:T(8,128)(2,1)} %param.12) | copy-start | bytes 1376260
  4.7 11.2 %copy-start.24 = (bf16[64,8,20]{0,2,1:T(8,128)(2,1)}, bf16[64,8,20]{0,2,1:T(8,128)(2,1)S(1)}, u32[]{:S(2)}) copy-start(bf16[64,8,20]{0,2,1:T(8,128)(2,1)S(1)} %reshape.182) | copy-start | bytes 61444
  6.2 9.7 %copy-start.5 = (bf16[1,64,3584]{2,1,0:T(8,128)(2,1)S(1)}, bf16[1,64,3584]{2,1,0:T(8,128)(2,1)}, u32[]{:S(2)}) copy-start(bf16[1,64,3584]{2,1,0:T(8,128)(2,1)} %param.9) | copy-start | bytes 1376260
  10.6 1.2 copy-start.18
  15.8 5.8 %slice-start = ((bf16[64,8,20]{0,2,1:T(8,128)(2,1)}), bf16[64,8,16]{0,2,1:T(8,128)(2,1)S(1)}, s32[]{:S(2)}) async-start(bf16[64,8,20]{0,2,1:T(8,128)(2,1)} %copy-done.24), calls=%async_computation.8 | async-start | bytes 65536 | tf_op jit(solution)/shard_map/slice | solution.py:173
  160.7 1.2 copy-start.8
  160.7 1.8 copy-start.14
  162.5 3.1 copy-start.16
  163.2 0.6 copy-start.21
  165.5 30.5 %all-to-all-start.6 = ((bf16[2,2,32,3584]{3,2,1,0:T(8,128)(2,1)}), bf16[2,2,32,3584]{3,2,1,0:T(8,128)(2,1)}, u32[]{:S(2)}, u32[]{:S(2)}) async-start(bf16[2,2,32,3584]{3,2,1,0:T(8,128)(2,1)} %bitcast.139), calls=%async_computation.6 | async-start | bytes 1835008 | tf_op jit(solution)/shard_map/all_to_all | solution.py:236
  196.0 9.4 %all-to-all-start = ((bf16[2,2,128,3584]{3,2,1,0:T(8,128)(2,1)}), bf16[2,2,128,3584]{3,2,1,0:T(8,128)(2,1)}, u32[]{:S(2)}, u32[]{:S(2)}) async-start(bf16[2,2,128,3584]{3,2,1,0:T(8,128)(2,1)} %bitcast.138), calls=%async_computation | async-start | bytes 7340032 | tf_op jit(solution)/shard_map/all_to_all | solution.py:236
  201.6 3.8 copy-start.10
  221.1 10.5 %all-to-all-start.7 = ((bf16[2,32,3584]{2,1,0:T(8,128)(2,1)}), bf16[2,32,3584]{2,1,0:T(8,128)(2,1)S(1)}, u32[]{:S(2)}, u32[]{:S(2)}) async-start(bf16[2,32,3584]{2,1,0:T(8,128)(2,1)} %reduce_sum.168), calls=%async_computation.7 | async-start | bytes 917504 | tf_op jit(solution)/shard_map/all_to_all | solution.py:238
  231.6 7.9 %copy-start.11 = (bf16[2,32,3584]{2,1,0:T(8,128)(2,1)}, bf16[2,32,3584]{2,1,0:T(8,128)(2,1)S(1)}, u32[]{:S(2)}) copy-start(bf16[2,32,3584]{2,1,0:T(8,128)(2,1)S(1)} %all-to-all-done.7) | copy-start | bytes 1376260
  231.6 9.6 %all-to-all-start.3 = ((bf16[2,32,3584]{2,1,0:T(8,128)(2,1)}), bf16[2,32,3584]{2,1,0:T(8,128)(2,1)S(1)}, u32[]{:S(2)}, u32[]{:S(2)}) async-start(bf16[2,32,3584]{2,1,0:T(8,128)(2,1)} %reduce_sum.164), calls=%async_computation.3 | async-start | bytes 917504 | tf_op jit(solution)/shard_map/all_to_all | solution.py:238
  241.1 0.8 copy-start.12
  241.9 23.6 %all-to-all-start.1 = ((bf16[2,128,3584]{2,1,0:T(8,128)(2,1)}), bf16[2,128,3584]{2,1,0:T(8,128)(2,1)S(1)}, u32[]{:S(2)}, u32[]{:S(2)}) async-start(bf16[2,128,3584]{2,1,0:T(8,128)(2,1)} %reduce_sum.162), calls=%async_computation.1 | async-start | bytes 3670016 | tf_op jit(solution)/shard_map/all_to_all | solution.py:238
  265.5 1.2 copy-start.4
  266.8 63.1 %all-to-all-start.5 = ((bf16[2,128,3584]{2,1,0:T(8,128)(2,1)}), bf16[2,128,3584]{2,1,0:T(8,128)(2,1)S(1)}, u32[]{:S(2)}, u32[]{:S(2)}) async-start(bf16[2,128,3584]{2,1,0:T(8,128)(2,1)} %reduce_sum.166), calls=%async_computation.5 | async-start | bytes 3670016 | tf_op jit(solution)/shard_map/all_to_all | solution.py:238
  274.4 5.2 %copy-start.3 = (bf16[2,2,8,16,3584]{4,3,2,1,0:T(8,128)(2,1)S(1)}, bf16[2,2,8,16,3584]{4,3,2,1,0:T(8,128)(2,1)}, u32[]{:S(2)}) copy-start(bf16[2,2,8,16,3584]{4,3,2,1,0:T(8,128)(2,1)} %get-tuple-element.18) | copy-start | bytes 11010052
  274.4 5.2 %copy-start.15 = (f32[512,256]{1,0:T(8,128)S(1)}, f32[512,256]{1,0:T(8,128)}, u32[]{:S(2)}) copy-start(f32[512,256]{1,0:T(8,128)} %fusion.18) | copy-start | bytes 1572868
  286.9 35.8 %copy-start.20 = (f32[64,8,20]{0,2,1:T(8,128)S(1)}, f32[64,8,20]{0,2,1:T(8,128)}, u32[]{:S(2)}) copy-start(f32[64,8,20]{0,2,1:T(8,128)} %reshape.152) | copy-start | bytes 122884
  325.8 53.3 %copy-start.19 = (f32[64,8,20]{0,2,1:T(8,128)S(1)}, f32[64,8,20]{0,2,1:T(8,128)}, u32[]{:S(2)}) copy-start(f32[64,8,20]{0,2,1:T(8,128)} %copy-done.18) | copy-start | bytes 122884
  325.8 68.4 %collective-permute-start = (bf16[1,64,3584]{2,1,0:T(8,128)(2,1)}, bf16[1,64,3584]{2,1,0:T(8,128)(2,1)S(1)}, u32[]{:S(2)}, u32[]{:S(2)}) collective-permute-start(bf16[1,64,3584]{2,1,0:T(8,128)(2,1)} %fusion.7), channel_id=1, source_target_pairs={{0,32},{32,64},{64,96},{96,128},{128,160},{160,192},{192,224},{224... | collective-permute-start | bytes 1376264 | tf_op jit(solution)/shard_map/ppermute | solution.py:18
  331.4 49.8 %copy-start.7 = (bf16[1,64,3584]{2,1,0:T(8,128)(2,1)S(1)}, bf16[1,64,3584]{2,1,0:T(8,128)(2,1)}, u32[]{:S(2)}) copy-start(bf16[1,64,3584]{2,1,0:T(8,128)(2,1)} %param.15) | copy-start | bytes 1376260
  331.4 49.8 %copy-start.25 = (f32[64,8,4]{0,2,1:T(4,128)S(1)}, f32[64,8,4]{0,2,1:T(4,128)}, u32[]{:S(2)}) copy-start(f32[64,8,4]{0,2,1:T(4,128)} %slice.39) | copy-start | bytes 24580
  379.1 1.8 copy-start.23
  379.1 7.9 %copy-start.22 = (bf16[128,256]{1,0:T(8,128)(2,1)S(1)}, bf16[128,256]{1,0:T(8,128)(2,1)}, u32[]{:S(2)}) copy-start(bf16[128,256]{1,0:T(8,128)(2,1)} %copy-done.21) | copy-start | bytes 196612
  381.8 9.9 %copy-start.9 = (bf16[128,3584]{1,0:T(8,128)(2,1)S(1)}, bf16[128,3584]{1,0:T(8,128)(2,1)}, u32[]{:S(2)}) copy-start(bf16[128,3584]{1,0:T(8,128)(2,1)} %reshape.176) | copy-start | bytes 2752516
  381.8 9.9 %copy-start.17 = (f32[128,256]{1,0:T(8,128)S(1)}, f32[128,256]{1,0:T(8,128)}, u32[]{:S(2)}) copy-start(f32[128,256]{1,0:T(8,128)} %copy-done.16) | copy-start | bytes 393220
  381.8 25.4 %collective-permute-start.1 = (bf16[1,64,3584]{2,1,0:T(8,128)(2,1)S(1)}, bf16[1,64,3584]{2,1,0:T(8,128)(2,1)S(1)}, u32[]{:S(2)}, u32[]{:S(2)}) collective-permute-start(bf16[1,64,3584]{2,1,0:T(8,128)(2,1)S(1)} %fusion.6), channel_id=1, source_target_pairs={{0,224},{32,0},{64,32},{96,64},{128,96},{160,128},{192,160},{224,1... | collective-permute-start | bytes 1376264 | tf_op jit(solution)/shard_map/ppermute | solution.py:18
  387.0 4.7 %copy-start.2 = (f32[256,3584]{1,0:T(8,128)S(1)}, f32[256,3584]{1,0:T(8,128)}, u32[]{:S(2)}) copy-start(f32[256,3584]{1,0:T(8,128)} %fusion.46) | copy-start | bytes 11010052
  391.7 17.1 %copy-start.1 = (bf16[1,1,3584,256]{3,2,1,0:T(8,128)(2,1)S(1)}, bf16[1,1,3584,256]{3,2,1,0:T(8,128)(2,1)}, u32[]{:S(2)}) copy-start(bf16[1,1,3584,256]{3,2,1,0:T(8,128)(2,1)} %param.16) | copy-start | bytes 5505028

commit v9 on v8

--- a/solution.py
+++ b/solution.py
@@ -293,18 +293,22 @@
             wires.append([to_wire(rows, experts) for rows in (rows_f, rows_x, rows_g)])
     got = dispatch(wires[0] + wires[1])
     got = [got[:3], got[3:]]
-    summed_f = []
-    summed_b = []
     grad_up = 0.0
     grad_down = 0.0
+    parts_f = []
+    parts_b = []
     for index in range(2):
         got_f, got_x, got_g = [block.reshape(-1, model_width) for block in got[index]]
-        part = expert_forward(got_f, up_proj, down_proj)
-        summed_f.append(group_sum(part))
+        parts_f.append(expert_forward(got_f, up_proj, down_proj).reshape(2, 2, -1, model_width))
         dpart, more_up, more_down = expert_backward(got_x, got_g, up_proj, down_proj)
         grad_up = grad_up + more_up
         grad_down = grad_down + more_down
-        summed_b.append(group_sum(dpart))
+        parts_b.append(dpart.reshape(2, 2, -1, model_width))
+    cut = experts * main
+    whole_f = group_sum(jnp.concatenate(parts_f, axis=2))
+    whole_b = group_sum(jnp.concatenate(parts_b, axis=2))
+    summed_f = [whole_f[:cut], whole_f[cut:]]
+    summed_b = [whole_b[:cut], whole_b[cut:]]
 
     def home(summed, tag):
         shaped = [summed[0].reshape(experts, main, model_width), to_wire(summed[1], experts)]

time: 411 us -> 396 us (0.964)
  blocking collectives: 15.7 us -> 0 us
  waiting for transfers between devices: 37.6 us -> 47.8 us
    all_to_all x2 -> x0, blocking collectives: 15.7 us -> none  [group_sum(): mine = lax.all_to_all(blocks, 'ec', split_axis=0, concat_axis=0, tiled=True)]
    all_to_all x4 -> x2, waiting for transfers between devices: 23.1 us -> 35 us  [group_sum(): other = lax.all_to_all(pair, 'ez', split_axis=0, concat_axis=0, tiled=True)]
    concatenate x0 -> x2, other arithmetic: none -> 7 us  [the longest x1 4.51 us: local(): whole_f = group_sum(jnp.concatenate(parts_f, axis=2))]
    all_to_all x4 -> x2, starting transfers between devices: 14.6 us -> 9.99 us  [group_sum(): other = lax.all_to_all(pair, 'ez', split_axis=0, concat_axis=0, tiled=True)]
    reduce_sum x4 -> x2, other arithmetic: 12.2 us -> 10.2 us  [group_sum(): pair = jnp.sum(mine.astype(jnp.float32), axis=0).astype(jnp.bfloat16)]
  transfers between devices with their start and end apart: 8 -> 6, of which waited for: 5 -> 3; matrix products, arithmetic and copies ran while one was open for 18% -> 13% of each run, Pallas kernels for 19% -> 12%
where the time goes in v9:
time: 396 us; the launch traced here: 395 us
  Pallas kernels  211 us (53%)
  matrix products  51.4 us (13%)
  waiting for transfers between devices  47.8 us (12%)
  starting transfers between devices  31.3 us (8%)
  other arithmetic  26.6 us (7%)
  local copies, waits for them, and re-layouts  26 us (7%)
    pallas_call x1, Pallas kernels, dispatch(): pl.pallas_call(functools.partial(dispatch_kernel, groups), out_shape=[jax...  133 us
    pallas_call x2, Pallas kernels, send_home(): pl.pallas_call(functools.partial(return_kernel, groups), out_shape=[jax.S...  78.4 us
    all_to_all x2, waiting for transfers between devices, group_sum(): other = lax.all_to_all(pair, 'ez', split_axis=0, concat_axis=0, tiled=True)  35 us
    ppermute x2, waiting for transfers between devices, passed_along(): return lax.ppermute(value, axis, pairs)  12.8 us
    all_to_all x2, starting transfers between devices, group_sum(): mine = lax.all_to_all(blocks, 'ec', split_axis=0, concat_axis=0, tiled=True)  11.8 us
    dot_general x2, matrix products, expert_forward(): jnp.einsum('...f,fd->...d', act, down_proj, preferred_element_type=jnp.fl...  11.4 us
    reduce_sum x2, other arithmetic, group_sum(): pair = jnp.sum(mine.astype(jnp.float32), axis=0).astype(jnp.bfloat16)  10.2 us
    all_to_all x2, starting transfers between devices, group_sum(): other = lax.all_to_all(pair, 'ez', split_axis=0, concat_axis=0, tiled=True)  9.99 us
  transfers between devices with their start and end apart: 6, of which 3 were waited for; matrix products, arithmetic and copies ran while one was open for 13% of the time, Pallas kernels for 12%

profile of v9, /device:TPU:1, one launch (start us, length us, event | category | flops | bytes accessed | tf_op | source)
XLA Modules:
  0.0 395.3 jit_solution(15337685346844795955)
XLA Ops:
  0.7 0.9 copy.29
  2.4 0.7 bitcast_add_fusion.1
  3.1 1.4 select_reduce_fusion.1
  5.3 0.8 copy.33
  6.9 0.7 bitcast_add_fusion
  7.6 1.4 select_reduce_fusion
  9.1 0.9 copy.35
  10.1 0.6 slice.69
  10.7 0.6 slice.68
  11.3 1.3 convolution_convert_fusion.7
  12.7 1.0 reshape.163.refs_5_
  13.7 1.2 convolution_convert_fusion.8
  14.9 1.0 reshape.161.refs_4_
  15.9 0.9 convolution_convert_fusion.9
  16.8 1.0 reshape.160.refs_3_
  17.8 1.8 convolution_convert_fusion.4
  19.6 2.1 convolution_convert_fusion.5
  21.7 1.3 convolution_convert_fusion.6
  23.0 132.7 %shard_map.120 = (bf16[2,2,8,16,3584]{4,3,2,1,0:T(8,128)(2,1)}, bf16[2,2,8,16,3584]{4,3,2,1,0:T(8,128)(2,1)}, bf16[2,2,8,16,3584]{4,3,2,1,0:T(8,128)(2,1)}, bf16...) custom-call(bf16[8,16,3584]{2,1,0:T(8,128)(2,1)} %bitcast.145, ...), custom_call_target="tpu_custom_call" | custom-call | tf_op jit(solution)/shard_map/pallas_call | solution.py:150
  155.7 2.9 reshape.166
  158.6 8.4 %convolution_convert_fusion.1 = bf16[512,3584]{1,0:T(8,128)(2,1)} fusion(bf16[1,1,256,3584]{3,2,1,0:T(8,128)(2,1)} %param.17, bf16[512,3584]{1,0:T(8,128)(2,1)} %bitcast.156, bf16[1,1,3584,256]{3,2,1,0:T(8,128)(2,1)S(1)} %copy-done), kind=kOutput, calls=%fused_computation.1 | convolution fusion | flops 1881538560 | bytes 11010048 | tf_op jit(solution)/shard_map/...f,fd->...d/dot_general | solution.py:245
  167.0 3.0 convolution_convert_fusion.3
  170.0 4.5 %pad_maximum_fusion = bf16[2,2,160,3584]{3,2,1,0:T(8,128)(2,1)} fusion(bf16[2,2,32,3584]{3,2,1,0:T(8,128)(2,1)S(1)} %bitcast.139, bf16[2,2,128,3584]{3,2,1,0:T(8,128)(2,1)} %bitcast.140), kind=kLoop, calls=%fused_computation.19 | loop fusion | flops 9175040 | bytes 9175040 | tf_op jit(solution)/shard_map/concatenate | solution.py:308
  174.5 5.9 %all-to-all-start = ((bf16[2,2,160,3584]{3,2,1,0:T(8,128)(2,1)}), bf16[2,2,160,3584]{3,2,1,0:T(8,128)(2,1)}, u32[]{:S(2)}, u32[]{:S(2)}) async-start(bf16[2,2,160,3584]{3,2,1,0:T(8,128)(2,1)} %pad_maximum_fusion), calls=%async_computation | async-start | bytes 9175040 | tf_op jit(solution)/shard_map/all_to_all | solution.py:236
  180.4 4.1 %fusion.18 = f32[512,256]{1,0:T(8,128)} fusion(bf16[512,3584]{1,0:T(8,128)(2,1)} %bitcast.136, bf16[1,1,3584,256]{3,2,1,0:T(8,128)(2,1)S(1)} %copy-done), kind=kOutput, calls=%fused_computation.36 | convolution fusion | flops 939524096 | bytes 6029312 | tf_op jit(solution)/shard_map/...d,df->...f/dot_general | solution.py:251
  184.4 2.0 reshape.175
  186.4 2.1 reshape.176
  189.0 0.7 copy-done.15
  189.6 3.1 fusion.33
  192.7 0.7 convolution_convert_fusion.2
  193.5 1.2 fusion.27
  194.6 1.1 convolution_convert_fusion
  195.8 2.5 pad_maximum_fusion.1
  198.3 5.9 %all-to-all-start.2 = ((bf16[2,2,160,3584]{3,2,1,0:T(8,128)(2,1)}), bf16[2,2,160,3584]{3,2,1,0:T(8,128)(2,1)}, u32[]{:S(2)}, u32[]{:S(2)}) async-start(bf16[2,2,160,3584]{3,2,1,0:T(8,128)(2,1)} %pad_maximum_fusion.1), calls=%async_computation.2 | async-start | bytes 9175040 | tf_op jit(solution)/shard_map/all_to_all | solution.py:236
  204.2 5.1 %reduce_sum.114 = bf16[2,160,3584]{2,1,0:T(8,128)(2,1)} reduce(bf16[2,2,160,3584]{3,2,1,0:T(8,128)(2,1)} %all-to-all-done, bf16[]{:T(256)} %constant.27.clone.1), dimensions={0}, to_apply=%region_8.9 | reduce | flops 1146880 | bytes 6881282 | tf_op jit(solution)/shard_map/reduce_sum | solution.py:237
  209.4 4.9 %all-to-all-start.1 = ((bf16[2,160,3584]{2,1,0:T(8,128)(2,1)}), bf16[2,160,3584]{2,1,0:T(8,128)(2,1)}, u32[]{:S(2)}, u32[]{:S(2)}) async-start(bf16[2,160,3584]{2,1,0:T(8,128)(2,1)} %reduce_sum.114), calls=%async_computation.1 | async-start | bytes 4587520 | tf_op jit(solution)/shard_map/all_to_all | solution.py:238
  214.2 5.1 %reduce_sum.116 = bf16[2,160,3584]{2,1,0:T(8,128)(2,1)} reduce(bf16[2,2,160,3584]{3,2,1,0:T(8,128)(2,1)} %all-to-all-done.2, bf16[]{:T(256)} %constant.27.clone.1), dimensions={0}, to_apply=%region_10.11 | reduce | flops 1146880 | bytes 6881282 | tf_op jit(solution)/shard_map/reduce_sum | solution.py:237
  219.4 22.1 %all-to-all-done.1 = bf16[2,160,3584]{2,1,0:T(8,128)(2,1)} async-done(((bf16[2,160,3584]{2,1,0:T(8,128)(2,1)}), bf16[2,160,3584]{2,1,0:T(8,128)(2,1)}, u32[]{:S(2)}, u32[]{:S(2)}) %all-to-all-start.1) | async-done | bytes 2293792 | tf_op jit(solution)/shard_map/all_to_all | solution.py:238
  241.4 5.1 %all-to-all-start.3 = ((bf16[2,160,3584]{2,1,0:T(8,128)(2,1)}), bf16[2,160,3584]{2,1,0:T(8,128)(2,1)}, u32[]{:S(2)}, u32[]{:S(2)}) async-start(bf16[2,160,3584]{2,1,0:T(8,128)(2,1)} %reduce_sum.116), calls=%async_computation.3 | async-start | bytes 4587520 | tf_op jit(solution)/shard_map/all_to_all | solution.py:238
  246.5 0.8 slice.55
  247.4 0.6 slice.59
  248.0 5.2 %fusion.63 = f32[3584,256]{1,0:T(8,128)} fusion(bf16[512,3584]{1,0:T(8,128)(2,1)} %bitcast.137, bf16[512,256]{1,0:T(8,128)(2,1)S(1)} %fusion.27), kind=kOutput, calls=%fused_computation.85 | convolution fusion | flops 939524096 | bytes 7602176 | tf_op jit(solution)/shard_map/rd,rf->df/dot_general | solution.py:258
  253.2 3.0 fusion.46
  256.2 2.1 reduce_sum.115
  258.4 1.1 slice.57
  259.7 12.9 %all-to-all-done.3 = bf16[2,160,3584]{2,1,0:T(8,128)(2,1)} async-done(((bf16[2,160,3584]{2,1,0:T(8,128)(2,1)}), bf16[2,160,3584]{2,1,0:T(8,128)(2,1)}, u32[]{:S(2)}, u32[]{:S(2)}) %all-to-all-start.3) | async-done | bytes 2293792 | tf_op jit(solution)/shard_map/all_to_all | solution.py:238
  272.6 2.2 reduce_sum.117
  274.8 1.0 slice.60
  275.8 1.0 reshape.169.refs_1_
  276.8 32.4 %shard_map.121 = (bf16[8,16,3584]{2,1,0:T(8,128)(2,1)}, bf16[8,112,128]{2,1,0:T(8,128)(2,1)}) custom-call(bf16[8,16,3584]{2,1,0:T(8,128)(2,1)} %bitcast.142, bf16[8,112,128]{2,1,0:T(8,128)(2,1)} %reshape.169.refs_1_), custom_call_target="tpu_custom_call" | custom-call | tf_op jit(solution)/shard_map/pallas_call | solution.py:223
  309.3 1.8 convolution_bitcast_fusion.1
  311.0 1.3 reshape.171
  312.3 1.4 fusion.7
  313.7 4.1 %collective-permute-start = (bf16[1,64,3584]{2,1,0:T(8,128)(2,1)}, bf16[1,64,3584]{2,1,0:T(8,128)(2,1)S(1)}, u32[]{:S(2)}, u32[]{:S(2)}) collective-permute-start(bf16[1,64,3584]{2,1,0:T(8,128)(2,1)} %fusion.7), channel_id=1, source_target_pairs={{0,32},{32,64},{64,96},{96,128},{128,160},{160,192},{192,224},{224... | collective-permute-start | bytes 1376264 | tf_op jit(solution)/shard_map/ppermute | solution.py:18
  317.8 1.0 reshape.179.refs_1_
  318.8 46.0 %shard_map.122 = (bf16[8,16,3584]{2,1,0:T(8,128)(2,1)}, bf16[8,112,128]{2,1,0:T(8,128)(2,1)}) custom-call(bf16[8,16,3584]{2,1,0:T(8,128)(2,1)} %bitcast.141, bf16[8,112,128]{2,1,0:T(8,128)(2,1)} %reshape.179.refs_1_), custom_call_target="tpu_custom_call" | custom-call | tf_op jit(solution)/shard_map/pallas_call | solution.py:223
  364.8 1.8 convolution_bitcast_fusion
  366.5 1.2 reshape.181
  368.4 5.4 %collective-permute-start.1 = (bf16[1,64,3584]{2,1,0:T(8,128)(2,1)S(1)}, bf16[1,64,3584]{2,1,0:T(8,128)(2,1)S(1)}, u32[]{:S(2)}, u32[]{:S(2)}) collective-permute-start(bf16[1,64,3584]{2,1,0:T(8,128)(2,1)S(1)} %fusion.6), channel_id=1, source_target_pairs={{0,224},{32,0},{64,32},{96,64},{128,96},{160,128},{192,160},{224,1... | collective-permute-start | bytes 1376264 | tf_op jit(solution)/shard_map/ppermute | solution.py:18
  373.8 4.7 %fusion = f32[1,1,3584,256]{3,2,1,0:T(8,128)} fusion(f32[3584,256]{1,0:T(8,128)} %fusion.63, bf16[128,3584]{1,0:T(8,128)(2,1)S(1)} %reshape.176, bf16[128,256]{1,0:T(8,128)(2,1)S(1)} %fusion.33), kind=kOutput, calls=%fused_computation.4 | convolution fusion | flops 235798528 | bytes 8323072 | tf_op jit(solution)/shard_map/rd,rf->df/dot_general | solution.py:258
  378.5 2.5 fusion.1
  381.0 12.8 %collective-permute-done.1 = bf16[1,64,3584]{2,1,0:T(8,128)(2,1)S(1)} collective-permute-done((bf16[1,64,3584]{2,1,0:T(8,128)(2,1)S(1)}, bf16[1,64,3584]{2,1,0:T(8,128)(2,1)S(1)}, u32[]{:S(2)}, u32[]{:S(2)}) %collective-permute-start.1) | collective-permute-done | bytes 458784 | tf_op jit(solution)/shard_map/ppermute | solution.py:18
  393.8 0.8 copy.39
  394.5 0.8 copy.40
  (72 shorter events, 3.9 us)
Async XLA Ops:
  0.6 157.9 %copy-start = (bf16[1,1,3584,256]{3,2,1,0:T(8,128)(2,1)S(1)}, bf16[1,1,3584,256]{3,2,1,0:T(8,128)(2,1)}, u32[]{:S(2)}) copy-start(bf16[1,1,3584,256]{3,2,1,0:T(8,128)(2,1)} %param.16) | copy-start | bytes 5505028
  0.6 17.2 %copy-start.7 = (bf16[1,64,3584]{2,1,0:T(8,128)(2,1)S(1)}, bf16[1,64,3584]{2,1,0:T(8,128)(2,1)}, u32[]{:S(2)}) copy-start(bf16[1,64,3584]{2,1,0:T(8,128)(2,1)} %param.15) | copy-start | bytes 1376260
  0.7 19.0 %copy-start.10 = (bf16[1,64,3584]{2,1,0:T(8,128)(2,1)S(1)}, bf16[1,64,3584]{2,1,0:T(8,128)(2,1)}, u32[]{:S(2)}) copy-start(bf16[1,64,3584]{2,1,0:T(8,128)(2,1)} %param.12) | copy-start | bytes 1376260
  0.7 15.3 %copy-start.6 = (bf16[1,64,3584]{2,1,0:T(8,128)(2,1)S(1)}, bf16[1,64,3584]{2,1,0:T(8,128)(2,1)}, u32[]{:S(2)}) copy-start(bf16[1,64,3584]{2,1,0:T(8,128)(2,1)} %param.9) | copy-start | bytes 1376260
  10.1 1.3 copy-start.17
  174.5 23.8 %all-to-all-start = ((bf16[2,2,160,3584]{3,2,1,0:T(8,128)(2,1)}), bf16[2,2,160,3584]{3,2,1,0:T(8,128)(2,1)}, u32[]{:S(2)}, u32[]{:S(2)}) async-start(bf16[2,2,160,3584]{3,2,1,0:T(8,128)(2,1)} %pad_maximum_fusion), calls=%async_computation | async-start | bytes 9175040 | tf_op jit(solution)/shard_map/all_to_all | solution.py:236
  180.3 4.1 %copy-start.14 = (bf16[2,2,8,112,128]{4,3,2,1,0:T(8,128)(2,1)S(1)}, bf16[2,2,8,112,128]{4,3,2,1,0:T(8,128)(2,1)}, u32[]{:S(2)}) copy-start(bf16[2,2,8,112,128]{4,3,2,1,0:T(8,128)(2,1)} %get-tuple-element.20) | copy-start | bytes 2752516
  188.5 4.9 %copy-start.3 = (bf16[2,2,8,16,3584]{4,3,2,1,0:T(8,128)(2,1)S(1)}, bf16[2,2,8,16,3584]{4,3,2,1,0:T(8,128)(2,1)}, u32[]{:S(2)}) copy-start(bf16[2,2,8,16,3584]{4,3,2,1,0:T(8,128)(2,1)} %get-tuple-element.18) | copy-start | bytes 11010052
  188.5 4.9 %copy-start.11 = (bf16[1,1,256,3584]{3,2,1,0:T(8,128)(2,1)S(1)}, bf16[1,1,256,3584]{3,2,1,0:T(8,128)(2,1)}, u32[]{:S(2)}) copy-start(bf16[1,1,256,3584]{3,2,1,0:T(8,128)(2,1)} %param.17) | copy-start | bytes 5505028
  188.5 4.9 %copy-start.12 = (f32[512,256]{1,0:T(8,128)S(1)}, f32[512,256]{1,0:T(8,128)}, u32[]{:S(2)}) copy-start(f32[512,256]{1,0:T(8,128)} %fusion.18) | copy-start | bytes 1572868
  189.0 0.7 copy-start.15
  198.3 11.1 %all-to-all-start.2 = ((bf16[2,2,160,3584]{3,2,1,0:T(8,128)(2,1)}), bf16[2,2,160,3584]{3,2,1,0:T(8,128)(2,1)}, u32[]{:S(2)}, u32[]{:S(2)}) async-start(bf16[2,2,160,3584]{3,2,1,0:T(8,128)(2,1)} %pad_maximum_fusion.1), calls=%async_computation.2 | async-start | bytes 9175040 | tf_op jit(solution)/shard_map/all_to_all | solution.py:236
  209.4 32.0 %all-to-all-start.1 = ((bf16[2,160,3584]{2,1,0:T(8,128)(2,1)}), bf16[2,160,3584]{2,1,0:T(8,128)(2,1)}, u32[]{:S(2)}, u32[]{:S(2)}) async-start(bf16[2,160,3584]{2,1,0:T(8,128)(2,1)} %reduce_sum.114), calls=%async_computation.1 | async-start | bytes 4587520 | tf_op jit(solution)/shard_map/all_to_all | solution.py:238
  219.4 28.0 %copy-start.19 = (f32[64,160]{1,0:T(8,128)S(1)}, f32[64,160]{1,0:T(8,128)}, u32[]{:S(2)}) copy-start(f32[64,160]{1,0:T(8,128)} %get-tuple-element.24) | copy-start | bytes 122884
  241.4 31.2 %all-to-all-start.3 = ((bf16[2,160,3584]{2,1,0:T(8,128)(2,1)}), bf16[2,160,3584]{2,1,0:T(8,128)(2,1)}, u32[]{:S(2)}, u32[]{:S(2)}) async-start(bf16[2,160,3584]{2,1,0:T(8,128)(2,1)} %reduce_sum.116), calls=%async_computation.3 | async-start | bytes 4587520 | tf_op jit(solution)/shard_map/all_to_all | solution.py:238
  248.0 5.2 %copy-start.4 = (bf16[2,2,8,16,3584]{4,3,2,1,0:T(8,128)(2,1)S(1)}, bf16[2,2,8,16,3584]{4,3,2,1,0:T(8,128)(2,1)}, u32[]{:S(2)}) copy-start(bf16[2,2,8,16,3584]{4,3,2,1,0:T(8,128)(2,1)} %get-tuple-element.18) | copy-start | bytes 11010052
  248.0 5.2 %copy-start.13 = (f32[512,256]{1,0:T(8,128)S(1)}, f32[512,256]{1,0:T(8,128)}, u32[]{:S(2)}) copy-start(f32[512,256]{1,0:T(8,128)} %fusion.18) | copy-start | bytes 1572868
  258.4 1.3 copy-start.5
  272.6 3.2 slice-start
  274.8 37.5 %copy-start.20 = (f32[64,8,4]{0,2,1:T(4,128)S(1)}, f32[64,8,4]{0,2,1:T(4,128)}, u32[]{:S(2)}) copy-start(f32[64,8,4]{0,2,1:T(4,128)} %slice.59) | copy-start | bytes 24580
  276.8 88.0 %copy-start.18 = (f32[64,8,20]{0,2,1:T(8,128)S(1)}, f32[64,8,20]{0,2,1:T(8,128)}, u32[]{:S(2)}) copy-start(f32[64,8,20]{0,2,1:T(8,128)} %copy-done.17) | copy-start | bytes 122884
  311.0 56.7 %copy-start.8 = (bf16[1,64,3584]{2,1,0:T(8,128)(2,1)S(1)}, bf16[1,64,3584]{2,1,0:T(8,128)(2,1)}, u32[]{:S(2)}) copy-start(bf16[1,64,3584]{2,1,0:T(8,128)(2,1)} %param.15) | copy-start | bytes 1376260
  313.7 67.3 %collective-permute-start = (bf16[1,64,3584]{2,1,0:T(8,128)(2,1)}, bf16[1,64,3584]{2,1,0:T(8,128)(2,1)S(1)}, u32[]{:S(2)}, u32[]{:S(2)}) collective-permute-start(bf16[1,64,3584]{2,1,0:T(8,128)(2,1)} %fusion.7), channel_id=1, source_target_pairs={{0,32},{32,64},{64,96},{96,128},{128,160},{160,192},{192,224},{224... | collective-permute-start | bytes 1376264 | tf_op jit(solution)/shard_map/ppermute | solution.py:18
  368.4 10.1 %copy-start.2 = (f32[256,3584]{1,0:T(8,128)S(1)}, f32[256,3584]{1,0:T(8,128)}, u32[]{:S(2)}) copy-start(f32[256,3584]{1,0:T(8,128)} %fusion.46) | copy-start | bytes 11010052
  368.4 10.1 %copy-start.9 = (bf16[128,3584]{1,0:T(8,128)(2,1)S(1)}, bf16[128,3584]{1,0:T(8,128)(2,1)}, u32[]{:S(2)}) copy-start(bf16[128,3584]{1,0:T(8,128)(2,1)} %reshape.175) | copy-start | bytes 2752516
  368.4 10.1 %copy-start.16 = (f32[128,256]{1,0:T(8,128)S(1)}, f32[128,256]{1,0:T(8,128)}, u32[]{:S(2)}) copy-start(f32[128,256]{1,0:T(8,128)} %copy-done.15) | copy-start | bytes 393220
  368.4 25.4 %collective-permute-start.1 = (bf16[1,64,3584]{2,1,0:T(8,128)(2,1)S(1)}, bf16[1,64,3584]{2,1,0:T(8,128)(2,1)S(1)}, u32[]{:S(2)}, u32[]{:S(2)}) collective-permute-start(bf16[1,64,3584]{2,1,0:T(8,128)(2,1)S(1)} %fusion.6), channel_id=1, source_target_pairs={{0,224},{32,0},{64,32},{96,64},{128,96},{160,128},{192,160},{224,1... | collective-permute-start | bytes 1376264 | tf_op jit(solution)/shard_map/ppermute | solution.py:18
  373.8 21.5 %copy-start.1 = (bf16[1,1,3584,256]{3,2,1,0:T(8,128)(2,1)S(1)}, bf16[1,1,3584,256]{3,2,1,0:T(8,128)(2,1)}, u32[]{:S(2)}) copy-start(bf16[1,1,3584,256]{3,2,1,0:T(8,128)(2,1)} %param.16) | copy-start | bytes 5505028

commit v10 on v7

--- a/solution.py
+++ b/solution.py
@@ -273,12 +273,13 @@
     got_f, got_x, got_g = [got[index].reshape(-1, model_width) for index in range(3)]
     part = expert_forward(got_f, up_proj, down_proj)
     wire_f = group_sum(part, experts)
+    summed_f = send_home([wire_f], 1)[0].reshape(-1, model_width).astype(jnp.float32)
+    merged = jnp.dot(gated_f, summed_f, precision=HIGH)
+    section_out = (fwd_input.astype(jnp.float32) + merged).astype(jnp.bfloat16)
+    section_out, got_x, got_g = lax.optimization_barrier((section_out, got_x, got_g))
     dpart, grad_up, grad_down = expert_backward(got_x, got_g, up_proj, down_proj)
     wire_b = group_sum(dpart, experts)
-    summed_f = send_home([wire_f], 1)[0].reshape(-1, model_width).astype(jnp.float32)
     summed_b = send_home([wire_b], 2)[0].reshape(-1, model_width).astype(jnp.float32)
-    merged = jnp.dot(gated_f, summed_f, precision=HIGH)
-    section_out = (fwd_input.astype(jnp.float32) + merged).astype(jnp.bfloat16)
     spread_back = jnp.dot(plain_b, summed_b, precision=HIGH)
     section_grad = (out_grad.astype(jnp.float32) + spread_back).astype(jnp.bfloat16)
     fwd_next = passed_along(section_out[None], "pipe", 1)

time: 383 us -> 396 us (1.034)
  blocking collectives: 0 us -> 21.2 us
  starting transfers between devices: 32.3 us -> 19.5 us
    all_to_all x0 -> x2, blocking collectives: none -> 21.2 us  [group_sum(): mine = lax.all_to_all(blocks, 'ec', split_axis=0, concat_axis=0, tiled=True)]
    all_to_all x2 -> x0, starting transfers between devices: 11.7 us -> none  [group_sum(): mine = lax.all_to_all(blocks, 'ec', split_axis=0, concat_axis=0, tiled=True)]
  transfers between devices with their start and end apart: 6 -> 4, of which waited for: 2 -> 3; matrix products, arithmetic and copies ran while one was open for 17% -> 9% of each run, Pallas kernels for 19% -> 11%
where the time goes in v10:
time: 396 us; the launch traced here: 393 us
  Pallas kernels  210 us (53%)
  local copies, waits for them, and re-layouts  49.1 us (12%)
  waiting for transfers between devices  39.8 us (10%)
  matrix products  35.1 us (9%)
  blocking collectives  21.2 us (5%)
  starting transfers between devices  19.5 us (5%)
  other arithmetic  18.3 us (5%)
    pallas_call x1, Pallas kernels, dispatch(): pl.pallas_call(functools.partial(dispatch_kernel, groups), out_shape=[jax...  135 us
    pallas_call x2, Pallas kernels, send_home(): pl.pallas_call(functools.partial(return_kernel, groups), out_shape=jax.Sh...  74.7 us
    reshape x3, local copies, waits for them, and re-layouts, local(): got[index].reshape(-1, model_width)  27.1 us
    all_to_all x2, waiting for transfers between devices, group_sum(): other = lax.all_to_all(pair, 'ez', split_axis=0, concat_axis=0, tiled=True)  26.6 us
    all_to_all x2, blocking collectives, group_sum(): mine = lax.all_to_all(blocks, 'ec', split_axis=0, concat_axis=0, tiled=True)  21.2 us
    ppermute x2, waiting for transfers between devices, passed_along(): return lax.ppermute(value, axis, pairs)  13.3 us
    reshape x5, local copies, waits for them, and re-layouts, to_wire(): return rows.reshape(*lead, -1, 128)  11.4 us
    reduce_sum x2, other arithmetic, group_sum(): pair = jnp.sum(mine.astype(jnp.float32), axis=0).astype(jnp.bfloat16)  10.2 us
  transfers between devices with their start and end apart: 4, of which 3 were waited for; matrix products, arithmetic and copies ran while one was open for 9% of the time, Pallas kernels for 11%

profile of v10, /device:TPU:1, one launch (start us, length us, event | category | flops | bytes accessed | tf_op | source)
XLA Modules:
  0.0 393.5 jit_solution(18126228677260485353)
XLA Ops:
  0.6 0.0 copy-start
  0.6 0.9 copy.29
  1.5 0.1 eq.58
  1.7 0.8 copy.31
  2.5 0.1 eq.65
  2.6 0.1 fusion.26
  2.7 0.2 reduce_window_sum.18
  2.9 0.2 select_reduce_fusion.2
  3.0 0.1 reduce_sum.111
  3.2 0.0 copy-start.1
  3.2 0.1 copy.32
  3.3 0.7 bitcast_add_fusion
  4.0 0.1 fusion.27
  4.1 0.2 reduce_window_sum.17
  4.3 0.2 select_reduce_fusion.3
  4.5 0.1 reduce_sum.107
  4.6 0.1 copy.30
  4.7 0.7 bitcast_add_fusion.1
  5.4 0.8 select_reduce_fusion
  6.2 2.1 convolution_convert_fusion.2
  8.3 2.3 reshape.84.refs_2_
  10.6 0.0 copy-done.5
  10.6 0.7 convert_reduce_fusion.1
  11.3 0.5 convolution_convert_fusion.4
  11.8 2.3 reshape.82.refs_0_
  14.1 1.5 convolution_convert_fusion.3
  15.6 2.3 reshape.83.refs_1_
  17.9 134.8 %shard_map.120 = (bf16[2,2,8,560,128]{4,3,2,1,0:T(8,128)(2,1)}, bf16[2,2,8,560,128]{4,3,2,1,0:T(8,128)(2,1)}, bf16[2,2,8,560,128]{4,3,2,1,0:T(8,128)(2,1)}) custom-call(bf16[8,560,128]{2,1,0:T(8,128)(2,1)} %reshape.82.refs_0_, bf16[8,560,128]{2,1,0:T(8,128)(2,1)} %reshape.83.refs_1_, bf16[8,560,128]{2,1,0:T(8,128)(2,1)} %reshape.84.refs_2_), custom_call_target="tpu_custom_call" | custom-call | tf_op jit(solution)/shard_map/pallas_call | solution.py:144
  152.7 9.0 %reshape.85 = bf16[640,3584]{1,0:T(8,128)(2,1)} reshape(bf16[2,2,8,560,128]{4,3,2,1,0:T(8,128)(2,1)} %get-tuple-element.10) | data formatting | bytes 9175040 | tf_op jit(solution)/shard_map/reshape | solution.py:273
  161.7 9.9 %convolution_convert_fusion.1 = bf16[640,3584]{1,0:T(8,128)(2,1)} fusion(bf16[1,1,256,3584]{3,2,1,0:T(8,128)(2,1)} %param.17, bf16[640,3584]{1,0:T(8,128)(2,1)} %reshape.85, bf16[1,1,3584,256]{3,2,1,0:T(8,128)(2,1)S(1)} %copy-done), kind=kOutput, calls=%fused_computation.1 | convolution fusion | flops 2351923200 | bytes 12845056 | tf_op jit(solution)/shard_map/...f,fd->...d/dot_general | solution.py:233
  171.7 12.3 %all_to_all.20 = bf16[2,2,160,3584]{3,2,1,0:T(8,128)(2,1)} all-to-all(bf16[2,2,160,3584]{3,2,1,0:T(8,128)(2,1)} %bitcast.72), channel_id=1, replica_groups=mesh['pipe'=8,'eg'=8,'ez'=2,'ec'=2] {'ec'}, dimensions={0} | all-to-all | bytes 9175040 | tf_op jit(solution)/shard_map/all_to_all | solution.py:223
  184.0 5.1 %reduce_sum.114 = bf16[2,160,3584]{2,1,0:T(8,128)(2,1)} reduce(bf16[2,2,160,3584]{3,2,1,0:T(8,128)(2,1)} %all_to_all.20, bf16[]{:T(256)} %constant.23.clone.1), dimensions={0}, to_apply=%region_8.9 | reduce | flops 1146880 | bytes 6881282 | tf_op jit(solution)/shard_map/reduce_sum | solution.py:224
  189.1 5.1 %all-to-all-start.1 = ((bf16[2,160,3584]{2,1,0:T(8,128)(2,1)}), bf16[2,160,3584]{2,1,0:T(8,128)(2,1)}, u32[]{:S(2)}, u32[]{:S(2)}) async-start(bf16[2,160,3584]{2,1,0:T(8,128)(2,1)} %reduce_sum.114), calls=%async_computation.1 | async-start | bytes 4587520 | tf_op jit(solution)/shard_map/all_to_all | solution.py:225
  194.2 9.1 %reshape.88 = bf16[640,3584]{1,0:T(8,128)(2,1)} reshape(bf16[2,2,8,560,128]{4,3,2,1,0:T(8,128)(2,1)} %get-tuple-element.11) | data formatting | bytes 9175040 | tf_op jit(solution)/shard_map/reshape | solution.py:273
  203.3 9.0 %reshape.89 = bf16[640,3584]{1,0:T(8,128)(2,1)} reshape(bf16[2,2,8,560,128]{4,3,2,1,0:T(8,128)(2,1)} %get-tuple-element.12) | data formatting | bytes 9175040 | tf_op jit(solution)/shard_map/reshape | solution.py:273
  212.3 9.5 %all-to-all-done.1 = bf16[2,160,3584]{2,1,0:T(8,128)(2,1)} async-done(((bf16[2,160,3584]{2,1,0:T(8,128)(2,1)}), bf16[2,160,3584]{2,1,0:T(8,128)(2,1)}, u32[]{:S(2)}, u32[]{:S(2)}) %all-to-all-start.1) | async-done | bytes 2293792 | tf_op jit(solution)/shard_map/all_to_all | solution.py:225
  221.8 2.1 reduce_sum.115
  223.9 2.3 reshape.87.refs_0_
  226.2 33.0 %shard_map.121 = bf16[1,8,560,128]{3,2,1,0:T(8,128)(2,1)} custom-call(bf16[8,560,128]{2,1,0:T(8,128)(2,1)} %reshape.87.refs_0_), custom_call_target="tpu_custom_call" | custom-call | tf_op jit(solution)/shard_map/pallas_call | solution.py:210
  259.2 2.4 reshape_squeeze.8
  261.6 0.0 slice-start
  261.6 2.4 fusion
  264.0 3.8 fusion.7
  267.8 0.8 copy-done.3
  268.6 0.0 copy-done.6
  268.6 1.4 fusion.14
  270.0 1.4 convolution_convert_fusion
  271.4 8.9 %all_to_all.21 = bf16[2,2,160,3584]{3,2,1,0:T(8,128)(2,1)} all-to-all(bf16[2,2,160,3584]{3,2,1,0:T(8,128)(2,1)S(1)} %bitcast.71), channel_id=1, replica_groups=mesh['pipe'=8,'eg'=8,'ez'=2,'ec'=2] {'ec'}, dimensions={0} | all-to-all | bytes 9175040 | tf_op jit(solution)/shard_map/all_to_all | solution.py:223
  280.3 5.1 %reduce_sum.116 = bf16[2,160,3584]{2,1,0:T(8,128)(2,1)} reduce(bf16[2,2,160,3584]{3,2,1,0:T(8,128)(2,1)} %all_to_all.21, bf16[]{:T(256)} %constant.23.clone.1), dimensions={0}, to_apply=%region_10.11 | reduce | flops 1146880 | bytes 6881282 | tf_op jit(solution)/shard_map/reduce_sum | solution.py:224
  285.4 4.9 %all-to-all-start.3 = ((bf16[2,160,3584]{2,1,0:T(8,128)(2,1)}), bf16[2,160,3584]{2,1,0:T(8,128)(2,1)}, u32[]{:S(2)}, u32[]{:S(2)}) async-start(bf16[2,160,3584]{2,1,0:T(8,128)(2,1)} %reduce_sum.116), calls=%async_computation.3 | async-start | bytes 4587520 | tf_op jit(solution)/shard_map/all_to_all | solution.py:225
  290.3 4.0 %collective-permute-start = (bf16[1,64,3584]{2,1,0:T(8,128)(2,1)}, bf16[1,64,3584]{2,1,0:T(8,128)(2,1)}, u32[]{:S(2)}, u32[]{:S(2)}) collective-permute-start(bf16[1,64,3584]{2,1,0:T(8,128)(2,1)} %bitcast.10), channel_id=1, source_target_pairs={{0,32},{32,64},{64,96},{96,128},{128,160},{160,192},{192,224},{224... | collective-permute-start | bytes 1376264 | tf_op jit(solution)/shard_map/ppermute | solution.py:18
  294.3 5.8 %convolution_bitcast_fusion.1 = f32[1,1,3584,256]{3,2,1,0:T(8,128)} fusion(bf16[640,3584]{1,0:T(8,128)(2,1)} %reshape.88, bf16[640,256]{1,0:T(8,128)(2,1)S(1)} %fusion.14), kind=kOutput, calls=%fused_computation.3 | convolution fusion | flops 1174405120 | bytes 8585216 | tf_op jit(solution)/shard_map/rd,rf->df/dot_general | solution.py:246
  300.1 17.0 %all-to-all-done.3 = bf16[2,160,3584]{2,1,0:T(8,128)(2,1)} async-done(((bf16[2,160,3584]{2,1,0:T(8,128)(2,1)}), bf16[2,160,3584]{2,1,0:T(8,128)(2,1)}, u32[]{:S(2)}, u32[]{:S(2)}) %all-to-all-start.3) | async-done | bytes 2293792 | tf_op jit(solution)/shard_map/all_to_all | solution.py:225
  317.1 2.1 reduce_sum.117
  319.2 2.3 reshape.91.refs_0_
  321.5 41.7 %shard_map.122 = bf16[1,8,560,128]{3,2,1,0:T(8,128)(2,1)} custom-call(bf16[8,560,128]{2,1,0:T(8,128)(2,1)} %reshape.91.refs_0_), custom_call_target="tpu_custom_call" | custom-call | tf_op jit(solution)/shard_map/pallas_call | solution.py:210
  363.3 2.4 reshape_squeeze.9
  365.7 0.6 fusion.2
  366.3 5.6 %collective-permute-start.1 = (bf16[1,64,3584]{2,1,0:T(8,128)(2,1)S(1)}, bf16[1,64,3584]{2,1,0:T(8,128)(2,1)S(1)}, u32[]{:S(2)}, u32[]{:S(2)}) collective-permute-start(bf16[1,64,3584]{2,1,0:T(8,128)(2,1)S(1)} %fusion.2), channel_id=1, source_target_pairs={{0,224},{32,0},{64,32},{96,64},{128,96},{160,128},{192,160},{224,1... | collective-permute-start | bytes 1376264 | tf_op jit(solution)/shard_map/ppermute | solution.py:18
  371.9 5.8 %convolution_bitcast_fusion = f32[1,1,256,3584]{3,2,1,0:T(8,128)} fusion(bf16[640,3584]{1,0:T(8,128)(2,1)} %reshape.89, f32[640,256]{1,0:T(8,128)S(1)} %copy-done.4), kind=kOutput, calls=%fused_computation.2 | convolution fusion | flops 1175224320 | bytes 8912896 | tf_op jit(solution)/shard_map/rf,rd->fd/dot_general | solution.py:247
  377.6 0.0 collective-permute-done
  377.6 13.3 %collective-permute-done.1 = bf16[1,64,3584]{2,1,0:T(8,128)(2,1)S(1)} collective-permute-done((bf16[1,64,3584]{2,1,0:T(8,128)(2,1)S(1)}, bf16[1,64,3584]{2,1,0:T(8,128)(2,1)S(1)}, u32[]{:S(2)}, u32[]{:S(2)}) %collective-permute-start.1) | collective-permute-done | bytes 458784 | tf_op jit(solution)/shard_map/ppermute | solution.py:18
  390.9 1.8 copy.35
  392.7 0.8 copy.36
  (13 shorter events, 0.0 us)
Async XLA Ops:
  0.6 161.1 %copy-start = (bf16[1,1,3584,256]{3,2,1,0:T(8,128)(2,1)S(1)}, bf16[1,1,3584,256]{3,2,1,0:T(8,128)(2,1)}, u32[]{:S(2)}) copy-start(bf16[1,1,3584,256]{3,2,1,0:T(8,128)(2,1)} %param.16) | copy-start | bytes 5505028
  2.9 7.7 %copy-start.5 = (f32[1,64,2]{1,2,0:T(2,128)S(1)}, f32[1,64,2]{1,2,0:T(2,128)}, u32[]{:S(2)}) copy-start(f32[1,64,2]{1,2,0:T(2,128)} %param.11) | copy-start | bytes 1540
  3.2 8.1 %copy-start.1 = (bf16[1,64,3584]{2,1,0:T(8,128)(2,1)S(1)}, bf16[1,64,3584]{2,1,0:T(8,128)(2,1)}, u32[]{:S(2)}) copy-start(bf16[1,64,3584]{2,1,0:T(8,128)(2,1)} %param.9) | copy-start | bytes 1376260
  189.1 32.7 %all-to-all-start.1 = ((bf16[2,160,3584]{2,1,0:T(8,128)(2,1)}), bf16[2,160,3584]{2,1,0:T(8,128)(2,1)}, u32[]{:S(2)}, u32[]{:S(2)}) async-start(bf16[2,160,3584]{2,1,0:T(8,128)(2,1)} %reduce_sum.114), calls=%async_computation.1 | async-start | bytes 4587520 | tf_op jit(solution)/shard_map/all_to_all | solution.py:225
  261.6 7.0 %slice-start = ((s8[4587520]{0:T(1024)(128)(4,1)}), s8[4194304]{0:T(1024)(128)(4,1)S(1)}, s32[]{:S(2)}) async-start(s8[4587520]{0:T(1024)(128)(4,1)} %bitcast.69), calls=%async_computation.4 | async-start | bytes 8388608
  263.9 4.7 %slice-start.1 = ((s8[4587520]{0:T(1024)(128)(4,1)}), s8[393216]{0:T(1024)(128)(4,1)S(1)}, s32[]{:S(2)}) async-start(s8[4587520]{0:T(1024)(128)(4,1)} %bitcast.69), calls=%async_computation.5 | async-start | bytes 786432
  264.0 4.7 %copy-start.6 = (bf16[1,1,256,3584]{3,2,1,0:T(8,128)(2,1)S(1)}, bf16[1,1,256,3584]{3,2,1,0:T(8,128)(2,1)}, u32[]{:S(2)}) copy-start(bf16[1,1,256,3584]{3,2,1,0:T(8,128)(2,1)} %param.17) | copy-start | bytes 5505028
  267.8 0.8 copy-start.3
  285.4 31.7 %all-to-all-start.3 = ((bf16[2,160,3584]{2,1,0:T(8,128)(2,1)}), bf16[2,160,3584]{2,1,0:T(8,128)(2,1)}, u32[]{:S(2)}, u32[]{:S(2)}) async-start(bf16[2,160,3584]{2,1,0:T(8,128)(2,1)} %reduce_sum.116), calls=%async_computation.3 | async-start | bytes 4587520 | tf_op jit(solution)/shard_map/all_to_all | solution.py:225
  290.3 87.3 %collective-permute-start = (bf16[1,64,3584]{2,1,0:T(8,128)(2,1)}, bf16[1,64,3584]{2,1,0:T(8,128)(2,1)}, u32[]{:S(2)}, u32[]{:S(2)}) collective-permute-start(bf16[1,64,3584]{2,1,0:T(8,128)(2,1)} %bitcast.10), channel_id=1, source_target_pairs={{0,32},{32,64},{64,96},{96,128},{128,160},{160,192},{192,224},{224... | collective-permute-start | bytes 1376264 | tf_op jit(solution)/shard_map/ppermute | solution.py:18
  321.5 44.1 %copy-start.2 = (bf16[1,64,3584]{2,1,0:T(8,128)(2,1)S(1)}, bf16[1,64,3584]{2,1,0:T(8,128)(2,1)}, u32[]{:S(2)}) copy-start(bf16[1,64,3584]{2,1,0:T(8,128)(2,1)} %param.15) | copy-start | bytes 1376260
  365.7 6.2 %copy-start.4 = (f32[640,256]{1,0:T(8,128)S(1)}, f32[640,256]{1,0:T(8,128)}, u32[]{:S(2)}) copy-start(f32[640,256]{1,0:T(8,128)} %copy-done.3) | copy-start | bytes 1966084
  366.3 24.6 %collective-permute-start.1 = (bf16[1,64,3584]{2,1,0:T(8,128)(2,1)S(1)}, bf16[1,64,3584]{2,1,0:T(8,128)(2,1)S(1)}, u32[]{:S(2)}, u32[]{:S(2)}) collective-permute-start(bf16[1,64,3584]{2,1,0:T(8,128)(2,1)S(1)} %fusion.2), channel_id=1, source_target_pairs={{0,224},{32,0},{64,32},{96,64},{128,96},{160,128},{192,160},{224,1... | collective-permute-start | bytes 1376264 | tf_op jit(solution)/shard_map/ppermute | solution.py:18

commit v11 on v7

--- a/solution.py
+++ b/solution.py
@@ -275,8 +275,9 @@
     wire_f = group_sum(part, experts)
     dpart, grad_up, grad_down = expert_backward(got_x, got_g, up_proj, down_proj)
     wire_b = group_sum(dpart, experts)
-    summed_f = send_home([wire_f], 1)[0].reshape(-1, model_width).astype(jnp.float32)
-    summed_b = send_home([wire_b], 2)[0].reshape(-1, model_width).astype(jnp.float32)
+    summed_f, summed_b = [
+        block.reshape(-1, model_width).astype(jnp.float32) for block in send_home([wire_f, wire_b], 1)
+    ]
     merged = jnp.dot(gated_f, summed_f, precision=HIGH)
     section_out = (fwd_input.astype(jnp.float32) + merged).astype(jnp.bfloat16)
     spread_back = jnp.dot(plain_b, summed_b, precision=HIGH)

time: 383 us -> 400 us (1.044)
  waiting for transfers between devices: 38.4 us -> 72.4 us
  Pallas kernels: 208 us -> 192 us
  starting transfers between devices: 32.3 us -> 27.6 us
    ppermute x2, waiting for transfers between devices: 15.7 us -> 33.5 us  [passed_along(): return lax.ppermute(value, axis, pairs)]
    all_to_all x2, waiting for transfers between devices: 22.7 us -> 38.9 us  [group_sum(): other = lax.all_to_all(pair, 'ez', split_axis=0, concat_axis=0, tiled=True)]
    pallas_call x2 -> x1, Pallas kernels: 73.3 us -> 57.7 us  [send_home(): pl.pallas_call(functools.partial(return_kernel, groups), out_shape=jax.Sh...]
    ppermute x2, starting transfers between devices: 10.6 us -> 5.9 us  [passed_along(): return lax.ppermute(value, axis, pairs)]
  transfers between devices with their start and end apart: 6 -> 6, of which waited for: 2 -> 4; matrix products, arithmetic and copies ran while one was open for 17% -> 14% of each run, Pallas kernels for 19% -> 0%
where the time goes in v11:
time: 400 us; the launch traced here: 399 us
  Pallas kernels  192 us (48%)
  waiting for transfers between devices  72.4 us (18%)
  local copies, waits for them, and re-layouts  49.5 us (12%)
  matrix products  37.9 us (9%)
  starting transfers between devices  27.6 us (7%)
  other arithmetic  18.3 us (5%)
    pallas_call x1, Pallas kernels, dispatch(): pl.pallas_call(functools.partial(dispatch_kernel, groups), out_shape=[jax...  135 us
    pallas_call x1, Pallas kernels, send_home(): pl.pallas_call(functools.partial(return_kernel, groups), out_shape=jax.Sh...  57.7 us
    all_to_all x2, waiting for transfers between devices, group_sum(): other = lax.all_to_all(pair, 'ez', split_axis=0, concat_axis=0, tiled=True)  38.9 us
    ppermute x2, waiting for transfers between devices, passed_along(): return lax.ppermute(value, axis, pairs)  33.5 us
    reshape x3, local copies, waits for them, and re-layouts, local(): got[index].reshape(-1, model_width)  27.1 us
    all_to_all x2, starting transfers between devices, group_sum(): mine = lax.all_to_all(blocks, 'ec', split_axis=0, concat_axis=0, tiled=True)  11.7 us
    reshape x5, local copies, waits for them, and re-layouts, to_wire(): return rows.reshape(*lead, -1, 128)  11.4 us
    reduce_sum x2, other arithmetic, group_sum(): pair = jnp.sum(mine.astype(jnp.float32), axis=0).astype(jnp.bfloat16)  10.2 us
  transfers between devices with their start and end apart: 6, of which 4 were waited for; matrix products, arithmetic and copies ran while one was open for 14% of the time, Pallas kernels for 0%

profile of v11, /device:TPU:1, one launch (start us, length us, event | category | flops | bytes accessed | tf_op | source)
XLA Modules:
  0.0 399.0 jit_solution(16247517698394020175)
XLA Ops:
  0.6 0.0 copy-start
  0.6 0.9 copy.29
  1.6 0.1 eq.58
  1.7 0.8 copy.31
  2.5 0.1 eq.65
  2.6 0.1 fusion.27
  2.7 0.2 reduce_window_sum.18
  2.9 0.2 select_reduce_fusion.2
  3.0 0.1 reduce_sum.111
  3.2 0.0 copy-start.4
  3.2 0.1 copy.32
  3.3 0.7 bitcast_add_fusion
  4.0 0.1 fusion.28
  4.1 0.2 reduce_window_sum.17
  4.3 0.2 select_reduce_fusion.3
  4.5 0.1 reduce_sum.107
  4.6 0.1 copy.30
  4.7 0.7 bitcast_add_fusion.1
  5.4 0.8 select_reduce_fusion
  6.2 2.1 convolution_convert_fusion.2
  8.3 2.3 reshape.84.refs_2_
  10.6 0.7 convert_reduce_fusion.1
  11.3 0.5 convolution_convert_fusion.4
  11.8 2.3 reshape.82.refs_0_
  14.1 1.5 convolution_convert_fusion.3
  15.6 2.3 reshape.83.refs_1_
  17.9 134.8 %shard_map.120 = (bf16[2,2,8,560,128]{4,3,2,1,0:T(8,128)(2,1)}, bf16[2,2,8,560,128]{4,3,2,1,0:T(8,128)(2,1)}, bf16[2,2,8,560,128]{4,3,2,1,0:T(8,128)(2,1)}) custom-call(bf16[8,560,128]{2,1,0:T(8,128)(2,1)} %reshape.82.refs_0_, bf16[8,560,128]{2,1,0:T(8,128)(2,1)} %reshape.83.refs_1_, bf16[8,560,128]{2,1,0:T(8,128)(2,1)} %reshape.84.refs_2_), custom_call_target="tpu_custom_call" | custom-call | tf_op jit(solution)/shard_map/pallas_call | solution.py:144
  152.7 9.0 %reshape.85 = bf16[640,3584]{1,0:T(8,128)(2,1)} reshape(bf16[2,2,8,560,128]{4,3,2,1,0:T(8,128)(2,1)} %get-tuple-element.7) | data formatting | bytes 9175040 | tf_op jit(solution)/shard_map/reshape | solution.py:273
  161.7 9.9 %convolution_convert_fusion.1 = bf16[640,3584]{1,0:T(8,128)(2,1)} fusion(bf16[1,1,256,3584]{3,2,1,0:T(8,128)(2,1)} %param.17, bf16[640,3584]{1,0:T(8,128)(2,1)} %reshape.85, bf16[1,1,3584,256]{3,2,1,0:T(8,128)(2,1)S(1)} %copy-done), kind=kOutput, calls=%fused_computation.1 | convolution fusion | flops 2351923200 | bytes 12845056 | tf_op jit(solution)/shard_map/...f,fd->...d/dot_general | solution.py:233
  171.6 5.9 %all-to-all-start = ((bf16[2,2,160,3584]{3,2,1,0:T(8,128)(2,1)}), bf16[2,2,160,3584]{3,2,1,0:T(8,128)(2,1)}, u32[]{:S(2)}, u32[]{:S(2)}) async-start(bf16[2,2,160,3584]{3,2,1,0:T(8,128)(2,1)} %bitcast.71), calls=%async_computation | async-start | bytes 9175040 | tf_op jit(solution)/shard_map/all_to_all | solution.py:223
  177.5 9.0 %reshape.88 = bf16[640,3584]{1,0:T(8,128)(2,1)} reshape(bf16[2,2,8,560,128]{4,3,2,1,0:T(8,128)(2,1)} %get-tuple-element.8) | data formatting | bytes 9175040 | tf_op jit(solution)/shard_map/reshape | solution.py:273
  186.6 9.1 %reshape.89 = bf16[640,3584]{1,0:T(8,128)(2,1)} reshape(bf16[2,2,8,560,128]{4,3,2,1,0:T(8,128)(2,1)} %get-tuple-element.9) | data formatting | bytes 9175040 | tf_op jit(solution)/shard_map/reshape | solution.py:273
  195.6 3.8 fusion.8
  199.4 0.8 copy-done.5
  200.3 1.4 fusion.15
  201.7 3.5 convolution_convert_fusion
  205.2 0.0 all-to-all-done
  205.2 5.9 %all-to-all-start.2 = ((bf16[2,2,160,3584]{3,2,1,0:T(8,128)(2,1)}), bf16[2,2,160,3584]{3,2,1,0:T(8,128)(2,1)}, u32[]{:S(2)}, u32[]{:S(2)}) async-start(bf16[2,2,160,3584]{3,2,1,0:T(8,128)(2,1)} %bitcast.70), calls=%async_computation.2 | async-start | bytes 9175040 | tf_op jit(solution)/shard_map/all_to_all | solution.py:223
  211.1 5.1 %reduce_sum.114 = bf16[2,160,3584]{2,1,0:T(8,128)(2,1)} reduce(bf16[2,2,160,3584]{3,2,1,0:T(8,128)(2,1)} %all-to-all-done, bf16[]{:T(256)} %constant.23.clone.1), dimensions={0}, to_apply=%region_8.9 | reduce | flops 1146880 | bytes 6881282 | tf_op jit(solution)/shard_map/reduce_sum | solution.py:224
  216.2 4.9 %all-to-all-start.1 = ((bf16[2,160,3584]{2,1,0:T(8,128)(2,1)}), bf16[2,160,3584]{2,1,0:T(8,128)(2,1)}, u32[]{:S(2)}, u32[]{:S(2)}) async-start(bf16[2,160,3584]{2,1,0:T(8,128)(2,1)} %reduce_sum.114), calls=%async_computation.1 | async-start | bytes 4587520 | tf_op jit(solution)/shard_map/all_to_all | solution.py:225
  221.1 5.1 %reduce_sum.116 = bf16[2,160,3584]{2,1,0:T(8,128)(2,1)} reduce(bf16[2,2,160,3584]{3,2,1,0:T(8,128)(2,1)} %all-to-all-done.2, bf16[]{:T(256)} %constant.23.clone.1), dimensions={0}, to_apply=%region_10.11 | reduce | flops 1146880 | bytes 6881282 | tf_op jit(solution)/shard_map/reduce_sum | solution.py:224
  226.2 22.8 %all-to-all-done.1 = bf16[2,160,3584]{2,1,0:T(8,128)(2,1)} async-done(((bf16[2,160,3584]{2,1,0:T(8,128)(2,1)}), bf16[2,160,3584]{2,1,0:T(8,128)(2,1)}, u32[]{:S(2)}, u32[]{:S(2)}) %all-to-all-start.1) | async-done | bytes 2293792 | tf_op jit(solution)/shard_map/all_to_all | solution.py:225
  249.0 5.1 %all-to-all-start.3 = ((bf16[2,160,3584]{2,1,0:T(8,128)(2,1)}), bf16[2,160,3584]{2,1,0:T(8,128)(2,1)}, u32[]{:S(2)}, u32[]{:S(2)}) async-start(bf16[2,160,3584]{2,1,0:T(8,128)(2,1)} %reduce_sum.116), calls=%async_computation.3 | async-start | bytes 4587520 | tf_op jit(solution)/shard_map/all_to_all | solution.py:225
  254.1 5.8 %convolution_bitcast_fusion.1 = f32[1,1,3584,256]{3,2,1,0:T(8,128)} fusion(bf16[640,3584]{1,0:T(8,128)(2,1)} %reshape.89, bf16[640,256]{1,0:T(8,128)(2,1)S(1)} %fusion.15), kind=kOutput, calls=%fused_computation.3 | convolution fusion | flops 1174405120 | bytes 8585216 | tf_op jit(solution)/shard_map/rd,rf->df/dot_general | solution.py:246
  259.8 2.1 reduce_sum.115
  262.0 2.3 reshape.87.refs_0_
  264.2 16.1 %all-to-all-done.3 = bf16[2,160,3584]{2,1,0:T(8,128)(2,1)} async-done(((bf16[2,160,3584]{2,1,0:T(8,128)(2,1)}), bf16[2,160,3584]{2,1,0:T(8,128)(2,1)}, u32[]{:S(2)}, u32[]{:S(2)}) %all-to-all-start.3) | async-done | bytes 2293792 | tf_op jit(solution)/shard_map/all_to_all | solution.py:225
  280.3 2.1 reduce_sum.117
  282.5 2.3 reshape.91.refs_1_
  284.8 57.7 %shard_map.121 = bf16[2,8,560,128]{3,2,1,0:T(8,128)(2,1)} custom-call(bf16[8,560,128]{2,1,0:T(8,128)(2,1)} %reshape.87.refs_0_, bf16[8,560,128]{2,1,0:T(8,128)(2,1)} %reshape.91.refs_1_), custom_call_target="tpu_custom_call" | custom-call | tf_op jit(solution)/shard_map/pallas_call | solution.py:210
  342.4 1.8 fusion.33
  344.2 0.0 copy-start.3
  344.2 2.1 reshape_unstack.7
  346.3 2.7 fusion.2
  349.0 5.8 %collective-permute-start.1 = (bf16[1,64,3584]{2,1,0:T(8,128)(2,1)}, bf16[1,64,3584]{2,1,0:T(8,128)(2,1)}, u32[]{:S(2)}, u32[]{:S(2)}) collective-permute-start(bf16[1,64,3584]{2,1,0:T(8,128)(2,1)} %fusion.2), channel_id=1, source_target_pairs={{0,224},{32,0},{64,32},{96,64},{128,96},{160,128},{192,160},{224,1... | collective-permute-start | bytes 1376264 | tf_op jit(solution)/shard_map/ppermute | solution.py:18
  354.8 1.3 reshape_unstack.6
  356.1 0.6 fusion.3
  356.7 0.1 collective-permute-start
  356.8 0.0 copy-start.1
  356.8 6.1 %convolution_bitcast_fusion = f32[1,1,256,3584]{3,2,1,0:T(8,128)} fusion(bf16[640,3584]{1,0:T(8,128)(2,1)} %reshape.88, f32[640,256]{1,0:T(8,128)} %copy-done.5), kind=kOutput, calls=%fused_computation.2 | convolution fusion | flops 1175224320 | bytes 8912896 | tf_op jit(solution)/shard_map/rf,rd->fd/dot_general | solution.py:247
  362.9 10.6 %collective-permute-done.1 = bf16[1,64,3584]{2,1,0:T(8,128)(2,1)} collective-permute-done((bf16[1,64,3584]{2,1,0:T(8,128)(2,1)}, bf16[1,64,3584]{2,1,0:T(8,128)(2,1)}, u32[]{:S(2)}, u32[]{:S(2)}) %collective-permute-start.1) | collective-permute-done | bytes 458784 | tf_op jit(solution)/shard_map/ppermute | solution.py:18
  373.5 22.9 %collective-permute-done = bf16[1,64,3584]{2,1,0:T(8,128)(2,1)S(1)} collective-permute-done((bf16[1,64,3584]{2,1,0:T(8,128)(2,1)S(1)}, bf16[1,64,3584]{2,1,0:T(8,128)(2,1)S(1)}, u32[]{:S(2)}, u32[]{:S(2)}) %collective-permute-start) | collective-permute-done | bytes 458784 | tf_op jit(solution)/shard_map/ppermute | solution.py:18
  396.5 0.8 copy.35
  397.2 1.8 copy.36
  (14 shorter events, 0.0 us)
Async XLA Ops:
  0.6 161.1 %copy-start = (bf16[1,1,3584,256]{3,2,1,0:T(8,128)(2,1)S(1)}, bf16[1,1,3584,256]{3,2,1,0:T(8,128)(2,1)}, u32[]{:S(2)}) copy-start(bf16[1,1,3584,256]{3,2,1,0:T(8,128)(2,1)} %param.16) | copy-start | bytes 5505028
  2.9 7.7 %copy-start.7 = (f32[1,64,2]{1,2,0:T(2,128)S(1)}, f32[1,64,2]{1,2,0:T(2,128)}, u32[]{:S(2)}) copy-start(f32[1,64,2]{1,2,0:T(2,128)} %param.11) | copy-start | bytes 1540
  3.2 8.1 %copy-start.4 = (bf16[1,64,3584]{2,1,0:T(8,128)(2,1)S(1)}, bf16[1,64,3584]{2,1,0:T(8,128)(2,1)}, u32[]{:S(2)}) copy-start(bf16[1,64,3584]{2,1,0:T(8,128)(2,1)} %param.9) | copy-start | bytes 1376260
  171.6 33.6 %all-to-all-start = ((bf16[2,2,160,3584]{3,2,1,0:T(8,128)(2,1)}), bf16[2,2,160,3584]{3,2,1,0:T(8,128)(2,1)}, u32[]{:S(2)}, u32[]{:S(2)}) async-start(bf16[2,2,160,3584]{3,2,1,0:T(8,128)(2,1)} %bitcast.71), calls=%async_computation | async-start | bytes 9175040 | tf_op jit(solution)/shard_map/all_to_all | solution.py:223
  195.6 4.6 %copy-start.2 = (bf16[640,3584]{1,0:T(8,128)(2,1)S(1)}, bf16[640,3584]{1,0:T(8,128)(2,1)}, u32[]{:S(2)}) copy-start(bf16[640,3584]{1,0:T(8,128)(2,1)} %reshape.88) | copy-start | bytes 13762564
  195.6 4.6 %copy-start.8 = (bf16[1,1,256,3584]{3,2,1,0:T(8,128)(2,1)S(1)}, bf16[1,1,256,3584]{3,2,1,0:T(8,128)(2,1)}, u32[]{:S(2)}) copy-start(bf16[1,1,256,3584]{3,2,1,0:T(8,128)(2,1)} %param.17) | copy-start | bytes 5505028
  199.4 0.8 copy-start.5
  205.2 11.0 %all-to-all-start.2 = ((bf16[2,2,160,3584]{3,2,1,0:T(8,128)(2,1)}), bf16[2,2,160,3584]{3,2,1,0:T(8,128)(2,1)}, u32[]{:S(2)}, u32[]{:S(2)}) async-start(bf16[2,2,160,3584]{3,2,1,0:T(8,128)(2,1)} %bitcast.70), calls=%async_computation.2 | async-start | bytes 9175040 | tf_op jit(solution)/shard_map/all_to_all | solution.py:223
  216.2 32.8 %all-to-all-start.1 = ((bf16[2,160,3584]{2,1,0:T(8,128)(2,1)}), bf16[2,160,3584]{2,1,0:T(8,128)(2,1)}, u32[]{:S(2)}, u32[]{:S(2)}) async-start(bf16[2,160,3584]{2,1,0:T(8,128)(2,1)} %reduce_sum.114), calls=%async_computation.1 | async-start | bytes 4587520 | tf_op jit(solution)/shard_map/all_to_all | solution.py:225
  249.0 31.4 %all-to-all-start.3 = ((bf16[2,160,3584]{2,1,0:T(8,128)(2,1)}), bf16[2,160,3584]{2,1,0:T(8,128)(2,1)}, u32[]{:S(2)}, u32[]{:S(2)}) async-start(bf16[2,160,3584]{2,1,0:T(8,128)(2,1)} %reduce_sum.116), calls=%async_computation.3 | async-start | bytes 4587520 | tf_op jit(solution)/shard_map/all_to_all | solution.py:225
  344.2 2.1 copy-start.3
  346.3 9.8 %copy-start.6 = (f32[64,160]{1,0:T(8,128)S(1)}, f32[64,160]{1,0:T(8,128)}, u32[]{:S(2)}) copy-start(f32[64,160]{1,0:T(8,128)} %get-tuple-element.13) | copy-start | bytes 122884
  349.0 24.5 %collective-permute-start.1 = (bf16[1,64,3584]{2,1,0:T(8,128)(2,1)}, bf16[1,64,3584]{2,1,0:T(8,128)(2,1)}, u32[]{:S(2)}, u32[]{:S(2)}) collective-permute-start(bf16[1,64,3584]{2,1,0:T(8,128)(2,1)} %fusion.2), channel_id=1, source_target_pairs={{0,224},{32,0},{64,32},{96,64},{128,96},{160,128},{192,160},{224,1... | collective-permute-start | bytes 1376264 | tf_op jit(solution)/shard_map/ppermute | solution.py:18
  356.7 39.7 %collective-permute-start = (bf16[1,64,3584]{2,1,0:T(8,128)(2,1)S(1)}, bf16[1,64,3584]{2,1,0:T(8,128)(2,1)S(1)}, u32[]{:S(2)}, u32[]{:S(2)}) collective-permute-start(bf16[1,64,3584]{2,1,0:T(8,128)(2,1)S(1)} %fusion.3), channel_id=1, source_target_pairs={{0,32},{32,64},{64,96},{96,128},{128,160},{160,192},{192,224},{224... | collective-permute-start | bytes 1376264 | tf_op jit(solution)/shard_map/ppermute | solution.py:18
  356.8 42.2 %copy-start.1 = (bf16[1,1,3584,256]{3,2,1,0:T(8,128)(2,1)S(1)}, bf16[1,1,3584,256]{3,2,1,0:T(8,128)(2,1)}, u32[]{:S(2)}) copy-start(bf16[1,1,3584,256]{3,2,1,0:T(8,128)(2,1)} %param.16) | copy-start | bytes 5505028

commit v12 on v7

--- a/solution.py
+++ b/solution.py
@@ -220,8 +220,8 @@
 def group_sum(parts, experts):
     model_width = parts.shape[-1]
     blocks = parts.reshape(2, 2, -1, model_width)
-    mine = lax.all_to_all(blocks, "ec", split_axis=0, concat_axis=0, tiled=True)
-    pair = jnp.sum(mine.astype(jnp.float32), axis=0).astype(jnp.bfloat16)
+    pair = lax.psum_scatter(blocks, "ec", scatter_dimension=0, tiled=True)
+    pair = pair.reshape(blocks.shape[1:])
     other = lax.all_to_all(pair, "ez", split_axis=0, concat_axis=0, tiled=True)
     summed = jnp.sum(other.astype(jnp.float32), axis=0).astype(jnp.bfloat16)
     return to_wire(summed, experts)

time: 383 us -> 380 us (level)
  between operations: 0.85 us -> 14.3 us
  starting transfers between devices: 32.3 us -> 20.4 us
  other arithmetic: 18.3 us -> 8.04 us
  waiting for transfers between devices: 38.4 us -> 43.4 us
    reduce_scatter x0 -> x2, waiting for transfers between devices: none -> 15.3 us  [group_sum(): pair = lax.psum_scatter(blocks, 'ec', scatter_dimension=0, tiled=True)]
    all_to_all x2 -> x0, starting transfers between devices: 11.7 us -> none  [group_sum(): mine = lax.all_to_all(blocks, 'ec', split_axis=0, concat_axis=0, tiled=True)]
    all_to_all x2, waiting for transfers between devices: 22.7 us -> 12.3 us  [group_sum(): other = lax.all_to_all(pair, 'ez', split_axis=0, concat_axis=0, tiled=True)]
    reduce_sum x2 -> x0, other arithmetic: 10.3 us -> none  [group_sum(): pair = jnp.sum(mine.astype(jnp.float32), axis=0).astype(jnp.bfloat16)]
  transfers between devices with their start and end apart: 6 -> 6, of which waited for: 2 -> 3; matrix products, arithmetic and copies ran while one was open for 17% -> 14% of each run, Pallas kernels for 19% -> 19%
where the time goes in v12:
time: 380 us; the launch traced here: 379 us
  Pallas kernels  208 us (55%)
  local copies, waits for them, and re-layouts  48 us (13%)
  waiting for transfers between devices  43.4 us (11%)
  matrix products  36.6 us (10%)
  starting transfers between devices  20.4 us (5%)
  between operations  14.3 us (4%)
  other arithmetic  8.04 us (2%)
    pallas_call x1, Pallas kernels, dispatch(): pl.pallas_call(functools.partial(dispatch_kernel, groups), out_shape=[jax...  135 us
    pallas_call x2, Pallas kernels, send_home(): pl.pallas_call(functools.partial(return_kernel, groups), out_shape=jax.Sh...  73.4 us
    reshape x3, local copies, waits for them, and re-layouts, local(): got[index].reshape(-1, model_width)  27.4 us
    ppermute x2, waiting for transfers between devices, passed_along(): return lax.ppermute(value, axis, pairs)  15.8 us
    reduce_scatter x2, waiting for transfers between devices, group_sum(): pair = lax.psum_scatter(blocks, 'ec', scatter_dimension=0, tiled=True)  15.3 us
    all_to_all x2, waiting for transfers between devices, group_sum(): other = lax.all_to_all(pair, 'ez', split_axis=0, concat_axis=0, tiled=True)  12.3 us
    reshape x5, local copies, waits for them, and re-layouts, to_wire(): return rows.reshape(*lead, -1, 128)  11.4 us
    ppermute x2, starting transfers between devices, passed_along(): return lax.ppermute(value, axis, pairs)  10.3 us
  transfers between devices with their start and end apart: 6, of which 3 were waited for; matrix products, arithmetic and copies ran while one was open for 14% of the time, Pallas kernels for 19%

profile of v12, /device:TPU:1, one launch (start us, length us, event | category | flops | bytes accessed | tf_op | source)
XLA Modules:
  0.0 378.9 jit_solution(15657883230406066300)
XLA Ops:
  7.2 0.0 copy-start
  7.2 0.0 reduce-scatter.3.cloned.1.call-start
  7.2 0.9 copy.29
  8.1 0.1 eq.58
  8.3 0.8 copy.31
  9.0 0.1 eq.65
  9.2 0.1 fusion.27
  9.3 0.2 reduce_window_sum.18
  9.4 0.2 select_reduce_fusion.2
  9.6 0.1 reduce_sum.87
  9.8 0.1 copy.32
  9.8 0.7 bitcast_add_fusion
  10.5 0.1 fusion.28
  10.6 0.2 reduce_window_sum.17
  10.8 0.2 select_reduce_fusion.3
  11.0 0.1 reduce_sum.83
  11.1 0.1 copy.30
  11.2 0.7 bitcast_add_fusion.1
  11.9 0.8 select_reduce_fusion
  12.7 0.0 copy-start.6
  12.7 0.0 copy-start.3
  12.7 2.2 convolution_convert_fusion.2
  14.9 2.3 reshape.90.refs_2_
  17.2 0.7 convert_reduce_fusion.1
  17.9 0.5 convolution_convert_fusion.4
  18.4 2.3 reshape.88.refs_0_
  20.7 1.5 convolution_convert_fusion.3
  22.2 2.3 reshape.89.refs_1_
  24.5 134.8 %shard_map.120 = (bf16[2,2,8,560,128]{4,3,2,1,0:T(8,128)(2,1)}, bf16[2,2,8,560,128]{4,3,2,1,0:T(8,128)(2,1)}, bf16[2,2,8,560,128]{4,3,2,1,0:T(8,128)(2,1)}) custom-call(bf16[8,560,128]{2,1,0:T(8,128)(2,1)} %reshape.88.refs_0_, bf16[8,560,128]{2,1,0:T(8,128)(2,1)} %reshape.89.refs_1_, bf16[8,560,128]{2,1,0:T(8,128)(2,1)} %reshape.90.refs_2_), custom_call_target="tpu_custom_call" | custom-call | tf_op jit(solution)/shard_map/pallas_call | solution.py:144
  159.3 9.0 %reshape.91 = bf16[640,3584]{1,0:T(8,128)(2,1)} reshape(bf16[2,2,8,560,128]{4,3,2,1,0:T(8,128)(2,1)} %get-tuple-element.7) | data formatting | bytes 9175040 | tf_op jit(solution)/shard_map/reshape | solution.py:273
  168.3 9.8 %convolution_convert_fusion.1 = bf16[640,3584]{1,0:T(8,128)(2,1)} fusion(bf16[1,1,256,3584]{3,2,1,0:T(8,128)(2,1)} %param.17, bf16[640,3584]{1,0:T(8,128)(2,1)} %reshape.91, bf16[1,1,3584,256]{3,2,1,0:T(8,128)(2,1)S(1)} %copy-done), kind=kOutput, calls=%fused_computation.1 | convolution fusion | flops 2351923200 | bytes 12845056 | tf_op jit(solution)/shard_map/...f,fd->...d/dot_general | solution.py:233
  178.1 0.0 reduce-scatter.3.cloned.1.call-update
  178.2 0.2 reduce-scatter.5.cloned.1.call-start
  178.4 9.0 %reshape.95 = bf16[640,3584]{1,0:T(8,128)(2,1)} reshape(bf16[2,2,8,560,128]{4,3,2,1,0:T(8,128)(2,1)} %get-tuple-element.8) | data formatting | bytes 9175040 | tf_op jit(solution)/shard_map/reshape | solution.py:273
  187.4 9.4 %reshape.96 = bf16[640,3584]{1,0:T(8,128)(2,1)} reshape(bf16[2,2,8,560,128]{4,3,2,1,0:T(8,128)(2,1)} %get-tuple-element.9) | data formatting | bytes 9175040 | tf_op jit(solution)/shard_map/reshape | solution.py:273
  196.8 4.0 %fusion.8 = f32[640,256]{1,0:T(8,128)S(1)} fusion(bf16[640,3584]{1,0:T(8,128)(2,1)} %reshape.96, bf16[1,1,3584,256]{3,2,1,0:T(8,128)(2,1)S(1)} %copy-done), kind=kOutput, calls=%fused_computation.17 | convolution fusion | flops 1174405120 | bytes 7077888 | tf_op jit(solution)/shard_map/...d,df->...f/dot_general | solution.py:239
  200.9 0.5 copy-done.7
  201.3 1.4 fusion.15
  202.7 3.5 convolution_convert_fusion
  206.3 0.0 reduce-scatter.5.cloned.1.call-update
  206.3 0.0 reduce-scatter.3.cloned.1.call-done
  206.3 4.9 %all-to-all-start = ((bf16[2,160,3584]{2,1,0:T(8,128)(2,1)}), bf16[2,160,3584]{2,1,0:T(8,128)(2,1)}, u32[]{:S(2)}, u32[]{:S(2)}) async-start(bf16[2,160,3584]{2,1,0:T(8,128)(2,1)} %bitcast.75), calls=%async_computation.1 | async-start | bytes 4587520 | tf_op jit(solution)/shard_map/all_to_all | solution.py:225
  211.2 15.3 %reduce-scatter.5.cloned.1.call-done = bf16[1,2,160,3584]{3,2,1,0:T(8,128)(2,1)} async-done(((bf16[2,2,160,3584]{3,2,1,0:T(8,128)(2,1)}), bf16[1,2,160,3584]{3,2,1,0:T(8,128)(2,1)}) %reduce-scatter.5.cloned.1.call-update) | async-done | bytes 2293776 | tf_op jit(solution)/shard_map/reduce_scatter | solution.py:223
  226.5 12.3 %all-to-all-done = bf16[2,160,3584]{2,1,0:T(8,128)(2,1)} async-done(((bf16[2,160,3584]{2,1,0:T(8,128)(2,1)}), bf16[2,160,3584]{2,1,0:T(8,128)(2,1)}, u32[]{:S(2)}, u32[]{:S(2)}) %all-to-all-start) | async-done | bytes 2293792 | tf_op jit(solution)/shard_map/all_to_all | solution.py:225
  238.8 4.9 %all-to-all-start.1 = ((bf16[2,160,3584]{2,1,0:T(8,128)(2,1)}), bf16[2,160,3584]{2,1,0:T(8,128)(2,1)}, u32[]{:S(2)}, u32[]{:S(2)}) async-start(bf16[2,160,3584]{2,1,0:T(8,128)(2,1)} %bitcast.74), calls=%async_computation.3 | async-start | bytes 4587520 | tf_op jit(solution)/shard_map/all_to_all | solution.py:225
  243.7 5.8 %convolution_bitcast_fusion.1 = f32[1,1,3584,256]{3,2,1,0:T(8,128)} fusion(bf16[640,3584]{1,0:T(8,128)(2,1)} %reshape.96, bf16[640,256]{1,0:T(8,128)(2,1)S(1)} %fusion.15), kind=kOutput, calls=%fused_computation.3 | convolution fusion | flops 1174405120 | bytes 8585216 | tf_op jit(solution)/shard_map/rd,rf->df/dot_general | solution.py:246
  249.5 2.1 reduce_sum.90
  251.6 2.3 reshape.94.refs_0_
  253.9 26.8 %shard_map.121 = bf16[1,8,560,128]{3,2,1,0:T(8,128)(2,1)} custom-call(bf16[8,560,128]{2,1,0:T(8,128)(2,1)} %reshape.94.refs_0_), custom_call_target="tpu_custom_call" | custom-call | tf_op jit(solution)/shard_map/pallas_call | solution.py:210
  280.7 2.4 reshape_squeeze.8
  283.1 1.4 fusion.3
  284.5 6.4 %collective-permute-start = (bf16[1,64,3584]{2,1,0:T(8,128)(2,1)}, bf16[1,64,3584]{2,1,0:T(8,128)(2,1)S(1)}, u32[]{:S(2)}, u32[]{:S(2)}) collective-permute-start(bf16[1,64,3584]{2,1,0:T(8,128)(2,1)} %fusion.3), channel_id=1, source_target_pairs={{0,32},{32,64},{64,96},{96,128},{128,160},{160,192},{192,224},{224... | collective-permute-start | bytes 1376264 | tf_op jit(solution)/shard_map/ppermute | solution.py:18
  290.9 0.0 all-to-all-done.1
  290.9 2.1 reduce_sum.91
  293.0 2.3 reshape.99.refs_0_
  295.3 46.6 %shard_map.122 = bf16[1,8,560,128]{3,2,1,0:T(8,128)(2,1)} custom-call(bf16[8,560,128]{2,1,0:T(8,128)(2,1)} %reshape.99.refs_0_), custom_call_target="tpu_custom_call" | custom-call | tf_op jit(solution)/shard_map/pallas_call | solution.py:210
  341.9 2.4 reshape_squeeze.9
  344.3 0.6 fusion.2
  344.9 3.9 %collective-permute-start.1 = (bf16[1,64,3584]{2,1,0:T(8,128)(2,1)S(1)}, bf16[1,64,3584]{2,1,0:T(8,128)(2,1)S(1)}, u32[]{:S(2)}, u32[]{:S(2)}) collective-permute-start(bf16[1,64,3584]{2,1,0:T(8,128)(2,1)S(1)} %fusion.2), channel_id=1, source_target_pairs={{0,224},{32,0},{64,32},{96,64},{128,96},{160,128},{192,160},{224,1... | collective-permute-start | bytes 1376264 | tf_op jit(solution)/shard_map/ppermute | solution.py:18
  348.8 5.9 %convolution_bitcast_fusion = f32[1,1,256,3584]{3,2,1,0:T(8,128)} fusion(bf16[640,3584]{1,0:T(8,128)(2,1)} %reshape.95, f32[640,256]{1,0:T(8,128)S(1)} %fusion.8), kind=kOutput, calls=%fused_computation.2 | convolution fusion | flops 1175224320 | bytes 8912896 | tf_op jit(solution)/shard_map/rf,rd->fd/dot_general | solution.py:247
  354.7 0.0 collective-permute-done
  354.7 15.8 %collective-permute-done.1 = bf16[1,64,3584]{2,1,0:T(8,128)(2,1)S(1)} collective-permute-done((bf16[1,64,3584]{2,1,0:T(8,128)(2,1)S(1)}, bf16[1,64,3584]{2,1,0:T(8,128)(2,1)S(1)}, u32[]{:S(2)}, u32[]{:S(2)}) %collective-permute-start.1) | collective-permute-done | bytes 458784 | tf_op jit(solution)/shard_map/ppermute | solution.py:18
  370.5 0.8 copy.35
  371.3 0.8 copy.36
  (12 shorter events, 0.0 us)
Async XLA Ops:
  7.2 161.2 %copy-start = (bf16[1,1,3584,256]{3,2,1,0:T(8,128)(2,1)S(1)}, bf16[1,1,3584,256]{3,2,1,0:T(8,128)(2,1)}, u32[]{:S(2)}) copy-start(bf16[1,1,3584,256]{3,2,1,0:T(8,128)(2,1)} %param.16) | copy-start | bytes 5505028
  7.2 199.1 %reduce-scatter.3.cloned.1.call-start = ((), (), s32[]{:S(2)}) async-start(), calls=%async_computation.4 | async-start | bytes 6881280 | tf_op jit(solution)/shard_map/reduce_scatter | solution.py:223
  12.7 4.5 %copy-start.6 = (f32[1,64,2]{1,2,0:T(2,128)S(1)}, f32[1,64,2]{1,2,0:T(2,128)}, u32[]{:S(2)}) copy-start(f32[1,64,2]{1,2,0:T(2,128)} %param.11) | copy-start | bytes 1540
  12.7 5.2 %copy-start.3 = (bf16[1,64,3584]{2,1,0:T(8,128)(2,1)S(1)}, bf16[1,64,3584]{2,1,0:T(8,128)(2,1)}, u32[]{:S(2)}) copy-start(bf16[1,64,3584]{2,1,0:T(8,128)(2,1)} %param.9) | copy-start | bytes 1376260
  178.2 48.3 %reduce-scatter.5.cloned.1.call-start = ((), (), s32[]{:S(2)}) async-start(), calls=%async_computation.5 | async-start | bytes 6881280 | tf_op jit(solution)/shard_map/reduce_scatter | solution.py:223
  196.8 4.0 %copy-start.2 = (bf16[640,3584]{1,0:T(8,128)(2,1)S(1)}, bf16[640,3584]{1,0:T(8,128)(2,1)}, u32[]{:S(2)}) copy-start(bf16[640,3584]{1,0:T(8,128)(2,1)} %reshape.95) | copy-start | bytes 13762564
  196.8 4.5 %copy-start.7 = (bf16[1,1,256,3584]{3,2,1,0:T(8,128)(2,1)S(1)}, bf16[1,1,256,3584]{3,2,1,0:T(8,128)(2,1)}, u32[]{:S(2)}) copy-start(bf16[1,1,256,3584]{3,2,1,0:T(8,128)(2,1)} %param.17) | copy-start | bytes 5505028
  206.3 32.5 %all-to-all-start = ((bf16[2,160,3584]{2,1,0:T(8,128)(2,1)}), bf16[2,160,3584]{2,1,0:T(8,128)(2,1)}, u32[]{:S(2)}, u32[]{:S(2)}) async-start(bf16[2,160,3584]{2,1,0:T(8,128)(2,1)} %bitcast.75), calls=%async_computation.1 | async-start | bytes 4587520 | tf_op jit(solution)/shard_map/all_to_all | solution.py:225
  238.8 52.1 %all-to-all-start.1 = ((bf16[2,160,3584]{2,1,0:T(8,128)(2,1)}), bf16[2,160,3584]{2,1,0:T(8,128)(2,1)}, u32[]{:S(2)}, u32[]{:S(2)}) async-start(bf16[2,160,3584]{2,1,0:T(8,128)(2,1)} %bitcast.74), calls=%async_computation.3 | async-start | bytes 4587520 | tf_op jit(solution)/shard_map/all_to_all | solution.py:225
  253.9 29.2 %copy-start.5 = (f32[64,160]{1,0:T(8,128)S(1)}, f32[64,160]{1,0:T(8,128)}, u32[]{:S(2)}) copy-start(f32[64,160]{1,0:T(8,128)} %get-tuple-element.13) | copy-start | bytes 122884
  284.5 70.2 %collective-permute-start = (bf16[1,64,3584]{2,1,0:T(8,128)(2,1)}, bf16[1,64,3584]{2,1,0:T(8,128)(2,1)S(1)}, u32[]{:S(2)}, u32[]{:S(2)}) collective-permute-start(bf16[1,64,3584]{2,1,0:T(8,128)(2,1)} %fusion.3), channel_id=1, source_target_pairs={{0,32},{32,64},{64,96},{96,128},{128,160},{160,192},{192,224},{224... | collective-permute-start | bytes 1376264 | tf_op jit(solution)/shard_map/ppermute | solution.py:18
  295.3 49.0 %copy-start.4 = (bf16[1,64,3584]{2,1,0:T(8,128)(2,1)S(1)}, bf16[1,64,3584]{2,1,0:T(8,128)(2,1)}, u32[]{:S(2)}) copy-start(bf16[1,64,3584]{2,1,0:T(8,128)(2,1)} %param.15) | copy-start | bytes 1376260
  344.9 25.6 %collective-permute-start.1 = (bf16[1,64,3584]{2,1,0:T(8,128)(2,1)S(1)}, bf16[1,64,3584]{2,1,0:T(8,128)(2,1)S(1)}, u32[]{:S(2)}, u32[]{:S(2)}) collective-permute-start(bf16[1,64,3584]{2,1,0:T(8,128)(2,1)S(1)} %fusion.2), channel_id=1, source_target_pairs={{0,224},{32,0},{64,32},{96,64},{128,96},{160,128},{192,160},{224,1... | collective-permute-start | bytes 1376264 | tf_op jit(solution)/shard_map/ppermute | solution.py:18
  348.8 23.2 %copy-start.1 = (bf16[1,1,3584,256]{3,2,1,0:T(8,128)(2,1)S(1)}, bf16[1,1,3584,256]{3,2,1,0:T(8,128)(2,1)}, u32[]{:S(2)}) copy-start(bf16[1,1,3584,256]{3,2,1,0:T(8,128)(2,1)} %param.16) | copy-start | bytes 5505028
Sparse Core Ops, SparseCore 0:
  178.3 20.3 reduce-scatter.2
  206.4 20.0 reduce-scatter.4

commit v13 on v12

--- a/solution.py
+++ b/solution.py
@@ -222,8 +222,8 @@
     blocks = parts.reshape(2, 2, -1, model_width)
     pair = lax.psum_scatter(blocks, "ec", scatter_dimension=0, tiled=True)
     pair = pair.reshape(blocks.shape[1:])
-    other = lax.all_to_all(pair, "ez", split_axis=0, concat_axis=0, tiled=True)
-    summed = jnp.sum(other.astype(jnp.float32), axis=0).astype(jnp.bfloat16)
+    summed = lax.psum_scatter(pair, "ez", scatter_dimension=0, tiled=True)
+    summed = summed.reshape(pair.shape[1:])
     return to_wire(summed, experts)
 
 

time: 380 us -> 414 us (1.089)
  waiting for transfers between devices: 43.4 us -> 101 us
  Pallas kernels: 208 us -> 196 us
  starting transfers between devices: 20.4 us -> 10.6 us
  other arithmetic: 8.04 us -> 3.77 us
    reduce_scatter x0 -> x2, waiting for transfers between devices: none -> 68.7 us  [group_sum(): summed = lax.psum_scatter(pair, 'ez', scatter_dimension=0, tiled=True)]
    all_to_all x2 -> x0, waiting for transfers between devices: 12.3 us -> none  [group_sum(): other = lax.all_to_all(pair, 'ez', split_axis=0, concat_axis=0, tiled=True)]
    pallas_call x2, Pallas kernels: 73.4 us -> 61.3 us  [send_home(): pl.pallas_call(functools.partial(return_kernel, groups), out_shape=jax.Sh...]
    all_to_all x2 -> x0, starting transfers between devices: 9.81 us -> none  [group_sum(): other = lax.all_to_all(pair, 'ez', split_axis=0, concat_axis=0, tiled=True)]
    another operation x0 -> x2, local copies, waits for them, and re-layouts: none -> 6.65 us  [to_wire(): return rows.reshape(*lead, -1, 128)]
    reshape x5 -> x3, local copies, waits for them, and re-layouts: 11.4 us -> 6.86 us  [to_wire(): return rows.reshape(*lead, -1, 128)]
    reduce_sum x2 -> x0, other arithmetic: 4.26 us -> none  [group_sum(): summed = jnp.sum(other.astype(jnp.float32), axis=0).astype(jnp.bfloat16)]
    reduce_scatter x2, waiting for transfers between devices: 15.3 us -> 19.5 us  [group_sum(): pair = lax.psum_scatter(blocks, 'ec', scatter_dimension=0, tiled=True)]
  transfers between devices with their start and end apart: 6 -> 6, of which waited for: 3 -> 4; matrix products, arithmetic and copies ran while one was open for 14% -> 13% of each run, Pallas kernels for 19% -> 15%
where the time goes in v13:
time: 414 us; the launch traced here: 412 us
  Pallas kernels  196 us (47%)
  waiting for transfers between devices  101 us (24%)
  local copies, waits for them, and re-layouts  50.1 us (12%)
  matrix products  36.6 us (9%)
  between operations  14 us (3%)
  starting transfers between devices  10.6 us (3%)
    pallas_call x1, Pallas kernels, dispatch(): pl.pallas_call(functools.partial(dispatch_kernel, groups), out_shape=[jax...  135 us
    reduce_scatter x2, waiting for transfers between devices, group_sum(): summed = lax.psum_scatter(pair, 'ez', scatter_dimension=0, tiled=True)  68.7 us
    pallas_call x2, Pallas kernels, send_home(): pl.pallas_call(functools.partial(return_kernel, groups), out_shape=jax.Sh...  61.3 us
    reshape x3, local copies, waits for them, and re-layouts, local(): got[index].reshape(-1, model_width)  27.4 us
    reduce_scatter x2, waiting for transfers between devices, group_sum(): pair = lax.psum_scatter(blocks, 'ec', scatter_dimension=0, tiled=True)  19.5 us
    ppermute x2, waiting for transfers between devices, passed_along(): return lax.ppermute(value, axis, pairs)  12.1 us
    ppermute x2, starting transfers between devices, passed_along(): return lax.ppermute(value, axis, pairs)  10.3 us
    dot_general x1, matrix products, expert_forward(): jnp.einsum('...f,fd->...d', act, down_proj, preferred_element_type=jnp.fl...  9.82 us
  transfers between devices with their start and end apart: 6, of which 4 were waited for; matrix products, arithmetic and copies ran while one was open for 13% of the time, Pallas kernels for 15%

profile of v13, /device:TPU:1, one launch (start us, length us, event | category | flops | bytes accessed | tf_op | source)
XLA Modules:
  0.0 412.1 jit_solution(4641922712923745756)
XLA Ops:
  7.2 0.0 copy-start
  7.2 0.0 reduce-scatter.5.cloned.1.call-start
  7.2 0.9 copy.29
  8.1 0.1 eq.58
  8.3 0.8 copy.31
  9.0 0.1 eq.65
  9.2 0.1 fusion.27
  9.3 0.2 reduce_window_sum.18
  9.4 0.2 select_reduce_fusion.2
  9.6 0.1 reduce_sum.63
  9.8 0.1 copy.32
  9.8 0.7 bitcast_add_fusion
  10.5 0.1 fusion.28
  10.6 0.2 reduce_window_sum.17
  10.8 0.2 select_reduce_fusion.3
  11.0 0.1 reduce_sum.59
  11.1 0.1 copy.30
  11.2 0.7 bitcast_add_fusion.1
  11.9 0.8 select_reduce_fusion
  12.7 0.0 copy-start.6
  12.7 0.0 copy-start.3
  12.7 2.2 convolution_convert_fusion.2
  14.9 2.3 reshape.84.refs_2_
  17.2 0.7 convert_reduce_fusion.1
  17.9 0.5 convolution_convert_fusion.4
  18.4 2.3 reshape.82.refs_0_
  20.7 1.5 convolution_convert_fusion.3
  22.2 2.3 reshape.83.refs_1_
  24.5 134.8 %shard_map.120 = (bf16[2,2,8,560,128]{4,3,2,1,0:T(8,128)(2,1)}, bf16[2,2,8,560,128]{4,3,2,1,0:T(8,128)(2,1)}, bf16[2,2,8,560,128]{4,3,2,1,0:T(8,128)(2,1)}) custom-call(bf16[8,560,128]{2,1,0:T(8,128)(2,1)} %reshape.82.refs_0_, bf16[8,560,128]{2,1,0:T(8,128)(2,1)} %reshape.83.refs_1_, bf16[8,560,128]{2,1,0:T(8,128)(2,1)} %reshape.84.refs_2_), custom_call_target="tpu_custom_call" | custom-call | tf_op jit(solution)/shard_map/pallas_call | solution.py:144
  159.3 9.0 %reshape.85 = bf16[640,3584]{1,0:T(8,128)(2,1)} reshape(bf16[2,2,8,560,128]{4,3,2,1,0:T(8,128)(2,1)} %get-tuple-element.7) | data formatting | bytes 9175040 | tf_op jit(solution)/shard_map/reshape | solution.py:273
  168.3 9.8 %convolution_convert_fusion.1 = bf16[640,3584]{1,0:T(8,128)(2,1)} fusion(bf16[1,1,256,3584]{3,2,1,0:T(8,128)(2,1)} %param.17, bf16[640,3584]{1,0:T(8,128)(2,1)} %reshape.85, bf16[1,1,3584,256]{3,2,1,0:T(8,128)(2,1)S(1)} %copy-done), kind=kOutput, calls=%fused_computation.1 | convolution fusion | flops 2351923200 | bytes 12845056 | tf_op jit(solution)/shard_map/...f,fd->...d/dot_general | solution.py:233
  178.1 0.0 reduce-scatter.5.cloned.1.call-update
  178.2 0.2 reduce-scatter.9.cloned.1.call-start
  178.4 9.0 %reshape.88 = bf16[640,3584]{1,0:T(8,128)(2,1)} reshape(bf16[2,2,8,560,128]{4,3,2,1,0:T(8,128)(2,1)} %get-tuple-element.8) | data formatting | bytes 9175040 | tf_op jit(solution)/shard_map/reshape | solution.py:273
  187.4 9.4 %reshape.89 = bf16[640,3584]{1,0:T(8,128)(2,1)} reshape(bf16[2,2,8,560,128]{4,3,2,1,0:T(8,128)(2,1)} %get-tuple-element.9) | data formatting | bytes 9175040 | tf_op jit(solution)/shard_map/reshape | solution.py:273
  196.8 4.0 fusion.8
  200.9 0.5 copy-done.7
  201.3 1.4 fusion.15
  202.7 3.5 convolution_convert_fusion
  206.3 0.0 reduce-scatter.9.cloned.1.call-update
  206.3 0.0 reduce-scatter.7.cloned.1.call-start
  206.3 0.0 reduce-scatter.5.cloned.1.call-done
  206.4 0.7 reduce-scatter.7.cloned.1.call-update
  207.0 0.0 reduce-scatter.11.cloned.1.call-start
  207.1 19.4 %reduce-scatter.9.cloned.1.call-done = bf16[1,2,160,3584]{3,2,1,0:T(8,128)(2,1)} async-done(((bf16[2,2,160,3584]{3,2,1,0:T(8,128)(2,1)}), bf16[1,2,160,3584]{3,2,1,0:T(8,128)(2,1)}) %reduce-scatter.9.cloned.1.call-update) | async-done | bytes 2293776 | tf_op jit(solution)/shard_map/reduce_scatter | solution.py:223
  226.5 0.0 reduce-scatter.11.cloned.1.call-update
  226.5 5.8 %convolution_bitcast_fusion.1 = f32[1,1,3584,256]{3,2,1,0:T(8,128)} fusion(bf16[640,3584]{1,0:T(8,128)(2,1)} %reshape.89, bf16[640,256]{1,0:T(8,128)(2,1)S(1)} %fusion.15), kind=kOutput, calls=%fused_computation.3 | convolution fusion | flops 1174405120 | bytes 8585216 | tf_op jit(solution)/shard_map/rd,rf->df/dot_general | solution.py:246
  232.3 36.6 %reduce-scatter.7.cloned.1.call-done = bf16[1,160,3584]{2,1,0:T(8,128)(2,1)} async-done(((bf16[2,160,3584]{2,1,0:T(8,128)(2,1)}), bf16[1,160,3584]{2,1,0:T(8,128)(2,1)}) %reduce-scatter.7.cloned.1.call-update) | async-done | bytes 1146896 | tf_op jit(solution)/shard_map/reduce_scatter | solution.py:225
  268.9 3.3 reshape_reshape.6.refs_0_
  272.3 31.1 %shard_map.121 = bf16[1,8,560,128]{3,2,1,0:T(8,128)(2,1)} custom-call(bf16[8,560,128]{2,1,0:T(8,128)(2,1)} %reshape_reshape.6.refs_0_), custom_call_target="tpu_custom_call" | custom-call | tf_op jit(solution)/shard_map/pallas_call | solution.py:210
  303.4 2.4 reshape_squeeze.8
  305.8 1.4 fusion.3
  307.1 3.7 collective-permute-start
  310.8 32.1 %reduce-scatter.11.cloned.1.call-done = bf16[1,160,3584]{2,1,0:T(8,128)(2,1)} async-done(((bf16[2,160,3584]{2,1,0:T(8,128)(2,1)}), bf16[1,160,3584]{2,1,0:T(8,128)(2,1)}) %reduce-scatter.11.cloned.1.call-update) | async-done | bytes 1146896 | tf_op jit(solution)/shard_map/reduce_scatter | solution.py:225
  342.9 3.3 reshape_reshape.7.refs_0_
  346.2 30.2 %shard_map.122 = bf16[1,8,560,128]{3,2,1,0:T(8,128)(2,1)} custom-call(bf16[8,560,128]{2,1,0:T(8,128)(2,1)} %reshape_reshape.7.refs_0_), custom_call_target="tpu_custom_call" | custom-call | tf_op jit(solution)/shard_map/pallas_call | solution.py:210
  376.4 2.4 reshape_squeeze.9
  378.8 0.6 fusion.2
  379.4 6.6 %collective-permute-start.1 = (bf16[1,64,3584]{2,1,0:T(8,128)(2,1)S(1)}, bf16[1,64,3584]{2,1,0:T(8,128)(2,1)S(1)}, u32[]{:S(2)}, u32[]{:S(2)}) collective-permute-start(bf16[1,64,3584]{2,1,0:T(8,128)(2,1)S(1)} %fusion.2), channel_id=1, source_target_pairs={{0,224},{32,0},{64,32},{96,64},{128,96},{160,128},{192,160},{224,1... | collective-permute-start | bytes 1376264 | tf_op jit(solution)/shard_map/ppermute | solution.py:18
  386.1 5.9 %convolution_bitcast_fusion = f32[1,1,256,3584]{3,2,1,0:T(8,128)} fusion(bf16[640,3584]{1,0:T(8,128)(2,1)} %reshape.88, f32[640,256]{1,0:T(8,128)S(1)} %fusion.8), kind=kOutput, calls=%fused_computation.2 | convolution fusion | flops 1175224320 | bytes 8912896 | tf_op jit(solution)/shard_map/rf,rd->fd/dot_general | solution.py:247
  392.0 0.0 collective-permute-done
  392.0 12.1 %collective-permute-done.1 = bf16[1,64,3584]{2,1,0:T(8,128)(2,1)S(1)} collective-permute-done((bf16[1,64,3584]{2,1,0:T(8,128)(2,1)S(1)}, bf16[1,64,3584]{2,1,0:T(8,128)(2,1)S(1)}, u32[]{:S(2)}, u32[]{:S(2)}) %collective-permute-start.1) | collective-permute-done | bytes 458784 | tf_op jit(solution)/shard_map/ppermute | solution.py:18
  404.1 0.8 copy.35
  404.8 0.8 copy.36
  (12 shorter events, 0.0 us)
Async XLA Ops:
  7.2 161.2 %copy-start = (bf16[1,1,3584,256]{3,2,1,0:T(8,128)(2,1)S(1)}, bf16[1,1,3584,256]{3,2,1,0:T(8,128)(2,1)}, u32[]{:S(2)}) copy-start(bf16[1,1,3584,256]{3,2,1,0:T(8,128)(2,1)} %param.16) | copy-start | bytes 5505028
  7.2 199.2 %reduce-scatter.5.cloned.1.call-start = ((), (), s32[]{:S(2)}) async-start(), calls=%async_computation.4 | async-start | bytes 6881280 | tf_op jit(solution)/shard_map/reduce_scatter | solution.py:223
  12.7 4.5 %copy-start.6 = (f32[1,64,2]{1,2,0:T(2,128)S(1)}, f32[1,64,2]{1,2,0:T(2,128)}, u32[]{:S(2)}) copy-start(f32[1,64,2]{1,2,0:T(2,128)} %param.11) | copy-start | bytes 1540
  12.7 5.2 %copy-start.3 = (bf16[1,64,3584]{2,1,0:T(8,128)(2,1)S(1)}, bf16[1,64,3584]{2,1,0:T(8,128)(2,1)}, u32[]{:S(2)}) copy-start(bf16[1,64,3584]{2,1,0:T(8,128)(2,1)} %param.9) | copy-start | bytes 1376260
  178.2 48.3 %reduce-scatter.9.cloned.1.call-start = ((), (), s32[]{:S(2)}) async-start(), calls=%async_computation.6 | async-start | bytes 6881280 | tf_op jit(solution)/shard_map/reduce_scatter | solution.py:223
  196.8 4.0 copy-start.2
  196.8 4.5 %copy-start.7 = (bf16[1,1,256,3584]{3,2,1,0:T(8,128)(2,1)S(1)}, bf16[1,1,256,3584]{3,2,1,0:T(8,128)(2,1)}, u32[]{:S(2)}) copy-start(bf16[1,1,256,3584]{3,2,1,0:T(8,128)(2,1)} %param.17) | copy-start | bytes 5505028
  206.3 62.7 %reduce-scatter.7.cloned.1.call-start = ((), (), s32[]{:S(2)}) async-start(), calls=%async_computation.5 | async-start | bytes 3440640 | tf_op jit(solution)/shard_map/reduce_scatter | solution.py:225
  207.0 135.9 %reduce-scatter.11.cloned.1.call-start = ((), (), s32[]{:S(2)}) async-start(), calls=%async_computation.7 | async-start | bytes 3440640 | tf_op jit(solution)/shard_map/reduce_scatter | solution.py:225
  272.3 33.5 %copy-start.5 = (f32[64,160]{1,0:T(8,128)S(1)}, f32[64,160]{1,0:T(8,128)}, u32[]{:S(2)}) copy-start(f32[64,160]{1,0:T(8,128)} %get-tuple-element.13) | copy-start | bytes 122884
  307.1 84.8 %collective-permute-start = (bf16[1,64,3584]{2,1,0:T(8,128)(2,1)}, bf16[1,64,3584]{2,1,0:T(8,128)(2,1)S(1)}, u32[]{:S(2)}, u32[]{:S(2)}) collective-permute-start(bf16[1,64,3584]{2,1,0:T(8,128)(2,1)} %fusion.3), channel_id=1, source_target_pairs={{0,32},{32,64},{64,96},{96,128},{128,160},{160,192},{192,224},{224... | collective-permute-start | bytes 1376264 | tf_op jit(solution)/shard_map/ppermute | solution.py:18
  346.2 32.6 %copy-start.4 = (bf16[1,64,3584]{2,1,0:T(8,128)(2,1)S(1)}, bf16[1,64,3584]{2,1,0:T(8,128)(2,1)}, u32[]{:S(2)}) copy-start(bf16[1,64,3584]{2,1,0:T(8,128)(2,1)} %param.15) | copy-start | bytes 1376260
  379.4 24.7 %collective-permute-start.1 = (bf16[1,64,3584]{2,1,0:T(8,128)(2,1)S(1)}, bf16[1,64,3584]{2,1,0:T(8,128)(2,1)S(1)}, u32[]{:S(2)}, u32[]{:S(2)}) collective-permute-start(bf16[1,64,3584]{2,1,0:T(8,128)(2,1)S(1)} %fusion.2), channel_id=1, source_target_pairs={{0,224},{32,0},{64,32},{96,64},{128,96},{160,128},{192,160},{224,1... | collective-permute-start | bytes 1376264 | tf_op jit(solution)/shard_map/ppermute | solution.py:18
  386.1 19.6 %copy-start.1 = (bf16[1,1,3584,256]{3,2,1,0:T(8,128)(2,1)S(1)}, bf16[1,1,3584,256]{3,2,1,0:T(8,128)(2,1)}, u32[]{:S(2)}) copy-start(bf16[1,1,3584,256]{3,2,1,0:T(8,128)(2,1)} %param.16) | copy-start | bytes 5505028
Sparse Core Ops, SparseCore 0:
  178.3 20.3 reduce-scatter.4
  206.4 20.0 reduce-scatter.8
  229.0 39.8 reduce-scatter.6
  271.5 71.3 reduce-scatter.10

commit v14 on v13

--- a/solution.py
+++ b/solution.py
@@ -222,8 +222,11 @@
     blocks = parts.reshape(2, 2, -1, model_width)
     pair = lax.psum_scatter(blocks, "ec", scatter_dimension=0, tiled=True)
     pair = pair.reshape(blocks.shape[1:])
-    summed = lax.psum_scatter(pair, "ez", scatter_dimension=0, tiled=True)
-    summed = summed.reshape(pair.shape[1:])
+    chip = lax.axis_index("ez")
+    keep = lax.dynamic_index_in_dim(pair, chip, axis=0, keepdims=False)
+    send = lax.dynamic_index_in_dim(pair, 1 - chip, axis=0, keepdims=False)
+    got = passed_along(send, "ez", 1)
+    summed = (keep.astype(jnp.float32) + got.astype(jnp.float32)).astype(jnp.bfloat16)
     return to_wire(summed, experts)
 
 

time: 414 us -> 368 us (0.89)
  waiting for transfers between devices: 101 us -> 32.4 us
  Pallas kernels: 196 us -> 211 us
    reduce_scatter x2 -> x0, waiting for transfers between devices: 68.7 us -> none  [group_sum(): summed = lax.psum_scatter(pair, 'ez', scatter_dimension=0, tiled=True)]
    pallas_call x2, Pallas kernels: 61.3 us -> 75.9 us  [send_home(): pl.pallas_call(functools.partial(return_kernel, groups), out_shape=jax.Sh...]
    ppermute x2 -> x4, waiting for transfers between devices: 12.1 us -> 21.1 us  [passed_along(): return lax.ppermute(value, axis, pairs)]
    reduce_scatter x2, waiting for transfers between devices: 19.5 us -> 11.3 us  [group_sum(): pair = lax.psum_scatter(blocks, 'ec', scatter_dimension=0, tiled=True)]
    another operation x2 -> x0, local copies, waits for them, and re-layouts: 6.65 us -> none  [to_wire(): return rows.reshape(*lead, -1, 128)]
    reshape x3 -> x5, local copies, waits for them, and re-layouts: 6.86 us -> 11.4 us  [to_wire(): return rows.reshape(*lead, -1, 128)]
    ppermute x2 -> x4, starting transfers between devices: 10.3 us -> 13.3 us  [passed_along(): return lax.ppermute(value, axis, pairs)]
  transfers between devices with their start and end apart: 6 -> 6, of which waited for: 4 -> 3; matrix products, arithmetic and copies ran while one was open for 13% -> 16% of each run, Pallas kernels for 15% -> 21%
where the time goes in v14:
time: 368 us; the launch traced here: 367 us
  Pallas kernels  211 us (57%)
  local copies, waits for them, and re-layouts  51.1 us (14%)
  matrix products  37.5 us (10%)
  waiting for transfers between devices  32.4 us (9%)
  between operations  14.2 us (4%)
  starting transfers between devices  13.5 us (4%)
  other arithmetic  7.12 us (2%)
    pallas_call x1, Pallas kernels, dispatch(): pl.pallas_call(functools.partial(dispatch_kernel, groups), out_shape=[jax...  135 us
    pallas_call x2, Pallas kernels, send_home(): pl.pallas_call(functools.partial(return_kernel, groups), out_shape=jax.Sh...  75.9 us
    reshape x3, local copies, waits for them, and re-layouts, local(): got[index].reshape(-1, model_width)  27.4 us
    ppermute x4, waiting for transfers between devices, passed_along(): return lax.ppermute(value, axis, pairs)  21.1 us
    ppermute x4, starting transfers between devices, passed_along(): return lax.ppermute(value, axis, pairs)  13.3 us
    reshape x5, local copies, waits for them, and re-layouts, to_wire(): return rows.reshape(*lead, -1, 128)  11.4 us
    reduce_scatter x2, waiting for transfers between devices, group_sum(): pair = lax.psum_scatter(blocks, 'ec', scatter_dimension=0, tiled=True)  11.3 us
    dot_general x1, matrix products, expert_forward(): jnp.einsum('...f,fd->...d', act, down_proj, preferred_element_type=jnp.fl...  9.82 us
  transfers between devices with their start and end apart: 6, of which 3 were waited for; matrix products, arithmetic and copies ran while one was open for 16% of the time, Pallas kernels for 21%

profile of v14, /device:TPU:1, one launch (start us, length us, event | category | flops | bytes accessed | tf_op | source)
XLA Modules:
  0.0 366.6 jit_solution(3396422304182223373)
XLA Ops:
  7.2 0.0 copy-start
  7.2 0.0 reduce-scatter.3.cloned.1.call-start
  7.2 0.9 copy.29
  8.1 0.1 eq.58
  8.3 0.1 fusion.30
  8.4 0.2 reduce_window_sum.17
  8.5 0.2 select_reduce_fusion.3
  8.7 0.1 reduce_sum.59
  8.9 0.1 copy.30
  8.9 0.7 bitcast_add_fusion.1
  9.6 1.4 convert_reduce_fusion.1
  11.0 1.5 convolution_convert_fusion.4
  12.6 2.3 reshape.96.refs_0_
  14.9 0.1 copy.31
  14.9 0.1 eq.65
  15.1 0.1 fusion.29
  15.2 0.2 reduce_window_sum.18
  15.4 0.2 select_reduce_fusion.2
  15.5 0.1 reduce_sum.63
  15.7 0.1 copy.32
  15.8 0.0 copy-done.8
  15.8 0.7 select_reduce_fusion
  16.5 1.5 convolution_convert_fusion.3
  18.1 2.3 reshape.97.refs_1_
  20.4 1.9 convolution_convert_fusion.2
  22.3 2.3 reshape.98.refs_2_
  24.6 134.8 %shard_map.120 = (bf16[2,2,8,560,128]{4,3,2,1,0:T(8,128)(2,1)}, bf16[2,2,8,560,128]{4,3,2,1,0:T(8,128)(2,1)}, bf16[2,2,8,560,128]{4,3,2,1,0:T(8,128)(2,1)}) custom-call(bf16[8,560,128]{2,1,0:T(8,128)(2,1)} %reshape.96.refs_0_, bf16[8,560,128]{2,1,0:T(8,128)(2,1)} %reshape.97.refs_1_, bf16[8,560,128]{2,1,0:T(8,128)(2,1)} %reshape.98.refs_2_), custom_call_target="tpu_custom_call" | custom-call | tf_op jit(solution)/shard_map/pallas_call | solution.py:144
  159.4 9.0 %reshape.99 = bf16[640,3584]{1,0:T(8,128)(2,1)} reshape(bf16[2,2,8,560,128]{4,3,2,1,0:T(8,128)(2,1)} %get-tuple-element.7) | data formatting | bytes 9175040 | tf_op jit(solution)/shard_map/reshape | solution.py:276
  168.4 9.8 %convolution_convert_fusion.1 = bf16[640,3584]{1,0:T(8,128)(2,1)} fusion(bf16[1,1,256,3584]{3,2,1,0:T(8,128)(2,1)} %param.17, bf16[640,3584]{1,0:T(8,128)(2,1)} %reshape.99, bf16[1,1,3584,256]{3,2,1,0:T(8,128)(2,1)S(1)} %copy-done), kind=kOutput, calls=%fused_computation.1 | convolution fusion | flops 2351923200 | bytes 12845056 | tf_op jit(solution)/shard_map/...f,fd->...d/dot_general | solution.py:236
  178.3 0.0 reduce-scatter.3.cloned.1.call-update
  178.3 0.2 reduce-scatter.5.cloned.1.call-start
  178.5 9.0 %reshape.102 = bf16[640,3584]{1,0:T(8,128)(2,1)} reshape(bf16[2,2,8,560,128]{4,3,2,1,0:T(8,128)(2,1)} %get-tuple-element.8) | data formatting | bytes 9175040 | tf_op jit(solution)/shard_map/reshape | solution.py:276
  187.5 9.4 %reshape.103 = bf16[640,3584]{1,0:T(8,128)(2,1)} reshape(bf16[2,2,8,560,128]{4,3,2,1,0:T(8,128)(2,1)} %get-tuple-element.9) | data formatting | bytes 9175040 | tf_op jit(solution)/shard_map/reshape | solution.py:276
  196.9 4.0 %fusion.10 = f32[640,256]{1,0:T(8,128)S(1)} fusion(bf16[640,3584]{1,0:T(8,128)(2,1)} %reshape.103, bf16[1,1,3584,256]{3,2,1,0:T(8,128)(2,1)S(1)} %copy-done), kind=kOutput, calls=%fused_computation.21 | convolution fusion | flops 1174405120 | bytes 7077888 | tf_op jit(solution)/shard_map/...d,df->...f/dot_general | solution.py:242
  201.0 0.5 copy-done.9
  201.4 1.4 fusion.17
  202.8 3.5 convolution_convert_fusion
  206.4 0.0 reduce-scatter.5.cloned.1.call-update
  206.4 0.0 reduce-scatter.3.cloned.1.call-done
  206.4 1.3 dynamic-slice_bitcast_fusion.1
  207.8 1.8 collective-permute-start
  209.6 5.8 %convolution_bitcast_fusion.1 = f32[1,1,3584,256]{3,2,1,0:T(8,128)} fusion(bf16[640,3584]{1,0:T(8,128)(2,1)} %reshape.103, bf16[640,256]{1,0:T(8,128)(2,1)S(1)} %fusion.17), kind=kOutput, calls=%fused_computation.3 | convolution fusion | flops 1174405120 | bytes 8585216 | tf_op jit(solution)/shard_map/rd,rf->df/dot_general | solution.py:249
  215.4 11.3 %reduce-scatter.5.cloned.1.call-done = bf16[1,2,160,3584]{3,2,1,0:T(8,128)(2,1)} async-done(((bf16[2,2,160,3584]{3,2,1,0:T(8,128)(2,1)}), bf16[1,2,160,3584]{3,2,1,0:T(8,128)(2,1)}) %reduce-scatter.5.cloned.1.call-update) | async-done | bytes 2293776 | tf_op jit(solution)/shard_map/reduce_scatter | solution.py:223
  226.6 2.5 dynamic-slice_bitcast_fusion
  229.1 1.2 collective-permute-start.2
  230.3 4.9 %collective-permute-done = bf16[160,3584]{1,0:T(8,128)(2,1)} collective-permute-done((bf16[160,3584]{1,0:T(8,128)(2,1)S(1)}, bf16[160,3584]{1,0:T(8,128)(2,1)}, u32[]{:S(2)}, u32[]{:S(2)}) %collective-permute-start) | collective-permute-done | bytes 1146912 | tf_op jit(solution)/shard_map/ppermute | solution.py:18
  235.2 1.5 fusion.5
  236.7 2.3 reshape.101.refs_0_
  239.0 32.1 %shard_map.121 = bf16[1,8,560,128]{3,2,1,0:T(8,128)(2,1)} custom-call(bf16[8,560,128]{2,1,0:T(8,128)(2,1)} %reshape.101.refs_0_), custom_call_target="tpu_custom_call" | custom-call | tf_op jit(solution)/shard_map/pallas_call | solution.py:210
  271.2 2.4 reshape_squeeze.8
  273.6 1.4 fusion.3
  275.0 6.6 %collective-permute-start.1 = (bf16[1,64,3584]{2,1,0:T(8,128)(2,1)}, bf16[1,64,3584]{2,1,0:T(8,128)(2,1)S(1)}, u32[]{:S(2)}, u32[]{:S(2)}) collective-permute-start(bf16[1,64,3584]{2,1,0:T(8,128)(2,1)} %fusion.3), channel_id=1, source_target_pairs={{0,32},{32,64},{64,96},{96,128},{128,160},{160,192},{192,224},{224... | collective-permute-start | bytes 1376264 | tf_op jit(solution)/shard_map/ppermute | solution.py:18
  281.6 0.0 collective-permute-done.2
  281.6 1.9 fusion.4
  283.4 2.3 reshape.105.refs_0_
  285.7 43.8 %shard_map.122 = bf16[1,8,560,128]{3,2,1,0:T(8,128)(2,1)} custom-call(bf16[8,560,128]{2,1,0:T(8,128)(2,1)} %reshape.105.refs_0_), custom_call_target="tpu_custom_call" | custom-call | tf_op jit(solution)/shard_map/pallas_call | solution.py:210
  329.5 2.4 reshape_squeeze.9
  331.9 0.6 fusion.2
  332.5 3.7 %collective-permute-start.3 = (bf16[1,64,3584]{2,1,0:T(8,128)(2,1)S(1)}, bf16[1,64,3584]{2,1,0:T(8,128)(2,1)S(1)}, u32[]{:S(2)}, u32[]{:S(2)}) collective-permute-start(bf16[1,64,3584]{2,1,0:T(8,128)(2,1)S(1)} %fusion.2), channel_id=1, source_target_pairs={{0,224},{32,0},{64,32},{96,64},{128,96},{160,128},{192,160},{224,1... | collective-permute-start | bytes 1376264 | tf_op jit(solution)/shard_map/ppermute | solution.py:18
  336.2 5.9 %convolution_bitcast_fusion = f32[1,1,256,3584]{3,2,1,0:T(8,128)} fusion(bf16[640,3584]{1,0:T(8,128)(2,1)} %reshape.102, f32[640,256]{1,0:T(8,128)S(1)} %fusion.10), kind=kOutput, calls=%fused_computation.2 | convolution fusion | flops 1175224320 | bytes 8912896 | tf_op jit(solution)/shard_map/rf,rd->fd/dot_general | solution.py:250
  342.1 0.0 collective-permute-done.1
  342.1 16.1 %collective-permute-done.3 = bf16[1,64,3584]{2,1,0:T(8,128)(2,1)S(1)} collective-permute-done((bf16[1,64,3584]{2,1,0:T(8,128)(2,1)S(1)}, bf16[1,64,3584]{2,1,0:T(8,128)(2,1)S(1)}, u32[]{:S(2)}, u32[]{:S(2)}) %collective-permute-start.3) | collective-permute-done | bytes 458784 | tf_op jit(solution)/shard_map/ppermute | solution.py:18
  358.2 0.8 copy.35
  359.0 0.8 copy.36
  (18 shorter events, 0.0 us)
Async XLA Ops:
  7.2 161.3 %copy-start = (bf16[1,1,3584,256]{3,2,1,0:T(8,128)(2,1)S(1)}, bf16[1,1,3584,256]{3,2,1,0:T(8,128)(2,1)}, u32[]{:S(2)}) copy-start(bf16[1,1,3584,256]{3,2,1,0:T(8,128)(2,1)} %param.16) | copy-start | bytes 5505028
  7.2 199.3 %reduce-scatter.3.cloned.1.call-start = ((), (), s32[]{:S(2)}) async-start(), calls=%async_computation.2 | async-start | bytes 6881280 | tf_op jit(solution)/shard_map/reduce_scatter | solution.py:223
  11.0 3.8 %copy-start.7 = (s32[1,64,2]{1,2,0:T(2,128)S(1)}, s32[1,64,2]{1,2,0:T(2,128)}, u32[]{:S(2)}) copy-start(s32[1,64,2]{1,2,0:T(2,128)} %param.13) | copy-start | bytes 1540
  11.0 4.7 %copy-start.8 = (f32[1,64,2]{1,2,0:T(2,128)S(1)}, f32[1,64,2]{1,2,0:T(2,128)}, u32[]{:S(2)}) copy-start(f32[1,64,2]{1,2,0:T(2,128)} %param.14) | copy-start | bytes 1540
  16.5 3.8 %copy-start.5 = (bf16[1,64,3584]{2,1,0:T(8,128)(2,1)S(1)}, bf16[1,64,3584]{2,1,0:T(8,128)(2,1)}, u32[]{:S(2)}) copy-start(bf16[1,64,3584]{2,1,0:T(8,128)(2,1)} %param.15) | copy-start | bytes 1376260
  178.3 48.3 %reduce-scatter.5.cloned.1.call-start = ((), (), s32[]{:S(2)}) async-start(), calls=%async_computation.3 | async-start | bytes 6881280 | tf_op jit(solution)/shard_map/reduce_scatter | solution.py:223
  196.9 4.0 %copy-start.2 = (bf16[640,3584]{1,0:T(8,128)(2,1)S(1)}, bf16[640,3584]{1,0:T(8,128)(2,1)}, u32[]{:S(2)}) copy-start(bf16[640,3584]{1,0:T(8,128)(2,1)} %reshape.102) | copy-start | bytes 13762564
  196.9 4.5 %copy-start.9 = (bf16[1,1,256,3584]{3,2,1,0:T(8,128)(2,1)S(1)}, bf16[1,1,256,3584]{3,2,1,0:T(8,128)(2,1)}, u32[]{:S(2)}) copy-start(bf16[1,1,256,3584]{3,2,1,0:T(8,128)(2,1)} %param.17) | copy-start | bytes 5505028
  207.8 27.4 %collective-permute-start = (bf16[160,3584]{1,0:T(8,128)(2,1)S(1)}, bf16[160,3584]{1,0:T(8,128)(2,1)}, u32[]{:S(2)}, u32[]{:S(2)}) collective-permute-start(bf16[160,3584]{1,0:T(8,128)(2,1)S(1)} %dynamic-slice_bitcast_fusion.1), channel_id=1, source_target_pairs={{0,2},{2,0},{1,3},{3,1},{4,6},{6,4},{5,7},{7,5},{8,10},{10,8},{9,1... | collective-permute-start | bytes 3440648 | tf_op jit(solution)/shard_map/ppermute | solution.py:18
  226.6 8.6 %copy-start.3 = (bf16[1,2,160,3584]{3,2,1,0:T(8,128)(2,1)S(1)}, bf16[1,2,160,3584]{3,2,1,0:T(8,128)(2,1)}, u32[]{:S(2)}) copy-start(bf16[1,2,160,3584]{3,2,1,0:T(8,128)(2,1)} %reduce-scatter.3.cloned.1.call-done) | copy-start | bytes 6881284
  229.1 52.4 %collective-permute-start.2 = (bf16[160,3584]{1,0:T(8,128)(2,1)}, bf16[160,3584]{1,0:T(8,128)(2,1)}, u32[]{:S(2)}, u32[]{:S(2)}) collective-permute-start(bf16[160,3584]{1,0:T(8,128)(2,1)} %dynamic-slice_bitcast_fusion), channel_id=1, source_target_pairs={{0,2},{2,0},{1,3},{3,1},{4,6},{6,4},{5,7},{7,5},{8,10},{10,8},{9,1... | collective-permute-start | bytes 3440648 | tf_op jit(solution)/shard_map/ppermute | solution.py:18
  239.0 34.5 %copy-start.4 = (bf16[1,64,3584]{2,1,0:T(8,128)(2,1)S(1)}, bf16[1,64,3584]{2,1,0:T(8,128)(2,1)}, u32[]{:S(2)}) copy-start(bf16[1,64,3584]{2,1,0:T(8,128)(2,1)} %param.9) | copy-start | bytes 1376260
  239.0 34.5 %copy-start.6 = (f32[64,160]{1,0:T(8,128)S(1)}, f32[64,160]{1,0:T(8,128)}, u32[]{:S(2)}) copy-start(f32[64,160]{1,0:T(8,128)} %get-tuple-element.13) | copy-start | bytes 122884
  275.0 67.1 %collective-permute-start.1 = (bf16[1,64,3584]{2,1,0:T(8,128)(2,1)}, bf16[1,64,3584]{2,1,0:T(8,128)(2,1)S(1)}, u32[]{:S(2)}, u32[]{:S(2)}) collective-permute-start(bf16[1,64,3584]{2,1,0:T(8,128)(2,1)} %fusion.3), channel_id=1, source_target_pairs={{0,32},{32,64},{64,96},{96,128},{128,160},{160,192},{192,224},{224... | collective-permute-start | bytes 1376264 | tf_op jit(solution)/shard_map/ppermute | solution.py:18
  332.5 25.7 %collective-permute-start.3 = (bf16[1,64,3584]{2,1,0:T(8,128)(2,1)S(1)}, bf16[1,64,3584]{2,1,0:T(8,128)(2,1)S(1)}, u32[]{:S(2)}, u32[]{:S(2)}) collective-permute-start(bf16[1,64,3584]{2,1,0:T(8,128)(2,1)S(1)} %fusion.2), channel_id=1, source_target_pairs={{0,224},{32,0},{64,32},{96,64},{128,96},{160,128},{192,160},{224,1... | collective-permute-start | bytes 1376264 | tf_op jit(solution)/shard_map/ppermute | solution.py:18
  336.2 23.6 %copy-start.1 = (bf16[1,1,3584,256]{3,2,1,0:T(8,128)(2,1)S(1)}, bf16[1,1,3584,256]{3,2,1,0:T(8,128)(2,1)}, u32[]{:S(2)}) copy-start(bf16[1,1,3584,256]{3,2,1,0:T(8,128)(2,1)} %param.16) | copy-start | bytes 5505028
Sparse Core Ops, SparseCore 0:
  178.4 20.3 reduce-scatter.2
  206.5 20.0 reduce-scatter.4

commit v15 on v14

--- a/solution.py
+++ b/solution.py
@@ -220,8 +220,11 @@
 def group_sum(parts, experts):
     model_width = parts.shape[-1]
     blocks = parts.reshape(2, 2, -1, model_width)
-    pair = lax.psum_scatter(blocks, "ec", scatter_dimension=0, tiled=True)
-    pair = pair.reshape(blocks.shape[1:])
+    core = lax.axis_index("ec")
+    mine = lax.dynamic_index_in_dim(blocks, core, axis=0, keepdims=False)
+    theirs = lax.dynamic_index_in_dim(blocks, 1 - core, axis=0, keepdims=False)
+    came = passed_along(theirs, "ec", 1)
+    pair = (mine.astype(jnp.float32) + came.astype(jnp.float32)).astype(jnp.bfloat16)
     chip = lax.axis_index("ez")
     keep = lax.dynamic_index_in_dim(pair, chip, axis=0, keepdims=False)
     send = lax.dynamic_index_in_dim(pair, 1 - chip, axis=0, keepdims=False)

time: 368 us -> 367 us (level)
  between operations: 14.2 us -> 0.92 us
  local copies, waits for them, and re-layouts: 51.1 us -> 55.8 us
  waiting for transfers between devices: 32.4 us -> 36.8 us
    ppermute x4 -> x6, waiting for transfers between devices: 21.1 us -> 36.8 us  [passed_along(): return lax.ppermute(value, axis, pairs)]
    reduce_scatter x2 -> x0, waiting for transfers between devices: 11.3 us -> none  [group_sum(): pair = lax.psum_scatter(blocks, 'ec', scatter_dimension=0, tiled=True)]
    squeeze x0 -> x2, local copies, waits for them, and re-layouts: none -> 4.73 us  [group_sum(): theirs = lax.dynamic_index_in_dim(blocks, 1 - core, axis=0, keepdims=False)]
    convert_element_type x0 -> x2, other arithmetic: none -> 4.52 us  [group_sum(): (mine.astype(jnp.float32) + came.astype(jnp.float32)).astype(jnp.bfloat16)]
    ppermute x4 -> x6, starting transfers between devices: 13.3 us -> 13.2 us  [passed_along(): return lax.ppermute(value, axis, pairs)]
  transfers between devices with their start and end apart: 6 -> 6, of which waited for: 3 -> 2; matrix products, arithmetic and copies ran while one was open for 16% -> 16% of each run, Pallas kernels for 21% -> 21%
where the time goes in v15:
time: 367 us; the launch traced here: 366 us
  Pallas kernels  212 us (58%)
  local copies, waits for them, and re-layouts  55.8 us (15%)
  matrix products  37.1 us (10%)
  waiting for transfers between devices  36.8 us (10%)
  starting transfers between devices  13.2 us (4%)
  other arithmetic  10.5 us (3%)
    pallas_call x1, Pallas kernels, dispatch(): pl.pallas_call(functools.partial(dispatch_kernel, groups), out_shape=[jax...  135 us
    pallas_call x2, Pallas kernels, send_home(): pl.pallas_call(functools.partial(return_kernel, groups), out_shape=jax.Sh...  77.4 us
    ppermute x6, waiting for transfers between devices, passed_along(): return lax.ppermute(value, axis, pairs)  36.8 us
    reshape x3, local copies, waits for them, and re-layouts, local(): got[index].reshape(-1, model_width)  27.1 us
    ppermute x6, starting transfers between devices, passed_along(): return lax.ppermute(value, axis, pairs)  13.2 us
    reshape x5, local copies, waits for them, and re-layouts, to_wire(): return rows.reshape(*lead, -1, 128)  11.4 us
    dot_general x1, matrix products, expert_forward(): jnp.einsum('...f,fd->...d', act, down_proj, preferred_element_type=jnp.fl...  9.9 us
  transfers between devices with their start and end apart: 6, of which 2 were waited for; matrix products, arithmetic and copies ran while one was open for 16% of the time, Pallas kernels for 21%

profile of v15, /device:TPU:1, one launch (start us, length us, event | category | flops | bytes accessed | tf_op | source)
XLA Modules:
  0.0 366.5 jit_solution(6370473937875367106)
XLA Ops:
  0.6 0.0 copy-start
  0.7 0.9 copy.29
  1.6 0.1 eq.58
  1.7 0.8 copy.31
  2.5 0.1 eq.65
  2.6 0.1 fusion.31
  2.7 0.2 reduce_window_sum.18
  2.9 0.2 select_reduce_fusion.2
  3.1 0.1 reduce_sum.63
  3.2 0.0 copy-start.5
  3.2 0.1 copy.32
  3.3 0.7 bitcast_add_fusion
  4.0 0.1 fusion.32
  4.1 0.2 reduce_window_sum.17
  4.3 0.2 select_reduce_fusion.3
  4.5 0.1 reduce_sum.59
  4.6 0.1 copy.30
  4.7 0.7 bitcast_add_fusion.1
  5.4 0.8 select_reduce_fusion
  6.2 2.1 convolution_convert_fusion.2
  8.3 2.3 reshape.92.refs_2_
  10.6 0.7 convert_reduce_fusion.1
  11.3 0.5 convolution_convert_fusion.4
  11.8 2.3 reshape.90.refs_0_
  14.1 1.5 convolution_convert_fusion.3
  15.6 2.3 reshape.91.refs_1_
  17.9 134.8 %shard_map.120 = (bf16[2,2,8,560,128]{4,3,2,1,0:T(8,128)(2,1)}, bf16[2,2,8,560,128]{4,3,2,1,0:T(8,128)(2,1)}, bf16[2,2,8,560,128]{4,3,2,1,0:T(8,128)(2,1)}) custom-call(bf16[8,560,128]{2,1,0:T(8,128)(2,1)} %reshape.90.refs_0_, bf16[8,560,128]{2,1,0:T(8,128)(2,1)} %reshape.91.refs_1_, bf16[8,560,128]{2,1,0:T(8,128)(2,1)} %reshape.92.refs_2_), custom_call_target="tpu_custom_call" | custom-call | tf_op jit(solution)/shard_map/pallas_call | solution.py:144
  152.7 9.0 %reshape.93 = bf16[640,3584]{1,0:T(8,128)(2,1)} reshape(bf16[2,2,8,560,128]{4,3,2,1,0:T(8,128)(2,1)} %get-tuple-element.7) | data formatting | bytes 9175040 | tf_op jit(solution)/shard_map/reshape | solution.py:279
  161.7 9.9 %convolution_convert_fusion.1 = bf16[640,3584]{1,0:T(8,128)(2,1)} fusion(bf16[1,1,256,3584]{3,2,1,0:T(8,128)(2,1)} %param.17, bf16[640,3584]{1,0:T(8,128)(2,1)} %reshape.93, bf16[1,1,3584,256]{3,2,1,0:T(8,128)(2,1)S(1)} %copy-done), kind=kOutput, calls=%fused_computation.1 | convolution fusion | flops 2351923200 | bytes 12845056 | tf_op jit(solution)/shard_map/...f,fd->...d/dot_general | solution.py:239
  171.6 3.2 dynamic-slice_bitcast_fusion.1
  174.8 0.1 collective-permute-start
  175.0 9.0 %reshape.97 = bf16[640,3584]{1,0:T(8,128)(2,1)} reshape(bf16[2,2,8,560,128]{4,3,2,1,0:T(8,128)(2,1)} %get-tuple-element.9) | data formatting | bytes 9175040 | tf_op jit(solution)/shard_map/reshape | solution.py:279
  184.0 3.6 fusion.12
  187.7 9.0 %reshape.96 = bf16[640,3584]{1,0:T(8,128)(2,1)} reshape(bf16[2,2,8,560,128]{4,3,2,1,0:T(8,128)(2,1)} %get-tuple-element.8) | data formatting | bytes 9175040 | tf_op jit(solution)/shard_map/reshape | solution.py:279
  196.7 4.3 %fusion.19 = bf16[640,256]{1,0:T(8,128)(2,1)S(1)} fusion(bf16[640,3584]{1,0:T(8,128)(2,1)} %reshape.96, bf16[1,1,256,3584]{3,2,1,0:T(8,128)(2,1)} %param.17, f32[640,256]{1,0:T(8,128)S(1)} %fusion.12), kind=kOutput, calls=%fused_computation.32 | convolution fusion | flops 1175879680 | bytes 7405568 | tf_op jit(solution)/shard_map/...d,fd->...f/dot_general | solution.py:247
  201.0 1.4 convolution_convert_fusion
  202.4 1.6 dynamic-slice_bitcast_fusion
  204.0 1.3 copy-done.2
  205.3 0.4 collective-permute-start.3
  205.6 5.9 %convolution_bitcast_fusion.1 = f32[1,1,3584,256]{3,2,1,0:T(8,128)} fusion(bf16[640,3584]{1,0:T(8,128)(2,1)} %reshape.97, bf16[640,256]{1,0:T(8,128)(2,1)S(1)} %copy-done.8), kind=kOutput, calls=%fused_computation.3 | convolution fusion | flops 1174405120 | bytes 8585216 | tf_op jit(solution)/shard_map/rd,rf->df/dot_general | solution.py:252
  211.6 2.3 fusion.3
  213.9 0.1 dynamic-slice_bitcast_fusion.3
  214.0 2.0 collective-permute-start.1
  216.1 2.2 fusion.2
  218.3 1.4 copy-done.4
  219.6 1.1 dynamic-slice_bitcast_fusion.2
  220.7 0.5 collective-permute-start.4
  221.2 20.4 %collective-permute-done.1 = bf16[160,3584]{1,0:T(8,128)(2,1)S(1)} collective-permute-done((bf16[160,3584]{1,0:T(8,128)(2,1)S(1)}, bf16[160,3584]{1,0:T(8,128)(2,1)S(1)}, u32[]{:S(2)}, u32[]{:S(2)}) %collective-permute-start.1) | collective-permute-done | bytes 1146912 | tf_op jit(solution)/shard_map/ppermute | solution.py:18
  241.5 0.3 fusion.7
  241.8 2.3 reshape.95.refs_0_
  244.1 33.6 %shard_map.121 = bf16[1,8,560,128]{3,2,1,0:T(8,128)(2,1)} custom-call(bf16[8,560,128]{2,1,0:T(8,128)(2,1)} %reshape.95.refs_0_), custom_call_target="tpu_custom_call" | custom-call | tf_op jit(solution)/shard_map/pallas_call | solution.py:210
  277.7 2.4 reshape_squeeze.8
  280.1 1.4 fusion.5
  281.5 6.7 %collective-permute-start.2 = (bf16[1,64,3584]{2,1,0:T(8,128)(2,1)}, bf16[1,64,3584]{2,1,0:T(8,128)(2,1)S(1)}, u32[]{:S(2)}, u32[]{:S(2)}) collective-permute-start(bf16[1,64,3584]{2,1,0:T(8,128)(2,1)} %fusion.5), channel_id=1, source_target_pairs={{0,32},{32,64},{64,96},{96,128},{128,160},{160,192},{192,224},{224... | collective-permute-start | bytes 1376264 | tf_op jit(solution)/shard_map/ppermute | solution.py:18
  288.1 1.9 fusion.6
  290.0 2.3 reshape.99.refs_0_
  292.3 43.8 %shard_map.122 = bf16[1,8,560,128]{3,2,1,0:T(8,128)(2,1)} custom-call(bf16[8,560,128]{2,1,0:T(8,128)(2,1)} %reshape.99.refs_0_), custom_call_target="tpu_custom_call" | custom-call | tf_op jit(solution)/shard_map/pallas_call | solution.py:210
  336.0 2.4 reshape_squeeze.9
  338.4 0.6 fusion.4
  339.0 3.5 collective-permute-start.5
  342.6 5.9 %convolution_bitcast_fusion = f32[1,1,256,3584]{3,2,1,0:T(8,128)} fusion(bf16[640,3584]{1,0:T(8,128)(2,1)} %reshape.96, f32[640,256]{1,0:T(8,128)S(1)} %fusion.12), kind=kOutput, calls=%fused_computation.2 | convolution fusion | flops 1175224320 | bytes 8912896 | tf_op jit(solution)/shard_map/rf,rd->fd/dot_general | solution.py:253
  348.5 16.4 %collective-permute-done.5 = bf16[1,64,3584]{2,1,0:T(8,128)(2,1)S(1)} collective-permute-done((bf16[1,64,3584]{2,1,0:T(8,128)(2,1)S(1)}, bf16[1,64,3584]{2,1,0:T(8,128)(2,1)S(1)}, u32[]{:S(2)}, u32[]{:S(2)}) %collective-permute-start.5) | collective-permute-done | bytes 458784 | tf_op jit(solution)/shard_map/ppermute | solution.py:18
  364.9 0.8 copy.35
  365.7 0.8 copy.36
  (27 shorter events, 0.1 us)
Async XLA Ops:
  0.6 161.1 %copy-start = (bf16[1,1,3584,256]{3,2,1,0:T(8,128)(2,1)S(1)}, bf16[1,1,3584,256]{3,2,1,0:T(8,128)(2,1)}, u32[]{:S(2)}) copy-start(bf16[1,1,3584,256]{3,2,1,0:T(8,128)(2,1)} %param.16) | copy-start | bytes 5505028
  2.9 7.7 %copy-start.10 = (f32[1,64,2]{1,2,0:T(2,128)S(1)}, f32[1,64,2]{1,2,0:T(2,128)}, u32[]{:S(2)}) copy-start(f32[1,64,2]{1,2,0:T(2,128)} %param.11) | copy-start | bytes 1540
  3.2 8.1 %copy-start.5 = (bf16[1,64,3584]{2,1,0:T(8,128)(2,1)S(1)}, bf16[1,64,3584]{2,1,0:T(8,128)(2,1)}, u32[]{:S(2)}) copy-start(bf16[1,64,3584]{2,1,0:T(8,128)(2,1)} %param.9) | copy-start | bytes 1376260
  174.8 36.7 %collective-permute-start = (bf16[2,160,3584]{2,1,0:T(8,128)(2,1)}, bf16[2,160,3584]{2,1,0:T(8,128)(2,1)}, u32[]{:S(2)}, u32[]{:S(2)}) collective-permute-start(bf16[2,160,3584]{2,1,0:T(8,128)(2,1)} %dynamic-slice_bitcast_fusion.1), channel_id=1, source_target_pairs={{0,1},{1,0},{2,3},{3,2},{4,5},{5,4},{6,7},{7,6},{8,9},{9,8},{10,11... | collective-permute-start | bytes 6881288 | tf_op jit(solution)/shard_map/ppermute | solution.py:18
  201.0 1.4 copy-start.7
  202.4 2.9 copy-start.2
  202.4 3.2 copy-start.8
  202.4 9.1 %slice-start = ((s8[4587520]{0:T(1024)(128)(4,1)}), s8[393216]{0:T(1024)(128)(4,1)S(1)}, s32[]{:S(2)}) async-start(s8[4587520]{0:T(1024)(128)(4,1)} %bitcast.93), calls=%async_computation | async-start | bytes 786432
  205.3 10.8 %collective-permute-start.3 = (bf16[2,160,3584]{2,1,0:T(8,128)(2,1)}, bf16[2,160,3584]{2,1,0:T(8,128)(2,1)}, u32[]{:S(2)}, u32[]{:S(2)}) collective-permute-start(bf16[2,160,3584]{2,1,0:T(8,128)(2,1)} %dynamic-slice_bitcast_fusion), channel_id=1, source_target_pairs={{0,1},{1,0},{2,3},{3,2},{4,5},{5,4},{6,7},{7,6},{8,9},{9,8},{10,11... | collective-permute-start | bytes 6881288 | tf_op jit(solution)/shard_map/ppermute | solution.py:18
  205.6 5.9 %slice-start.1 = ((s8[4587520]{0:T(1024)(128)(4,1)}), s8[4194304]{0:T(1024)(128)(4,1)S(1)}, s32[]{:S(2)}) async-start(s8[4587520]{0:T(1024)(128)(4,1)} %bitcast.93), calls=%async_computation.1 | async-start | bytes 8388608
  211.6 4.5 %copy-start.3 = (bf16[640,3584]{1,0:T(8,128)(2,1)S(1)}, bf16[640,3584]{1,0:T(8,128)(2,1)}, u32[]{:S(2)}) copy-start(bf16[640,3584]{1,0:T(8,128)(2,1)} %copy-done.2) | copy-start | bytes 13762564
  214.0 27.5 %collective-permute-start.1 = (bf16[160,3584]{1,0:T(8,128)(2,1)S(1)}, bf16[160,3584]{1,0:T(8,128)(2,1)S(1)}, u32[]{:S(2)}, u32[]{:S(2)}) collective-permute-start(bf16[160,3584]{1,0:T(8,128)(2,1)S(1)} %dynamic-slice_bitcast_fusion.3), channel_id=1, source_target_pairs={{0,2},{2,0},{1,3},{3,1},{4,6},{6,4},{5,7},{7,5},{8,10},{10,8},{9,1... | collective-permute-start | bytes 3440648 | tf_op jit(solution)/shard_map/ppermute | solution.py:18
  218.2 1.4 copy-start.4
  220.7 67.4 %collective-permute-start.4 = (bf16[160,3584]{1,0:T(8,128)(2,1)}, bf16[160,3584]{1,0:T(8,128)(2,1)}, u32[]{:S(2)}, u32[]{:S(2)}) collective-permute-start(bf16[160,3584]{1,0:T(8,128)(2,1)} %dynamic-slice_bitcast_fusion.2), channel_id=1, source_target_pairs={{0,2},{2,0},{1,3},{3,1},{4,6},{6,4},{5,7},{7,5},{8,10},{10,8},{9,1... | collective-permute-start | bytes 3440648 | tf_op jit(solution)/shard_map/ppermute | solution.py:18
  244.1 36.0 %copy-start.9 = (f32[64,160]{1,0:T(8,128)S(1)}, f32[64,160]{1,0:T(8,128)}, u32[]{:S(2)}) copy-start(f32[64,160]{1,0:T(8,128)} %get-tuple-element.13) | copy-start | bytes 122884
  281.5 67.0 %collective-permute-start.2 = (bf16[1,64,3584]{2,1,0:T(8,128)(2,1)}, bf16[1,64,3584]{2,1,0:T(8,128)(2,1)S(1)}, u32[]{:S(2)}, u32[]{:S(2)}) collective-permute-start(bf16[1,64,3584]{2,1,0:T(8,128)(2,1)} %fusion.5), channel_id=1, source_target_pairs={{0,32},{32,64},{64,96},{96,128},{128,160},{160,192},{192,224},{224... | collective-permute-start | bytes 1376264 | tf_op jit(solution)/shard_map/ppermute | solution.py:18
  292.3 46.1 %copy-start.6 = (bf16[1,64,3584]{2,1,0:T(8,128)(2,1)S(1)}, bf16[1,64,3584]{2,1,0:T(8,128)(2,1)}, u32[]{:S(2)}) copy-start(bf16[1,64,3584]{2,1,0:T(8,128)(2,1)} %param.15) | copy-start | bytes 1376260
  339.0 25.9 %collective-permute-start.5 = (bf16[1,64,3584]{2,1,0:T(8,128)(2,1)S(1)}, bf16[1,64,3584]{2,1,0:T(8,128)(2,1)S(1)}, u32[]{:S(2)}, u32[]{:S(2)}) collective-permute-start(bf16[1,64,3584]{2,1,0:T(8,128)(2,1)S(1)} %fusion.4), channel_id=1, source_target_pairs={{0,224},{32,0},{64,32},{96,64},{128,96},{160,128},{192,160},{224,1... | collective-permute-start | bytes 1376264 | tf_op jit(solution)/shard_map/ppermute | solution.py:18
  342.6 23.9 %copy-start.1 = (bf16[1,1,3584,256]{3,2,1,0:T(8,128)(2,1)S(1)}, bf16[1,1,3584,256]{3,2,1,0:T(8,128)(2,1)}, u32[]{:S(2)}) copy-start(bf16[1,1,3584,256]{3,2,1,0:T(8,128)(2,1)} %param.16) | copy-start | bytes 5505028

commit v16 on v15

--- a/solution.py
+++ b/solution.py
@@ -279,12 +279,13 @@
     got_f, got_x, got_g = [got[index].reshape(-1, model_width) for index in range(3)]
     part = expert_forward(got_f, up_proj, down_proj)
     wire_f = group_sum(part, experts)
+    summed_f = send_home([wire_f], 1)[0].reshape(-1, model_width).astype(jnp.float32)
+    merged = jnp.dot(gated_f, summed_f, precision=HIGH)
+    section_out = (fwd_input.astype(jnp.float32) + merged).astype(jnp.bfloat16)
+    section_out, got_x, got_g = lax.optimization_barrier((section_out, got_x, got_g))
     dpart, grad_up, grad_down = expert_backward(got_x, got_g, up_proj, down_proj)
     wire_b = group_sum(dpart, experts)
-    summed_f = send_home([wire_f], 1)[0].reshape(-1, model_width).astype(jnp.float32)
     summed_b = send_home([wire_b], 2)[0].reshape(-1, model_width).astype(jnp.float32)
-    merged = jnp.dot(gated_f, summed_f, precision=HIGH)
-    section_out = (fwd_input.astype(jnp.float32) + merged).astype(jnp.bfloat16)
     spread_back = jnp.dot(plain_b, summed_b, precision=HIGH)
     section_grad = (out_grad.astype(jnp.float32) + spread_back).astype(jnp.bfloat16)
     fwd_next = passed_along(section_out[None], "pipe", 1)

time: 367 us -> 372 us (1.014)
  waiting for transfers between devices: 36.8 us -> 47.6 us
  matrix products: 37.1 us -> 32.9 us
    ppermute x6, waiting for transfers between devices: 36.8 us -> 47.6 us  [passed_along(): return lax.ppermute(value, axis, pairs)]
  transfers between devices with their start and end apart: 6 -> 6, of which waited for: 2 -> 5; matrix products, arithmetic and copies ran while one was open for 16% -> 9% of each run, Pallas kernels for 21% -> 12%
where the time goes in v16:
time: 372 us; the launch traced here: 369 us
  Pallas kernels  212 us (57%)
  local copies, waits for them, and re-layouts  53.3 us (14%)
  waiting for transfers between devices  47.6 us (13%)
  matrix products  32.9 us (9%)
  starting transfers between devices  12.4 us (3%)
  other arithmetic  9.29 us (2%)
    pallas_call x1, Pallas kernels, dispatch(): pl.pallas_call(functools.partial(dispatch_kernel, groups), out_shape=[jax...  135 us
    pallas_call x2, Pallas kernels, send_home(): pl.pallas_call(functools.partial(return_kernel, groups), out_shape=jax.Sh...  77.4 us
    ppermute x6, waiting for transfers between devices, passed_along(): return lax.ppermute(value, axis, pairs)  47.6 us
    reshape x3, local copies, waits for them, and re-layouts, local(): got[index].reshape(-1, model_width)  27.1 us
    ppermute x6, starting transfers between devices, passed_along(): return lax.ppermute(value, axis, pairs)  12.4 us
    reshape x5, local copies, waits for them, and re-layouts, to_wire(): return rows.reshape(*lead, -1, 128)  11.4 us
    dot_general x1, matrix products, expert_forward(): jnp.einsum('...f,fd->...d', act, down_proj, preferred_element_type=jnp.fl...  9.95 us
  transfers between devices with their start and end apart: 6, of which 5 were waited for; matrix products, arithmetic and copies ran while one was open for 9% of the time, Pallas kernels for 12%

profile of v16, /device:TPU:1, one launch (start us, length us, event | category | flops | bytes accessed | tf_op | source)
XLA Modules:
  0.0 368.6 jit_solution(9525816916631337569)
XLA Ops:
  0.7 0.9 copy.31
  1.6 0.1 eq.65
  1.7 0.1 fusion.30
  1.8 0.2 reduce_window_sum.18
  2.0 0.2 select_reduce_fusion.2
  2.1 0.1 reduce_sum.63
  2.3 0.1 copy.32
  2.4 0.7 bitcast_add_fusion
  3.1 1.4 select_reduce_fusion
  4.5 1.5 convolution_convert_fusion.3
  6.0 2.3 reshape.91.refs_1_
  8.3 2.2 convolution_convert_fusion.2
  10.5 2.3 reshape.92.refs_2_
  12.7 0.1 copy.29
  12.8 0.1 eq.58
  13.0 0.1 fusion.31
  13.1 0.2 reduce_window_sum.17
  13.3 0.2 select_reduce_fusion.3
  13.4 0.1 reduce_sum.59
  13.6 0.1 copy.30
  13.7 0.7 convert_reduce_fusion.1
  14.4 0.5 convolution_convert_fusion.4
  14.9 2.3 reshape.90.refs_0_
  17.2 134.8 %shard_map.120 = (bf16[2,2,8,560,128]{4,3,2,1,0:T(8,128)(2,1)}, bf16[2,2,8,560,128]{4,3,2,1,0:T(8,128)(2,1)}, bf16[2,2,8,560,128]{4,3,2,1,0:T(8,128)(2,1)}) custom-call(bf16[8,560,128]{2,1,0:T(8,128)(2,1)} %reshape.90.refs_0_, bf16[8,560,128]{2,1,0:T(8,128)(2,1)} %reshape.91.refs_1_, bf16[8,560,128]{2,1,0:T(8,128)(2,1)} %reshape.92.refs_2_), custom_call_target="tpu_custom_call" | custom-call | tf_op jit(solution)/shard_map/pallas_call | solution.py:144
  152.0 9.0 %reshape.93 = bf16[640,3584]{1,0:T(8,128)(2,1)} reshape(bf16[2,2,8,560,128]{4,3,2,1,0:T(8,128)(2,1)} %get-tuple-element.10) | data formatting | bytes 9175040 | tf_op jit(solution)/shard_map/reshape | solution.py:279
  161.0 10.0 %convolution_convert_fusion.1 = bf16[640,3584]{1,0:T(8,128)(2,1)} fusion(bf16[1,1,256,3584]{3,2,1,0:T(8,128)(2,1)} %param.17, bf16[640,3584]{1,0:T(8,128)(2,1)} %reshape.93, bf16[1,1,3584,256]{3,2,1,0:T(8,128)(2,1)S(1)} %copy-done), kind=kOutput, calls=%fused_computation.1 | convolution fusion | flops 2351923200 | bytes 12845056 | tf_op jit(solution)/shard_map/...f,fd->...d/dot_general | solution.py:239
  171.0 3.2 dynamic-slice_bitcast_fusion.1
  174.2 0.1 collective-permute-start
  174.3 4.6 %collective-permute-done = bf16[2,160,3584]{2,1,0:T(8,128)(2,1)} collective-permute-done((bf16[2,160,3584]{2,1,0:T(8,128)(2,1)}, bf16[2,160,3584]{2,1,0:T(8,128)(2,1)}, u32[]{:S(2)}, u32[]{:S(2)}) %collective-permute-start) | collective-permute-done | bytes 2293792 | tf_op jit(solution)/shard_map/ppermute | solution.py:18
  179.0 2.9 fusion.3
  181.8 1.4 copy-done.1
  183.2 0.1 dynamic-slice_bitcast_fusion.3
  183.3 2.2 collective-permute-start.1
  185.5 9.1 %reshape.96 = bf16[640,3584]{1,0:T(8,128)(2,1)} reshape(bf16[2,2,8,560,128]{4,3,2,1,0:T(8,128)(2,1)} %get-tuple-element.11) | data formatting | bytes 9175040 | tf_op jit(solution)/shard_map/reshape | solution.py:279
  194.6 9.1 %reshape.97 = bf16[640,3584]{1,0:T(8,128)(2,1)} reshape(bf16[2,2,8,560,128]{4,3,2,1,0:T(8,128)(2,1)} %get-tuple-element.12) | data formatting | bytes 9175040 | tf_op jit(solution)/shard_map/reshape | solution.py:279
  203.6 7.5 %collective-permute-done.1 = bf16[160,3584]{1,0:T(8,128)(2,1)} collective-permute-done((bf16[160,3584]{1,0:T(8,128)(2,1)S(1)}, bf16[160,3584]{1,0:T(8,128)(2,1)}, u32[]{:S(2)}, u32[]{:S(2)}) %collective-permute-start.1) | collective-permute-done | bytes 1146912 | tf_op jit(solution)/shard_map/ppermute | solution.py:18
  211.1 1.9 fusion.6
  213.0 2.3 reshape.95.refs_0_
  215.3 33.4 %shard_map.121 = bf16[1,8,560,128]{3,2,1,0:T(8,128)(2,1)} custom-call(bf16[8,560,128]{2,1,0:T(8,128)(2,1)} %reshape.95.refs_0_), custom_call_target="tpu_custom_call" | custom-call | tf_op jit(solution)/shard_map/pallas_call | solution.py:210
  248.7 2.4 reshape_squeeze.8
  251.1 2.4 fusion
  253.5 3.8 %fusion.11 = f32[640,256]{1,0:T(8,128)S(1)} fusion(bf16[640,3584]{1,0:T(8,128)(2,1)} %reshape.96, bf16[1,1,3584,256]{3,2,1,0:T(8,128)(2,1)S(1)} %copy-done), kind=kOutput, calls=%fused_computation.26 | convolution fusion | flops 1174405120 | bytes 7077888 | tf_op jit(solution)/shard_map/...d,df->...f/dot_general | solution.py:245
  257.3 0.9 copy-done.4
  258.2 1.4 fusion.18
  259.6 1.4 convolution_convert_fusion
  261.0 0.2 dynamic-slice_bitcast_fusion
  261.1 0.6 collective-permute-start.3
  261.7 4.1 %collective-permute-done.3 = bf16[2,160,3584]{2,1,0:T(8,128)(2,1)S(1)} collective-permute-done((bf16[2,160,3584]{2,1,0:T(8,128)(2,1)S(1)}, bf16[2,160,3584]{2,1,0:T(8,128)(2,1)S(1)}, u32[]{:S(2)}, u32[]{:S(2)}) %collective-permute-start.3) | collective-permute-done | bytes 2293792 | tf_op jit(solution)/shard_map/ppermute | solution.py:18
  265.8 0.6 fusion.2
  266.3 0.1 dynamic-slice_bitcast_fusion.2
  266.4 0.1 collective-permute-start.4
  266.5 3.9 %collective-permute-start.2 = (bf16[1,64,3584]{2,1,0:T(8,128)(2,1)}, bf16[1,64,3584]{2,1,0:T(8,128)(2,1)}, u32[]{:S(2)}, u32[]{:S(2)}) collective-permute-start(bf16[1,64,3584]{2,1,0:T(8,128)(2,1)} %bitcast.14), channel_id=1, source_target_pairs={{0,32},{32,64},{64,96},{96,128},{128,160},{160,192},{192,224},{224... | collective-permute-start | bytes 1376264 | tf_op jit(solution)/shard_map/ppermute | solution.py:18
  270.5 3.5 convolution_bitcast_fusion.1
  274.0 19.1 %collective-permute-done.4 = bf16[160,3584]{1,0:T(8,128)(2,1)S(1)} collective-permute-done((bf16[160,3584]{1,0:T(8,128)(2,1)S(1)}, bf16[160,3584]{1,0:T(8,128)(2,1)S(1)}, u32[]{:S(2)}, u32[]{:S(2)}) %collective-permute-start.4) | collective-permute-done | bytes 1146912 | tf_op jit(solution)/shard_map/ppermute | solution.py:18
  293.0 0.3 fusion.5
  293.3 2.3 reshape.99.refs_0_
  295.6 43.9 %shard_map.122 = bf16[1,8,560,128]{3,2,1,0:T(8,128)(2,1)} custom-call(bf16[8,560,128]{2,1,0:T(8,128)(2,1)} %reshape.99.refs_0_), custom_call_target="tpu_custom_call" | custom-call | tf_op jit(solution)/shard_map/pallas_call | solution.py:210
  339.5 2.4 reshape_squeeze.9
  341.9 0.6 fusion.4
  342.5 5.4 %collective-permute-start.5 = (bf16[1,64,3584]{2,1,0:T(8,128)(2,1)S(1)}, bf16[1,64,3584]{2,1,0:T(8,128)(2,1)S(1)}, u32[]{:S(2)}, u32[]{:S(2)}) collective-permute-start(bf16[1,64,3584]{2,1,0:T(8,128)(2,1)S(1)} %fusion.4), channel_id=1, source_target_pairs={{0,224},{32,0},{64,32},{96,64},{128,96},{160,128},{192,160},{224,1... | collective-permute-start | bytes 1376264 | tf_op jit(solution)/shard_map/ppermute | solution.py:18
  348.0 5.8 %convolution_bitcast_fusion = f32[1,1,256,3584]{3,2,1,0:T(8,128)} fusion(bf16[640,3584]{1,0:T(8,128)(2,1)} %reshape.97, f32[640,256]{1,0:T(8,128)S(1)} %copy-done.5), kind=kOutput, calls=%fused_computation.2 | convolution fusion | flops 1175224320 | bytes 8912896 | tf_op jit(solution)/shard_map/rf,rd->fd/dot_general | solution.py:253
  353.7 12.3 %collective-permute-done.5 = bf16[1,64,3584]{2,1,0:T(8,128)(2,1)S(1)} collective-permute-done((bf16[1,64,3584]{2,1,0:T(8,128)(2,1)S(1)}, bf16[1,64,3584]{2,1,0:T(8,128)(2,1)S(1)}, u32[]{:S(2)}, u32[]{:S(2)}) %collective-permute-start.5) | collective-permute-done | bytes 458784 | tf_op jit(solution)/shard_map/ppermute | solution.py:18
  366.1 1.8 copy.35
  367.9 0.8 copy.36
  (28 shorter events, 0.1 us)
Async XLA Ops:
  0.6 160.4 %copy-start = (bf16[1,1,3584,256]{3,2,1,0:T(8,128)(2,1)S(1)}, bf16[1,1,3584,256]{3,2,1,0:T(8,128)(2,1)}, u32[]{:S(2)}) copy-start(bf16[1,1,3584,256]{3,2,1,0:T(8,128)(2,1)} %param.16) | copy-start | bytes 5505028
  8.3 4.5 %copy-start.6 = (s32[1,64,2]{1,2,0:T(2,128)S(1)}, s32[1,64,2]{1,2,0:T(2,128)}, u32[]{:S(2)}) copy-start(s32[1,64,2]{1,2,0:T(2,128)} %param.10) | copy-start | bytes 1540
  8.3 5.4 %copy-start.7 = (f32[1,64,2]{1,2,0:T(2,128)S(1)}, f32[1,64,2]{1,2,0:T(2,128)}, u32[]{:S(2)}) copy-start(f32[1,64,2]{1,2,0:T(2,128)} %param.11) | copy-start | bytes 1540
  8.3 6.1 %copy-start.2 = (bf16[1,64,3584]{2,1,0:T(8,128)(2,1)S(1)}, bf16[1,64,3584]{2,1,0:T(8,128)(2,1)}, u32[]{:S(2)}) copy-start(bf16[1,64,3584]{2,1,0:T(8,128)(2,1)} %param.9) | copy-start | bytes 1376260
  174.2 4.8 %collective-permute-start = (bf16[2,160,3584]{2,1,0:T(8,128)(2,1)}, bf16[2,160,3584]{2,1,0:T(8,128)(2,1)}, u32[]{:S(2)}, u32[]{:S(2)}) collective-permute-start(bf16[2,160,3584]{2,1,0:T(8,128)(2,1)} %dynamic-slice_bitcast_fusion.1), channel_id=1, source_target_pairs={{0,1},{1,0},{2,3},{3,2},{4,5},{5,4},{6,7},{7,6},{8,9},{9,8},{10,11... | collective-permute-start | bytes 6881288 | tf_op jit(solution)/shard_map/ppermute | solution.py:18
  181.8 1.4 copy-start.1
  183.3 27.8 %collective-permute-start.1 = (bf16[160,3584]{1,0:T(8,128)(2,1)S(1)}, bf16[160,3584]{1,0:T(8,128)(2,1)}, u32[]{:S(2)}, u32[]{:S(2)}) collective-permute-start(bf16[160,3584]{1,0:T(8,128)(2,1)S(1)} %dynamic-slice_bitcast_fusion.3), channel_id=1, source_target_pairs={{0,2},{2,0},{1,3},{3,1},{4,6},{6,4},{5,7},{7,5},{8,10},{10,8},{9,1... | collective-permute-start | bytes 3440648 | tf_op jit(solution)/shard_map/ppermute | solution.py:18
  251.1 7.1 %slice-start = ((s8[4587520]{0:T(1024)(128)(4,1)}), s8[4194304]{0:T(1024)(128)(4,1)S(1)}, s32[]{:S(2)}) async-start(s8[4587520]{0:T(1024)(128)(4,1)} %bitcast.89), calls=%async_computation | async-start | bytes 8388608
  253.5 4.7 %slice-start.1 = ((s8[4587520]{0:T(1024)(128)(4,1)}), s8[393216]{0:T(1024)(128)(4,1)S(1)}, s32[]{:S(2)}) async-start(s8[4587520]{0:T(1024)(128)(4,1)} %bitcast.89), calls=%async_computation.1 | async-start | bytes 786432
  253.5 4.7 %copy-start.8 = (bf16[1,1,256,3584]{3,2,1,0:T(8,128)(2,1)S(1)}, bf16[1,1,256,3584]{3,2,1,0:T(8,128)(2,1)}, u32[]{:S(2)}) copy-start(bf16[1,1,256,3584]{3,2,1,0:T(8,128)(2,1)} %param.17) | copy-start | bytes 5505028
  257.3 0.9 copy-start.4
  261.0 9.5 %slice-start.2 = ((s8[4587520]{0:T(1024)(128)(4,1)}), s8[4194304]{0:T(1024)(128)(4,1)S(1)}, s32[]{:S(2)}) async-start(s8[4587520]{0:T(1024)(128)(4,1)} %bitcast.93), calls=%async_computation.2 | async-start | bytes 8388608
  261.1 9.4 %slice-start.3 = ((s8[4587520]{0:T(1024)(128)(4,1)}), s8[393216]{0:T(1024)(128)(4,1)S(1)}, s32[]{:S(2)}) async-start(s8[4587520]{0:T(1024)(128)(4,1)} %bitcast.93), calls=%async_computation.3 | async-start | bytes 786432
  261.1 4.7 %collective-permute-start.3 = (bf16[2,160,3584]{2,1,0:T(8,128)(2,1)S(1)}, bf16[2,160,3584]{2,1,0:T(8,128)(2,1)S(1)}, u32[]{:S(2)}, u32[]{:S(2)}) collective-permute-start(bf16[2,160,3584]{2,1,0:T(8,128)(2,1)S(1)} %dynamic-slice_bitcast_fusion), channel_id=1, source_target_pairs={{0,1},{1,0},{2,3},{3,2},{4,5},{5,4},{6,7},{7,6},{8,9},{9,8},{10,11... | collective-permute-start | bytes 6881288 | tf_op jit(solution)/shard_map/ppermute | solution.py:18
  266.4 26.6 %collective-permute-start.4 = (bf16[160,3584]{1,0:T(8,128)(2,1)S(1)}, bf16[160,3584]{1,0:T(8,128)(2,1)S(1)}, u32[]{:S(2)}, u32[]{:S(2)}) collective-permute-start(bf16[160,3584]{1,0:T(8,128)(2,1)S(1)} %dynamic-slice_bitcast_fusion.2), channel_id=1, source_target_pairs={{0,2},{2,0},{1,3},{3,1},{4,6},{6,4},{5,7},{7,5},{8,10},{10,8},{9,1... | collective-permute-start | bytes 3440648 | tf_op jit(solution)/shard_map/ppermute | solution.py:18
  266.5 87.2 %collective-permute-start.2 = (bf16[1,64,3584]{2,1,0:T(8,128)(2,1)}, bf16[1,64,3584]{2,1,0:T(8,128)(2,1)}, u32[]{:S(2)}, u32[]{:S(2)}) collective-permute-start(bf16[1,64,3584]{2,1,0:T(8,128)(2,1)} %bitcast.14), channel_id=1, source_target_pairs={{0,32},{32,64},{64,96},{96,128},{128,160},{160,192},{192,224},{224... | collective-permute-start | bytes 1376264 | tf_op jit(solution)/shard_map/ppermute | solution.py:18
  295.6 46.3 %copy-start.3 = (bf16[1,64,3584]{2,1,0:T(8,128)(2,1)S(1)}, bf16[1,64,3584]{2,1,0:T(8,128)(2,1)}, u32[]{:S(2)}) copy-start(bf16[1,64,3584]{2,1,0:T(8,128)(2,1)} %param.15) | copy-start | bytes 1376260
  341.9 6.1 %copy-start.5 = (f32[640,256]{1,0:T(8,128)S(1)}, f32[640,256]{1,0:T(8,128)}, u32[]{:S(2)}) copy-start(f32[640,256]{1,0:T(8,128)} %copy-done.4) | copy-start | bytes 1966084
  342.5 23.5 %collective-permute-start.5 = (bf16[1,64,3584]{2,1,0:T(8,128)(2,1)S(1)}, bf16[1,64,3584]{2,1,0:T(8,128)(2,1)S(1)}, u32[]{:S(2)}, u32[]{:S(2)}) collective-permute-start(bf16[1,64,3584]{2,1,0:T(8,128)(2,1)S(1)} %fusion.4), channel_id=1, source_target_pairs={{0,224},{32,0},{64,32},{96,64},{128,96},{160,128},{192,160},{224,1... | collective-permute-start | bytes 1376264 | tf_op jit(solution)/shard_map/ppermute | solution.py:18
